TPU v7x, 128 devices: a whole 4x4x4 slice. The times are simulated.
128 devices in a mesh: bx: 4 (over x), by: 8 (over y, core), bz: 4 (over z).
Axes of the slice: x: 4, y: 4, z: 4, core: 2. Of those that a mesh axis runs over, the one named last changes fastest.
Arguments:
- counts: bfloat16 [256, 64, 128, 128], P(('bx', 'by', 'bz')), may hold values from 0.099609375 to 10
- row_split: bfloat16 [256, 64, 128, 256], P(('bx', 'by', 'bz')), may hold values from 0 to 0.03125
- col_split: bfloat16 [256, 64, 128, 256], P(('bx', 'by', 'bz')), may hold values from 0 to 0.03125
- efficiency: bfloat16 [64, 128, 128], replicated, may hold values from 0.5 to 1.5
- lorentz: float32 [3600], replicated, may hold values from 0.3 to 3
- angles: int32 [256], P(('bx', 'by', 'bz')), may hold values from 0 to 3599
- tile_owner: int32 [16384, 1], P(('bx', 'by', 'bz')), may hold values from 0 to 127; in each aligned block of 128 rows (0 to 127, 128 to 255, ...) at most 4 rows name the same one
- tile_box: int32 [16384], P(('bx', 'by', 'bz')), may hold values from 0 to 127
Outputs:
- intensity: float32 [8, 8, 4, 64, 256], P('bx', 'by', 'bz')
Inputs may be any that keep to these rules, and one draw needn't show every extreme that they name: `tile_owner`: among the 128 tiles of one device, no owner is named more than 4 times, a bound that some block reaches.
All inputs are finite; a program needn't handle non-finite values.
Results may differ from a plain program's by a relative error of at most 0.0003.
Values sent between devices are 32-bit elements; how exact they have to be, the bound alone decides.
A program may use at most 128 MiB of HBM per device.

v0:
```python
import jax
import jax.numpy as jnp
from jax import lax
from jax.sharding import PartitionSpec as P

VX = 8
VY = 8
VZ = 4
GX = 8
GY = 8
GZ = 4
BOXX = 4
BOXY = 4
BOXZ = 4
BOX_BRICK = 64


def swapped(array, axis, stride):
    return lax.ppermute(array, axis, [(i, i ^ 1 << stride) for i in range(lax.axis_size(axis))])


def shards(counts, row_split, col_split, efficiency, lorentz, angles, tile_owner, tile_box):
    frames_here, tiles_frame, pixels, unused_width = counts.shape
    voxels = row_split.shape[-1]
    size_x = lax.axis_size("bx")
    size_y = lax.axis_size("by")
    size_z = lax.axis_size("bz")
    devices_all = size_x * size_y * size_z
    tiles_here = frames_here * tiles_frame
    capacity = max(4, 4 * tiles_here // devices_all)
    local_x = GX // size_x
    local_y = GY // size_y
    local_z = GZ // size_z
    boxes_here = local_x * local_y * local_z * BOX_BRICK
    picks = angles[:, None] == jnp.arange(lorentz.shape[0], dtype=jnp.int32)[None, :]
    factor = jnp.sum(jnp.where(picks, lorentz[None, :], 0.0), axis=1)
    counted = jnp.einsum("ftpq,ftqv->ftpv", counts, col_split, preferred_element_type=jnp.float32)
    value = jnp.sum(row_split * counted, axis=2) * factor[:, None, None]
    seen = jnp.einsum("tpq,ftqv->ftpv", efficiency, col_split, preferred_element_type=jnp.float32)
    weight = jnp.sum(row_split * seen, axis=2)
    payload = jnp.stack([value, weight], axis=2).reshape(tiles_here, 2 * voxels)
    owner = tile_owner[:, 0]
    marks = (owner[:, None] == jnp.arange(devices_all, dtype=jnp.int32)[None, :]).astype(jnp.int32)
    before = jnp.cumsum(marks, axis=0) - marks
    rank = jnp.sum(before * marks, axis=1)
    slot = owner * capacity + rank
    outgoing = jnp.zeros((devices_all * capacity, 2 * voxels), jnp.float32).at[slot].set(payload)
    labels = jnp.full((devices_all * capacity,), -1, jnp.int32).at[slot].set(tile_box)
    arrived, arrived_ids = (
        lax.all_to_all(
            outgoing.reshape(devices_all, capacity, 2 * voxels),
            ("bx", "by", "bz"),
            split_axis=0,
            concat_axis=0,
            tiled=True,
        ),
        lax.all_to_all(
            labels.reshape(devices_all, capacity),
            ("bx", "by", "bz"),
            split_axis=0,
            concat_axis=0,
            tiled=True,
        ),
    )
    arrived = arrived.reshape(devices_all * capacity, 2 * voxels)
    arrived_ids = arrived_ids.reshape(devices_all * capacity)
    wanted = (jnp.arange(boxes_here, dtype=jnp.int32)[:, None] == arrived_ids[None, :]).astype(
        jnp.float32
    )
    sums = jnp.dot(
        wanted, arrived, precision=lax.Precision.HIGHEST, preferred_element_type=jnp.float32
    )
    volume = sums.reshape(local_x, local_y, local_z, BOXX, BOXY, BOXZ, 2, VX, VY, VZ)
    flipped = jnp.flip(volume, (0, 3, 7))
    for bit in range(size_x.bit_length() - 1):
        flipped = swapped(flipped, "bx", bit)
    volume = 0.5 * (volume + flipped)
    flipped = jnp.flip(volume, (1, 4, 8))
    for bit in range(size_y.bit_length() - 1):
        flipped = swapped(flipped, "by", bit)
    volume = 0.5 * (volume + flipped)
    flipped = jnp.flip(volume, (2, 5, 9))
    for bit in range(size_z.bit_length() - 1):
        flipped = swapped(flipped, "bz", bit)
    volume = 0.5 * (volume + flipped)
    result = volume[:, :, :, :, :, :, 0] / jnp.maximum(volume[:, :, :, :, :, :, 1], 1.0)
    return result.reshape(local_x, local_y, local_z, BOX_BRICK, voxels)


def solution(mesh):
    return jax.shard_map(
        shards,
        mesh=mesh,
        in_specs=(
            P(("bx", "by", "bz"), None, None, None),
            P(("bx", "by", "bz"), None, None, None),
            P(("bx", "by", "bz"), None, None, None),
            P(),
            P(),
            P(("bx", "by", "bz")),
            P(("bx", "by", "bz"), None),
            P(("bx", "by", "bz")),
        ),
        out_specs=P("bx", "by", "bz", None, None),
        check_vma=False,
    )
```

profile of v0, /device:TPU:1, one launch (start us, length us, event | category | flops | bytes accessed | tf_op | source)
XLA Modules:
  0.0 689.6 jit_solution(1173405332276246856)
XLA Ops:
  0.0 0.9 fusion.12
  0.9 0.2 reduce_window_sum.11
  1.1 0.8 select_reduce_fusion
  1.9 0.7 fusion.16
  2.6 1.1 scatter_custom_fusion
  3.7 0.7 all_to_all.9
  4.4 11.5 %all-to-all-start = ((s32[128,1,4]{2,1,0:T(1,128)}), s32[128,1,4]{2,1,0:T(1,128)S(1)}, u32[]{:S(2)}, u32[]{:S(2)}) async-start(s32[128,1,4]{2,1,0:T(1,128)} %bitcast.3), calls=%async_computation | async-start | bytes 131072 | tf_op jit(solution)/shard_map/all_to_all | solution.py:57
  15.9 9.3 %fusion = f32[2,64,256]{2,1,0:T(8,128)S(1)} fusion(bf16[2,64,128,256]{3,2,1,0:T(8,128)(2,1)} %param.9, bf16[2,64,128,128]{3,2,1,0:T(8,128)(2,1)} %param.8, bf16[2,64,128,256]{3,2,1,0:T(8,128)(2,1)} %param.10), kind=kOutput, calls=%fused_computation.4 | convolution fusion | flops 1086291968 | bytes 21102592 | tf_op jit(solution)/shard_map/ftpq,ftqv->ftpv/dot_general | solution.py:37
  25.3 0.0 copy-start.4
  25.3 8.1 %fusion.1 = f32[2,64,256]{2,1,0:T(8,128)S(1)} fusion(bf16[2,64,128,256]{3,2,1,0:T(8,128)(2,1)} %param.9, bf16[2,64,128,256]{3,2,1,0:T(8,128)(2,1)} %param.10, bf16[64,128,128]{2,1,0:T(8,128)(2,1)S(1)} %copy-done), kind=kOutput, calls=%fused_computation.5 | convolution fusion | flops 1086291968 | bytes 19005440 | tf_op jit(solution)/shard_map/tpq,ftqv->ftpv/dot_general | solution.py:39
  33.4 0.1 stack.7
  33.6 0.2 fusion.13
  33.8 0.2 reshape_multiply_fusion
  33.9 0.2 pad_maximum_fusion
  34.2 1.3 scatter_custom_fusion.1
  35.5 1.3 reshape.89
  36.8 9.8 %all-to-all-start.1 = ((f32[128,4,512]{2,1,0:T(4,128)}), f32[128,4,512]{2,1,0:T(4,128)S(1)}, u32[]{:S(2)}, u32[]{:S(2)}) async-start(f32[128,4,512]{2,1,0:T(4,128)} %reshape.89), calls=%async_computation.1 | async-start | bytes 2097152 | tf_op jit(solution)/shard_map/all_to_all | solution.py:50
  46.6 0.5 broadcast.86
  47.1 0.8 reduce.3
  47.9 0.1 eq.80
  48.0 18.1 %all-to-all-done.1 = f32[128,4,512]{2,1,0:T(4,128)S(1)} async-done(((f32[128,4,512]{2,1,0:T(4,128)}), f32[128,4,512]{2,1,0:T(4,128)S(1)}, u32[]{:S(2)}, u32[]{:S(2)}) %all-to-all-start.1) | async-done | bytes 1048608 | tf_op jit(solution)/shard_map/all_to_all | solution.py:50
  66.1 0.4 reshape.90
  66.5 0.3 copy.26
  66.8 0.3 dot_general.18
  67.1 7.1 %fusion.4 = f32[2,4,4,4,2,8,8,4]{6,3,7,5,4,2,1,0:T(4,128)S(1)} fusion(f32[2,8,8,4,512,1,1,1]{4,3,2,1,0,7,6,5:T(4,128)S(1)} %bitcast.38, s32[512]{0:T(512)S(1)} %eq.80, s32[2,4,4,4]{3,2,1,0:T(4,128)S(1)} %multiply_add_fusion.1), kind=kOutput, calls=%fused_computation.15 | convolution fusion | flops 402718720 | bytes 1313280 | tf_op jit(solution)/shard_map/dot_general | solution.py:70
  74.3 0.7 reverse_bitcast_fusion
  75.0 0.4 collective-permute-start
  75.4 91.5 %collective-permute-done = f32[2,1,1,4,4,4,2,8,8,4]{8,5,9,7,6,4,3,0,2,1:T(4,128)S(1)} collective-permute-done((f32[2,1,1,4,4,4,2,8,8,4]{8,5,9,7,6,4,3,0,2,1:T(4,128)S(1)}, f32[2,1,1,4,4,4,2,8,8,4]{8,5,9,7,6,4,3,0,2,1:T(4,128)S(1)}, u32[]{:S(2)}, u32[]{:S(2)}) %collective-permute-start) | collective-permute-done | bytes 262176 | tf_op jit(solution)/shard_map/ppermute | solution.py:19
  166.8 0.9 collective-permute-start.1
  167.7 91.5 %collective-permute-done.1 = f32[2,1,1,4,4,4,2,8,8,4]{8,5,9,7,6,4,3,0,2,1:T(4,128)S(1)} collective-permute-done((f32[2,1,1,4,4,4,2,8,8,4]{8,5,9,7,6,4,3,0,2,1:T(4,128)S(1)}, f32[2,1,1,4,4,4,2,8,8,4]{8,5,9,7,6,4,3,0,2,1:T(4,128)S(1)}, u32[]{:S(2)}, u32[]{:S(2)}) %collective-permute-start.1) | collective-permute-done | bytes 262176 | tf_op jit(solution)/shard_map/ppermute | solution.py:19
  259.2 3.4 bitcast_add_fusion
  262.6 12.1 %reverse.10 = f32[2,1,1,4,4,4,2,8,8,4]{8,5,9,7,6,4,3,0,2,1:T(4,128)} reverse(f32[2,1,1,4,4,4,2,8,8,4]{8,5,9,7,6,4,3,0,2,1:T(4,128)} %bitcast_add_fusion), dimensions={1,4,8} | reverse | bytes 524288 | tf_op jit(solution)/shard_map/reverse
  274.7 3.4 broadcast_multiply_fusion.1
  278.1 2.2 collective-permute-start.2
  280.3 6.8 collective-permute-done.2
  287.1 91.8 %collective-permute-done.3 = f32[2,1,1,4,4,4,2,8,8,4]{8,5,9,7,6,4,3,0,2,1:T(4,128)S(1)} collective-permute-done((f32[2,1,1,4,4,4,2,8,8,4]{8,5,9,7,6,4,3,0,2,1:T(4,128)S(1)}, f32[2,1,1,4,4,4,2,8,8,4]{8,5,9,7,6,4,3,0,2,1:T(4,128)S(1)}, u32[]{:S(2)}, u32[]{:S(2)}) %collective-permute-start.3) | collective-permute-done | bytes 262176 | tf_op jit(solution)/shard_map/ppermute | solution.py:19
  378.9 0.1 collective-permute-start.4
  379.0 92.3 %collective-permute-done.4 = f32[2,1,1,4,4,4,2,8,8,4]{8,5,9,7,6,4,3,0,2,1:T(4,128)S(1)} collective-permute-done((f32[2,1,1,4,4,4,2,8,8,4]{8,5,9,7,6,4,3,0,2,1:T(4,128)S(1)}, f32[2,1,1,4,4,4,2,8,8,4]{8,5,9,7,6,4,3,0,2,1:T(4,128)S(1)}, u32[]{:S(2)}, u32[]{:S(2)}) %collective-permute-start.4) | collective-permute-done | bytes 262176 | tf_op jit(solution)/shard_map/ppermute | solution.py:19
  471.3 3.8 multiply_add_fusion
  475.1 11.8 %reverse.11 = f32[2,1,1,4,4,4,2,8,8,4]{8,5,9,7,6,4,3,0,2,1:T(4,128)} reverse(f32[2,1,1,4,4,4,2,8,8,4]{8,5,9,7,6,4,3,0,2,1:T(4,128)} %multiply_add_fusion), dimensions={2,5,9} | reverse | bytes 524288 | tf_op jit(solution)/shard_map/reverse.1
  487.0 3.4 broadcast_multiply_fusion
  490.4 0.6 collective-permute-start.5
  491.0 89.4 %collective-permute-done.5 = f32[2,1,1,4,4,4,2,8,8,4]{8,5,9,7,6,4,3,0,2,1:T(4,128)S(1)} collective-permute-done((f32[2,1,1,4,4,4,2,8,8,4]{8,5,9,7,6,4,3,0,2,1:T(4,128)S(1)}, f32[2,1,1,4,4,4,2,8,8,4]{8,5,9,7,6,4,3,0,2,1:T(4,128)S(1)}, u32[]{:S(2)}, u32[]{:S(2)}) %collective-permute-start.5) | collective-permute-done | bytes 262176 | tf_op jit(solution)/shard_map/ppermute | solution.py:19
  580.4 89.7 %collective-permute-done.6 = f32[2,1,1,4,4,4,2,8,8,4]{8,5,9,7,6,4,3,0,2,1:T(4,128)S(1)} collective-permute-done((f32[2,1,1,4,4,4,2,8,8,4]{8,5,9,7,6,4,3,0,2,1:T(4,128)S(1)}, f32[2,1,1,4,4,4,2,8,8,4]{8,5,9,7,6,4,3,0,2,1:T(4,128)S(1)}, u32[]{:S(2)}, u32[]{:S(2)}) %collective-permute-start.6) | collective-permute-done | bytes 262176 | tf_op jit(solution)/shard_map/ppermute | solution.py:19
  670.2 2.8 add_multiply_fusion
  672.9 2.1 fusion.2
  675.0 9.1 %copy.28 = f32[2,1,1,4,4,4,1,8,8,4]{9,8,7,5,4,3,0,6,2,1:T(8,128)} copy(f32[2,1,1,4,4,4,1,8,8,4]{8,5,9,7,6,4,3,0,2,1:T(4,128)} %fusion.2) | data formatting | bytes 262144 | tf_op jit(solution)/shard_map/div | solution.py:86
  684.1 5.5 div.16
  (16 shorter events, 0.1 us)
Async XLA Ops:
  0.0 25.3 %copy-start = (bf16[64,128,128]{2,1,0:T(8,128)(2,1)S(1)}, bf16[64,128,128]{2,1,0:T(8,128)(2,1)}, u32[]{:S(2)}) copy-start(bf16[64,128,128]{2,1,0:T(8,128)(2,1)} %param.11) | copy-start | bytes 6291460
  4.4 32.4 %all-to-all-start = ((s32[128,1,4]{2,1,0:T(1,128)}), s32[128,1,4]{2,1,0:T(1,128)S(1)}, u32[]{:S(2)}, u32[]{:S(2)}) async-start(s32[128,1,4]{2,1,0:T(1,128)} %bitcast.3), calls=%async_computation | async-start | bytes 131072 | tf_op jit(solution)/shard_map/all_to_all | solution.py:57
  25.3 8.3 %copy-start.4 = (f32[3600]{0:T(1024)S(1)}, f32[3600]{0:T(1024)}, u32[]{:S(2)}) copy-start(f32[3600]{0:T(1024)} %param.12) | copy-start | bytes 43204
  25.3 8.3 %copy-start.5 = (s32[2]{0:T(128)S(1)}, s32[2]{0:T(128)}, u32[]{:S(2)}) copy-start(s32[2]{0:T(128)} %param.13) | copy-start | bytes 28
  36.8 29.4 %all-to-all-start.1 = ((f32[128,4,512]{2,1,0:T(4,128)}), f32[128,4,512]{2,1,0:T(4,128)S(1)}, u32[]{:S(2)}, u32[]{:S(2)}) async-start(f32[128,4,512]{2,1,0:T(4,128)} %reshape.89), calls=%async_computation.1 | async-start | bytes 2097152 | tf_op jit(solution)/shard_map/all_to_all | solution.py:50
  75.0 91.8 %collective-permute-start = (f32[2,1,1,4,4,4,2,8,8,4]{8,5,9,7,6,4,3,0,2,1:T(4,128)S(1)}, f32[2,1,1,4,4,4,2,8,8,4]{8,5,9,7,6,4,3,0,2,1:T(4,128)S(1)}, u32[]{:S(2)}, u32[]{:S(2)}) collective-permute-start(f32[2,1,1,4,4,4,2,8,8,4]{8,5,9,7,6,4,3,0,2,1:T(4,128)S(1)} %reverse_bitcast_fusion), channel_id=1, source_target_pairs={{0,32},{32,0},{64,96},{96,64},{1,33},{33,1},{65,97},{97,65},{2,34}... | collective-permute-start | bytes 786440 | tf_op jit(solution)/shard_map/ppermute | solution.py:19
  166.8 92.3 %collective-permute-start.1 = (f32[2,1,1,4,4,4,2,8,8,4]{8,5,9,7,6,4,3,0,2,1:T(4,128)S(1)}, f32[2,1,1,4,4,4,2,8,8,4]{8,5,9,7,6,4,3,0,2,1:T(4,128)S(1)}, u32[]{:S(2)}, u32[]{:S(2)}) collective-permute-start(f32[2,1,1,4,4,4,2,8,8,4]{8,5,9,7,6,4,3,0,2,1:T(4,128)S(1)} %collective-permute-done), channel_id=1, source_target_pairs={{0,64},{32,96},{64,0},{96,32},{1,65},{33,97},{65,1},{97,33},{2,66}... | collective-permute-start | bytes 786440 | tf_op jit(solution)/shard_map/ppermute | solution.py:19
  274.7 196.6 %copy-start.2 = (f32[2,1,1,4,4,4,2,8,8,4]{8,5,9,7,6,4,3,0,2,1:T(4,128)S(1)}, f32[2,1,1,4,4,4,2,8,8,4]{8,5,9,7,6,4,3,0,2,1:T(4,128)}, u32[]{:S(2)}) copy-start(f32[2,1,1,4,4,4,2,8,8,4]{8,5,9,7,6,4,3,0,2,1:T(4,128)} %bitcast_add_fusion) | copy-start | bytes 786436
  278.1 9.0 %collective-permute-start.2 = (f32[2,1,1,4,4,4,2,8,8,4]{8,5,9,7,6,4,3,0,2,1:T(4,128)S(1)}, f32[2,1,1,4,4,4,2,8,8,4]{8,5,9,7,6,4,3,0,2,1:T(4,128)S(1)}, u32[]{:S(2)}, u32[]{:S(2)}) collective-permute-start(f32[2,1,1,4,4,4,2,8,8,4]{8,5,9,7,6,4,3,0,2,1:T(4,128)S(1)} %broadcast_multiply_fusion.1), channel_id=1, source_target_pairs={{0,4},{4,0},{8,12},{12,8},{16,20},{20,16},{24,28},{28,24},{1,5},{5... | collective-permute-start | bytes 786440 | tf_op jit(solution)/shard_map/ppermute | solution.py:19
  287.1 91.8 %collective-permute-start.3 = (f32[2,1,1,4,4,4,2,8,8,4]{8,5,9,7,6,4,3,0,2,1:T(4,128)S(1)}, f32[2,1,1,4,4,4,2,8,8,4]{8,5,9,7,6,4,3,0,2,1:T(4,128)S(1)}, u32[]{:S(2)}, u32[]{:S(2)}) collective-permute-start(f32[2,1,1,4,4,4,2,8,8,4]{8,5,9,7,6,4,3,0,2,1:T(4,128)S(1)} %collective-permute-done.2), channel_id=1, source_target_pairs={{0,8},{4,12},{8,0},{12,4},{16,24},{20,28},{24,16},{28,20},{1,9},{5... | collective-permute-start | bytes 786440 | tf_op jit(solution)/shard_map/ppermute | solution.py:19
  378.9 92.4 %collective-permute-start.4 = (f32[2,1,1,4,4,4,2,8,8,4]{8,5,9,7,6,4,3,0,2,1:T(4,128)S(1)}, f32[2,1,1,4,4,4,2,8,8,4]{8,5,9,7,6,4,3,0,2,1:T(4,128)S(1)}, u32[]{:S(2)}, u32[]{:S(2)}) collective-permute-start(f32[2,1,1,4,4,4,2,8,8,4]{8,5,9,7,6,4,3,0,2,1:T(4,128)S(1)} %collective-permute-done.3), channel_id=1, source_target_pairs={{0,16},{4,20},{8,24},{12,28},{16,0},{20,4},{24,8},{28,12},{1,17},{... | collective-permute-start | bytes 786440 | tf_op jit(solution)/shard_map/ppermute | solution.py:19
  487.0 183.2 %copy-start.3 = (f32[2,1,1,4,4,4,2,8,8,4]{8,5,9,7,6,4,3,0,2,1:T(4,128)S(1)}, f32[2,1,1,4,4,4,2,8,8,4]{8,5,9,7,6,4,3,0,2,1:T(4,128)}, u32[]{:S(2)}) copy-start(f32[2,1,1,4,4,4,2,8,8,4]{8,5,9,7,6,4,3,0,2,1:T(4,128)} %multiply_add_fusion) | copy-start | bytes 786436
  490.4 90.0 %collective-permute-start.5 = (f32[2,1,1,4,4,4,2,8,8,4]{8,5,9,7,6,4,3,0,2,1:T(4,128)S(1)}, f32[2,1,1,4,4,4,2,8,8,4]{8,5,9,7,6,4,3,0,2,1:T(4,128)S(1)}, u32[]{:S(2)}, u32[]{:S(2)}) collective-permute-start(f32[2,1,1,4,4,4,2,8,8,4]{8,5,9,7,6,4,3,0,2,1:T(4,128)S(1)} %broadcast_multiply_fusion), channel_id=1, source_target_pairs={{0,1},{1,0},{2,3},{3,2},{4,5},{5,4},{6,7},{7,6},{8,9},{9,8},{10,11... | collective-permute-start | bytes 786440 | tf_op jit(solution)/shard_map/ppermute | solution.py:19
  580.4 89.7 %collective-permute-start.6 = (f32[2,1,1,4,4,4,2,8,8,4]{8,5,9,7,6,4,3,0,2,1:T(4,128)S(1)}, f32[2,1,1,4,4,4,2,8,8,4]{8,5,9,7,6,4,3,0,2,1:T(4,128)S(1)}, u32[]{:S(2)}, u32[]{:S(2)}) collective-permute-start(f32[2,1,1,4,4,4,2,8,8,4]{8,5,9,7,6,4,3,0,2,1:T(4,128)S(1)} %collective-permute-done.5), channel_id=1, source_target_pairs={{0,2},{1,3},{2,0},{3,1},{4,6},{5,7},{6,4},{7,5},{8,10},{9,11},{10,... | collective-permute-start | bytes 786440 | tf_op jit(solution)/shard_map/ppermute | solution.py:19
  672.9 16.7 %copy-start.1 = (bf16[64,128,128]{2,1,0:T(8,128)(2,1)S(1)}, bf16[64,128,128]{2,1,0:T(8,128)(2,1)}, u32[]{:S(2)}) copy-start(bf16[64,128,128]{2,1,0:T(8,128)(2,1)} %param.11) | copy-start | bytes 6291460
where the time goes:
time: 694 us; the launch traced here: 690 us
  waiting for transfers between devices  571 us (82%)
  local copies, waits for them, and re-layouts  45.4 us (7%)
  starting transfers between devices  25.5 us (4%)
  matrix products  24.6 us (4%)
  other arithmetic  22.9 us (3%)
    ppermute x7, waiting for transfers between devices, swapped(): lax.ppermute(array, axis, [(i, i ^ 1 << stride) for i in range(lax.axis_s...  553 us
    another operation x2, local copies, waits for them, and re-layouts  23.9 us
    all_to_all x1, waiting for transfers between devices, shards(): lax.all_to_all(outgoing.reshape(devices_all, capacity, 2 * voxels), ('bx'...  18.1 us
    div x2, local copies, waits for them, and re-layouts, shards(): volume[:, :, :, :, :, :, 0] / jnp.maximum(volume[:, :, :, :, :, :, 1], 1.0)  14.6 us
  transfers between devices with their start and end apart: 9, of which 8 were waited for; matrix products, arithmetic and copies ran while one was open for 3% of the time, Pallas kernels for 0%

commit v1 on v0

v1 whole, which is shorter than its diff:
```python
import numpy as np
import jax
import jax.numpy as jnp
from jax import lax
from jax.sharding import PartitionSpec as P

VX = 8
VY = 8
VZ = 4
GX = 8
GY = 8
GZ = 4
BOXX = 4
BOXY = 4
BOXZ = 4
BOX_BRICK = 64


def mirrored(array, axis):
    size = lax.axis_size(axis)
    if size == 1:
        return array
    return lax.ppermute(array, axis, [(i, size - 1 - i) for i in range(size)])


def flip_table(sizes, flipped):
    index = np.arange(int(np.prod(sizes))).reshape(sizes)
    return np.flip(index, flipped).reshape(-1).astype(np.int32)


def permuting(table):
    size = table.shape[0]
    return (jnp.asarray(table)[:, None] == lax.iota(jnp.int32, size)[None, :]).astype(jnp.float32)


def laue_step(volume, axis, row_table, lane_table):
    partner = mirrored(volume, axis)
    rows = permuting(row_table)
    lanes = permuting(np.concatenate([lane_table, lane_table + lane_table.shape[0]])).T
    moved = jnp.dot(rows, partner, precision=lax.Precision.HIGHEST, preferred_element_type=jnp.float32)
    moved = jnp.dot(moved, lanes, precision=lax.Precision.HIGHEST, preferred_element_type=jnp.float32)
    return 0.5 * (volume + moved)


def shards(counts, row_split, col_split, efficiency, lorentz, angles, tile_owner, tile_box):
    frames_here, tiles_frame, pixels, unused_width = counts.shape
    voxels = row_split.shape[-1]
    size_x = lax.axis_size("bx")
    size_y = lax.axis_size("by")
    size_z = lax.axis_size("bz")
    devices_all = size_x * size_y * size_z
    tiles_here = frames_here * tiles_frame
    capacity = max(4, 4 * tiles_here // devices_all)
    local_x = GX // size_x
    local_y = GY // size_y
    local_z = GZ // size_z
    boxes_here = local_x * local_y * local_z * BOX_BRICK
    picks = angles[:, None] == jnp.arange(lorentz.shape[0], dtype=jnp.int32)[None, :]
    factor = jnp.sum(jnp.where(picks, lorentz[None, :], 0.0), axis=1)
    counted = jnp.einsum("ftpq,ftqv->ftpv", counts, col_split, preferred_element_type=jnp.float32)
    value = jnp.sum(row_split * counted, axis=2) * factor[:, None, None]
    seen = jnp.einsum("tpq,ftqv->ftpv", efficiency, col_split, preferred_element_type=jnp.float32)
    weight = jnp.sum(row_split * seen, axis=2)
    payload = jnp.concatenate(
        [value.reshape(tiles_here, voxels), weight.reshape(tiles_here, voxels)], axis=1
    )
    owner = tile_owner[:, 0]
    marks = (owner[:, None] == jnp.arange(devices_all, dtype=jnp.int32)[None, :]).astype(jnp.int32)
    before = jnp.cumsum(marks, axis=0) - marks
    rank = jnp.sum(before * marks, axis=1)
    slot = owner * capacity + rank
    outgoing = jnp.zeros((devices_all * capacity, 2 * voxels), jnp.float32).at[slot].set(payload)
    labels = jnp.full((devices_all * capacity,), -1.0, jnp.float32).at[slot].set(
        tile_box.astype(jnp.float32)
    )
    label_width = 128
    labels = jnp.pad(labels.reshape(devices_all, capacity), ((0, 0), (0, label_width - capacity)))
    packed = jnp.concatenate(
        [outgoing.reshape(devices_all, capacity * 2 * voxels), labels], axis=1
    )
    arrived = lax.all_to_all(packed, ("bx", "by", "bz"), split_axis=0, concat_axis=0, tiled=True)
    arrived_payload = arrived[:, : capacity * 2 * voxels].reshape(devices_all * capacity, 2 * voxels)
    arrived_ids = arrived[:, capacity * 2 * voxels : capacity * 2 * voxels + capacity].reshape(
        devices_all * capacity
    )
    wanted = (
        jnp.arange(boxes_here, dtype=jnp.float32)[:, None] == arrived_ids[None, :]
    ).astype(jnp.float32)
    sums = jnp.dot(
        wanted, arrived_payload, precision=lax.Precision.HIGHEST, preferred_element_type=jnp.float32
    )
    row_sizes = (local_x, local_y, local_z, BOXX, BOXY, BOXZ)
    lane_sizes = (VX, VY, VZ)
    volume = laue_step(sums, "bx", flip_table(row_sizes, (0, 3)), flip_table(lane_sizes, (0,)))
    volume = laue_step(volume, "by", flip_table(row_sizes, (1, 4)), flip_table(lane_sizes, (1,)))
    volume = laue_step(volume, "bz", flip_table(row_sizes, (2, 5)), flip_table(lane_sizes, (2,)))
    result = volume[:, :voxels] / jnp.maximum(volume[:, voxels:], 1.0)
    return result.reshape(local_x, local_y, local_z, BOX_BRICK, voxels)


def solution(mesh):
    return jax.shard_map(
        shards,
        mesh=mesh,
        in_specs=(
            P(("bx", "by", "bz"), None, None, None),
            P(("bx", "by", "bz"), None, None, None),
            P(("bx", "by", "bz"), None, None, None),
            P(),
            P(),
            P(("bx", "by", "bz")),
            P(("bx", "by", "bz"), None),
            P(("bx", "by", "bz")),
        ),
        out_specs=P("bx", "by", "bz", None, None),
        check_vma=False,
    )
```

time: 694 us -> 94.2 us (0.14)
  waiting for transfers between devices: 571 us -> 24.5 us
  local copies, waits for them, and re-layouts: 45.4 us -> 6.32 us
  blocking collectives: 0 us -> 31.6 us
  starting transfers between devices: 25.5 us -> 2.26 us
  other arithmetic: 22.9 us -> 7.49 us
    ppermute x7 -> x3, waiting for transfers between devices: 553 us -> 24.5 us  [mirrored(): return lax.ppermute(array, axis, [(i, size - 1 - i) for i in range(size)])]
    all_to_all x0 -> x1, blocking collectives: none -> 31.6 us  [shards(): lax.all_to_all(packed, ('bx', 'by', 'bz'), split_axis=0, concat_axis=0, t...]
    another operation x3 -> x0, local copies, waits for them, and re-layouts: 24 us -> none
    all_to_all x2 -> x0, starting transfers between devices: 21.3 us -> none  [the longest x1 11.5 us: shards(): lax.all_to_all(labels.reshape(devices_all, capacity), ('bx', 'by', 'bz'),...]
    all_to_all x2 -> x0, waiting for transfers between devices: 18.1 us -> none  [the longest x1 18.1 us: shards(): lax.all_to_all(outgoing.reshape(devices_all, capacity, 2 * voxels), ('bx'...]
    div x2 -> x0, local copies, waits for them, and re-layouts: 14.6 us -> none  [shards(): volume[:, :, :, :, :, :, 0] / jnp.maximum(volume[:, :, :, :, :, :, 1], 1.0)]
    add x2 -> x0, other arithmetic: 7.26 us -> none  [shards(): volume = 0.5 * (volume + flipped)]
  transfers between devices with their start and end apart: 9 -> 3, of which waited for: 8 -> 3; matrix products, arithmetic and copies ran while one was open for 3% -> 0% of each run, Pallas kernels for 0% -> 0%
where the time goes in v1:
time: 94.2 us; the launch traced here: 93.6 us
  blocking collectives  31.6 us (34%)
  waiting for transfers between devices  24.5 us (26%)
  matrix products  21.3 us (23%)
  other arithmetic  7.49 us (8%)
  local copies, waits for them, and re-layouts  6.32 us (7%)
  starting transfers between devices  2.26 us (2%)
    all_to_all x1, blocking collectives, shards(): lax.all_to_all(packed, ('bx', 'by', 'bz'), split_axis=0, concat_axis=0, t...  31.6 us
    ppermute x3, waiting for transfers between devices, mirrored(): return lax.ppermute(array, axis, [(i, size - 1 - i) for i in range(size)])  24.5 us
    dot_general x1, matrix products, shards(): jnp.einsum('ftpq,ftqv->ftpv', counts, col_split, preferred_element_type=j...  9.33 us
    dot_general x1, matrix products, shards(): jnp.einsum('tpq,ftqv->ftpv', efficiency, col_split, preferred_element_typ...  8.13 us
    dot_general x3, matrix products, laue_step(): jnp.dot(moved, lanes, precision=lax.Precision.HIGHEST, preferred_element_...  2.35 us
    ppermute x3, starting transfers between devices, mirrored(): return lax.ppermute(array, axis, [(i, size - 1 - i) for i in range(size)])  2.26 us
  transfers between devices with their start and end apart: 3, of which 3 were waited for; matrix products, arithmetic and copies ran while one was open for 0% of the time, Pallas kernels for 0%

profile of v1, /device:TPU:1, one launch (start us, length us, event | category | flops | bytes accessed | tf_op | source)
XLA Modules:
  0.0 93.6 jit_solution(8027923759856025801)
XLA Ops:
  0.0 0.0 copy-start
  0.0 1.1 %fusion.24 = f32[2]{0:T(128)S(1)} fusion(s32[2]{0:T(128)} %param.19, f32[3600]{0:T(1024)} %param.18), kind=kLoop, calls=%fused_computation.46 | loop fusion | flops 21598 | bytes 14416 | tf_op jit(solution)/shard_map/reduce_sum | solution.py:59
  1.1 0.1 mul.42
  1.2 0.1 mul.43
  1.3 0.7 convert_element_type.10
  1.9 0.7 fusion.17
  2.7 0.2 reduce_window_sum.11
  2.8 0.8 select_reduce_fusion
  3.7 0.7 fusion.27
  4.3 1.0 %scatter_custom_fusion.1 = f32[512]{0:T(512)S(1)} fusion(s32[128]{0:T(128)S(1)} %fusion.27, f32[128]{0:T(128)S(1)} %convert_element_type.10, f32[]{:T(128)} %constant.11.clone.1), kind=kCustom, calls=%fused_computation.48 | custom fusion | bytes 2052 | tf_op jit(solution)/shard_map/scatter | solution.py:73
  5.3 0.1 reshape.33
  5.4 9.3 %fusion = f32[2,64,256]{2,1,0:T(8,128)S(1)} fusion(bf16[2,64,128,256]{3,2,1,0:T(8,128)(2,1)} %param.15, bf16[2,64,128,128]{3,2,1,0:T(8,128)(2,1)} %param.14, bf16[2,64,128,256]{3,2,1,0:T(8,128)(2,1)} %param.16), kind=kOutput, calls=%fused_computation.4 | convolution fusion | flops 1086291968 | bytes 21102592 | tf_op jit(solution)/shard_map/ftpq,ftqv->ftpv/dot_general | solution.py:60
  14.8 0.0 copy-done
  14.8 8.1 %fusion.1 = f32[2,64,256]{2,1,0:T(8,128)S(1)} fusion(bf16[2,64,128,256]{3,2,1,0:T(8,128)(2,1)} %param.15, bf16[2,64,128,256]{3,2,1,0:T(8,128)(2,1)} %param.16, bf16[64,128,128]{2,1,0:T(8,128)(2,1)S(1)} %copy-done), kind=kOutput, calls=%fused_computation.5 | convolution fusion | flops 1086291968 | bytes 19005440 | tf_op jit(solution)/shard_map/tpq,ftqv->ftpv/dot_general | solution.py:62
  22.9 0.1 bitcast_multiply_fusion
  23.0 1.3 %scatter_custom_fusion = f32[512,512]{1,0:T(8,128)S(1)} fusion(s32[128]{0:T(128)S(1)} %fusion.27, f32[]{:T(128)} %constant.13.clone.1, f32[128,256]{1,0:T(8,128)S(1)} %bitcast.35, f32[]{:T(128)} %constant.45, f32[128,256]{1,0:T(8,128)S(1)} %bitcast_multiply_fusion), kind=kCustom, calls=%fused_computation.22 | custom fusion | flops 65536 | bytes 1310728 | tf_op jit(solution)/shard_map/scatter | solution.py:72
  24.3 1.5 %reshape.32 = f32[128,2048]{1,0:T(8,128)} reshape(f32[512,512]{1,0:T(8,128)S(1)} %scatter_custom_fusion) | data formatting | bytes 2097152 | tf_op jit(solution)/shard_map/reshape | solution.py:79
  25.8 1.3 %select_maximum_fusion = f32[128,2176]{1,0:T(8,128)S(1)} fusion(f32[128,4]{1,0:T(8,128)S(1)} %reshape.33, f32[128,2048]{1,0:T(8,128)} %reshape.32), kind=kLoop, calls=%fused_computation.13 | loop fusion | flops 835584 | bytes 2164736 | tf_op jit(solution)/shard_map/concatenate | solution.py:78
  27.1 0.8 all_to_all.8
  27.8 31.6 %all_to_all.12 = f32[128,1,2176]{2,1,0:T(1,128)S(1)} all-to-all(f32[128,1,2176]{2,1,0:T(1,128)S(1)} %all_to_all.8), channel_id=1, replica_groups=mesh['bx'=4,'by'=8,'bz'=4] {'bx','by','bz'}, dimensions={0} | all-to-all | bytes 2228224 | tf_op jit(solution)/shard_map/all_to_all | solution.py:81
  59.4 0.0 copy-start.6
  59.4 0.1 copy.25
  59.5 0.0 copy-start.2
  59.5 0.0 copy-start.4
  59.5 0.0 copy-start.1
  59.6 1.1 %slice.17 = f32[128,2048]{1,0:T(8,128)} slice(f32[128,2176]{1,0:T(8,128)S(1)} %bitcast.34), slice={[0:128], [0:2048]} | slice | bytes 2097152 | tf_op jit(solution)/shard_map/slice | solution.py:82
  60.7 0.1 eq.129
  60.8 1.5 %reshape.34 = f32[512,512]{1,0:T(8,128)S(1)} reshape(f32[128,2048]{1,0:T(8,128)} %slice.17) | data formatting | bytes 2097152 | tf_op jit(solution)/shard_map/reshape | solution.py:82
  62.3 0.5 fusion.14
  62.8 1.0 %collective-permute-start = (f32[128,512]{1,0:T(8,128)S(1)}, f32[128,512]{1,0:T(8,128)S(1)}, u32[]{:S(2)}, u32[]{:S(2)}) collective-permute-start(f32[128,512]{1,0:T(8,128)S(1)} %fusion.14), channel_id=1, source_target_pairs={{0,96},{32,64},{64,32},{96,0},{1,97},{33,65},{65,33},{97,1},{2,98}... | collective-permute-start | bytes 786440 | tf_op jit(solution)/shard_map/ppermute | solution.py:23
  63.8 7.8 %collective-permute-done = f32[128,512]{1,0:T(8,128)S(1)} collective-permute-done((f32[128,512]{1,0:T(8,128)S(1)}, f32[128,512]{1,0:T(8,128)S(1)}, u32[]{:S(2)}, u32[]{:S(2)}) %collective-permute-start) | collective-permute-done | bytes 262176 | tf_op jit(solution)/shard_map/ppermute | solution.py:23
  71.6 0.0 copy-done.6
  71.6 0.3 fusion.18
  71.9 0.0 copy-done.3
  71.9 0.8 fusion.5
  72.7 1.2 %collective-permute-start.1 = (f32[128,512]{1,0:T(8,128)S(1)}, f32[128,512]{1,0:T(8,128)S(1)}, u32[]{:S(2)}, u32[]{:S(2)}) collective-permute-start(f32[128,512]{1,0:T(8,128)S(1)} %fusion.5), channel_id=1, source_target_pairs={{0,28},{4,24},{8,20},{12,16},{16,12},{20,8},{24,4},{28,0},{1,29},{... | collective-permute-start | bytes 786440 | tf_op jit(solution)/shard_map/ppermute | solution.py:23
  74.0 8.5 %collective-permute-done.1 = f32[128,512]{1,0:T(8,128)S(1)} collective-permute-done((f32[128,512]{1,0:T(8,128)S(1)}, f32[128,512]{1,0:T(8,128)S(1)}, u32[]{:S(2)}, u32[]{:S(2)}) %collective-permute-start.1) | collective-permute-done | bytes 262176 | tf_op jit(solution)/shard_map/ppermute | solution.py:23
  82.5 0.0 copy-done.5
  82.5 0.3 fusion.19
  82.8 0.0 copy-done.2
  82.8 0.8 fusion.4
  83.6 0.1 collective-permute-start.2
  83.7 8.2 %collective-permute-done.2 = f32[128,512]{1,0:T(8,128)S(1)} collective-permute-done((f32[128,512]{1,0:T(8,128)S(1)}, f32[128,512]{1,0:T(8,128)S(1)}, u32[]{:S(2)}, u32[]{:S(2)}) %collective-permute-start.2) | collective-permute-done | bytes 262176 | tf_op jit(solution)/shard_map/ppermute | solution.py:23
  91.8 0.0 copy-done.4
  91.8 0.3 fusion.20
  92.1 0.0 copy-done.1
  92.2 0.8 fusion.3
  92.9 0.7 fusion.15
  (3 shorter events, 0.0 us)
Async XLA Ops:
  0.0 14.8 %copy-start = (bf16[64,128,128]{2,1,0:T(8,128)(2,1)S(1)}, bf16[64,128,128]{2,1,0:T(8,128)(2,1)}, u32[]{:S(2)}) copy-start(bf16[64,128,128]{2,1,0:T(8,128)(2,1)} %param.17) | copy-start | bytes 6291460
  59.4 12.2 %copy-start.6 = (s32[128]{0:T(128)S(1)}, s32[128]{0:T(128)}, u32[]{:S(2)}) copy-start(s32[128]{0:T(128)} %constant.33.clone) | copy-start | bytes 1540
  59.4 12.5 %copy-start.3 = (s32[512]{0:T(512)S(1)}, s32[512]{0:T(512)}, u32[]{:S(2)}) copy-start(s32[512]{0:T(512)} %constant.34.clone) | copy-start | bytes 6148
  59.4 23.0 %copy-start.5 = (s32[128]{0:T(128)S(1)}, s32[128]{0:T(128)}, u32[]{:S(2)}) copy-start(s32[128]{0:T(128)} %constant.35.clone) | copy-start | bytes 1540
  59.5 23.3 %copy-start.2 = (s32[512]{0:T(512)S(1)}, s32[512]{0:T(512)}, u32[]{:S(2)}) copy-start(s32[512]{0:T(512)} %constant.36.clone) | copy-start | bytes 6148
  59.5 32.3 %copy-start.4 = (s32[128]{0:T(128)S(1)}, s32[128]{0:T(128)}, u32[]{:S(2)}) copy-start(s32[128]{0:T(128)} %constant.37.clone) | copy-start | bytes 1540
  59.5 32.6 %copy-start.1 = (s32[512]{0:T(512)S(1)}, s32[512]{0:T(512)}, u32[]{:S(2)}) copy-start(s32[512]{0:T(512)} %constant.38.clone) | copy-start | bytes 6148
  62.8 8.8 %collective-permute-start = (f32[128,512]{1,0:T(8,128)S(1)}, f32[128,512]{1,0:T(8,128)S(1)}, u32[]{:S(2)}, u32[]{:S(2)}) collective-permute-start(f32[128,512]{1,0:T(8,128)S(1)} %fusion.14), channel_id=1, source_target_pairs={{0,96},{32,64},{64,32},{96,0},{1,97},{33,65},{65,33},{97,1},{2,98}... | collective-permute-start | bytes 786440 | tf_op jit(solution)/shard_map/ppermute | solution.py:23
  72.7 9.7 %collective-permute-start.1 = (f32[128,512]{1,0:T(8,128)S(1)}, f32[128,512]{1,0:T(8,128)S(1)}, u32[]{:S(2)}, u32[]{:S(2)}) collective-permute-start(f32[128,512]{1,0:T(8,128)S(1)} %fusion.5), channel_id=1, source_target_pairs={{0,28},{4,24},{8,20},{12,16},{16,12},{20,8},{24,4},{28,0},{1,29},{... | collective-permute-start | bytes 786440 | tf_op jit(solution)/shard_map/ppermute | solution.py:23
  83.6 8.2 %collective-permute-start.2 = (f32[128,512]{1,0:T(8,128)S(1)}, f32[128,512]{1,0:T(8,128)S(1)}, u32[]{:S(2)}, u32[]{:S(2)}) collective-permute-start(f32[128,512]{1,0:T(8,128)S(1)} %fusion.4), channel_id=1, source_target_pairs={{0,3},{1,2},{2,1},{3,0},{4,7},{5,6},{6,5},{7,4},{8,11},{9,10},{10,... | collective-permute-start | bytes 786440 | tf_op jit(solution)/shard_map/ppermute | solution.py:23

commit v2 on v1

--- a/solution.py
+++ b/solution.py
@@ -3,6 +3,8 @@
 import jax.numpy as jnp
 from jax import lax
 from jax.sharding import PartitionSpec as P
+from jax.experimental import pallas as pl
+from jax.experimental.pallas import tpu as pltpu
 
 VX = 8
 VY = 8
@@ -42,6 +44,47 @@
     return 0.5 * (volume + moved)
 
 
+def tile_kernel(factor_ref, counts_ref, eff_ref, rows_ref, cols_ref, out_ref):
+    block, unused_pixels, voxels = rows_ref.shape
+    for t in range(block):
+        cols = cols_ref[t]
+        rows = rows_ref[t].astype(jnp.float32)
+        counted = jnp.dot(counts_ref[t], cols, preferred_element_type=jnp.float32)
+        seen = jnp.dot(eff_ref[t], cols, preferred_element_type=jnp.float32)
+        value = jnp.sum(rows * counted, axis=0, keepdims=True)
+        weight = jnp.sum(rows * seen, axis=0, keepdims=True)
+        out_ref[t : t + 1, :voxels] = value * factor_ref[t : t + 1, :]
+        out_ref[t : t + 1, voxels:] = weight
+
+
+def tile_payload(counts, row_split, col_split, efficiency, factor):
+    frames_here, tiles_frame, pixels, columns = counts.shape
+    voxels = row_split.shape[-1]
+    tiles_here = frames_here * tiles_frame
+    block = 8
+    per_frame = tiles_frame // block
+    tile_factor = jnp.repeat(factor, tiles_frame)[:, None]
+    return pl.pallas_call(
+        tile_kernel,
+        grid=(tiles_here // block,),
+        in_specs=[
+            pl.BlockSpec((block, 1), lambda i: (i, 0)),
+            pl.BlockSpec((block, pixels, columns), lambda i: (i, 0, 0)),
+            pl.BlockSpec((block, pixels, columns), lambda i: (i % per_frame, 0, 0)),
+            pl.BlockSpec((block, pixels, voxels), lambda i: (i, 0, 0)),
+            pl.BlockSpec((block, pixels, voxels), lambda i: (i, 0, 0)),
+        ],
+        out_specs=pl.BlockSpec((block, 2 * voxels), lambda i: (i, 0)),
+        out_shape=jax.ShapeDtypeStruct((tiles_here, 2 * voxels), jnp.float32),
+    )(
+        tile_factor,
+        counts.reshape(tiles_here, pixels, columns),
+        efficiency,
+        row_split.reshape(tiles_here, pixels, voxels),
+        col_split.reshape(tiles_here, pixels, voxels),
+    )
+
+
 def shards(counts, row_split, col_split, efficiency, lorentz, angles, tile_owner, tile_box):
     frames_here, tiles_frame, pixels, unused_width = counts.shape
     voxels = row_split.shape[-1]
@@ -57,13 +100,7 @@
     boxes_here = local_x * local_y * local_z * BOX_BRICK
     picks = angles[:, None] == jnp.arange(lorentz.shape[0], dtype=jnp.int32)[None, :]
     factor = jnp.sum(jnp.where(picks, lorentz[None, :], 0.0), axis=1)
-    counted = jnp.einsum("ftpq,ftqv->ftpv", counts, col_split, preferred_element_type=jnp.float32)
-    value = jnp.sum(row_split * counted, axis=2) * factor[:, None, None]
-    seen = jnp.einsum("tpq,ftqv->ftpv", efficiency, col_split, preferred_element_type=jnp.float32)
-    weight = jnp.sum(row_split * seen, axis=2)
-    payload = jnp.concatenate(
-        [value.reshape(tiles_here, voxels), weight.reshape(tiles_here, voxels)], axis=1
-    )
+    payload = tile_payload(counts, row_split, col_split, efficiency, factor)
     owner = tile_owner[:, 0]
     marks = (owner[:, None] == jnp.arange(devices_all, dtype=jnp.int32)[None, :]).astype(jnp.int32)
     before = jnp.cumsum(marks, axis=0) - marks

time: 94.2 us -> 90.1 us (0.956)
  matrix products: 21.3 us -> 3.8 us
  Pallas kernels: 0 us -> 16.6 us
  other arithmetic: 7.49 us -> 4.76 us
    dot_general x2 -> x0, matrix products: 17.5 us -> none  [the longest x1 9.33 us: shards(): jnp.einsum('ftpq,ftqv->ftpv', counts, col_split, preferred_element_type=j...]
    pallas_call x0 -> x1, Pallas kernels: none -> 16.6 us  [tile_payload(): pl.pallas_call(tile_kernel, grid=(tiles_here // block,), in_specs=[pl.Blo...]
    scatter x0 -> x1, local copies, waits for them, and re-layouts: none -> 1.68 us  [shards(): jnp.zeros((devices_all * capacity, 2 * voxels), jnp.float32).at[slot]]
    scatter x1 -> x0, other arithmetic: 1.28 us -> none  [shards(): jnp.zeros((devices_all * capacity, 2 * voxels), jnp.float32).at[slot]]
    reshape x1, local copies, waits for them, and re-layouts: 1.54 us -> 0.29 us  [shards(): arrived[:, :capacity * 2 * voxels]]
    concatenate x1, other arithmetic: 1.3 us -> 0.08 us  [shards(): jnp.concatenate([outgoing.reshape(devices_all, capacity * 2 * voxels), la...]
    slice x1, local copies, waits for them, and re-layouts: 1.09 us -> 0.09 us  [shards(): arrived[:, :capacity * 2 * voxels]]
    reshape x1, local copies, waits for them, and re-layouts: 1.46 us -> 0.47 us  [shards(): outgoing.reshape(devices_all, capacity * 2 * voxels)]
where the time goes in v2:
time: 90.1 us; the launch traced here: 89.1 us
  blocking collectives  31.6 us (35%)
  waiting for transfers between devices  24.4 us (27%)
  Pallas kernels  16.6 us (18%)
  local copies, waits for them, and re-layouts  5.46 us (6%)
  other arithmetic  4.76 us (5%)
  matrix products  3.8 us (4%)
  starting transfers between devices  2.27 us (3%)
    all_to_all x1, blocking collectives, shards(): lax.all_to_all(packed, ('bx', 'by', 'bz'), split_axis=0, concat_axis=0, t...  31.6 us
    ppermute x3, waiting for transfers between devices, mirrored(): return lax.ppermute(array, axis, [(i, size - 1 - i) for i in range(size)])  24.4 us
    pallas_call x1, Pallas kernels, tile_payload(): pl.pallas_call(tile_kernel, grid=(tiles_here // block,), in_specs=[pl.Blo...  16.6 us
    dot_general x3, matrix products, laue_step(): jnp.dot(moved, lanes, precision=lax.Precision.HIGHEST, preferred_element_...  2.35 us
    ppermute x3, starting transfers between devices, mirrored(): return lax.ppermute(array, axis, [(i, size - 1 - i) for i in range(size)])  2.27 us
  transfers between devices with their start and end apart: 3, of which 3 were waited for; matrix products, arithmetic and copies ran while one was open for 0% of the time, Pallas kernels for 0%

profile of v2, /device:TPU:1, one launch (start us, length us, event | category | flops | bytes accessed | tf_op | source)
XLA Modules:
  0.0 89.1 jit_solution(2898109545955784025)
XLA Ops:
  0.0 0.7 convert_element_type.7
  0.7 0.9 %fusion.18 = f32[2]{0:T(128)S(1)} fusion(s32[2]{0:T(128)} %param.19, f32[3600]{0:T(1024)} %param.18), kind=kLoop, calls=%fused_computation.37 | loop fusion | flops 21598 | bytes 14416 | tf_op jit(solution)/shard_map/reduce_sum | solution.py:102
  1.6 0.1 broadcast_in_dim.21
  1.7 0.8 broadcast_in_dim_reshape.5.factor_ref
  2.4 0.7 fusion.11
  3.2 0.2 reduce_window_sum.11
  3.4 0.8 select_reduce_fusion
  4.2 0.7 fusion.21
  4.9 1.0 %scatter_custom_fusion.1 = f32[512]{0:T(512)S(1)} fusion(s32[128]{0:T(128)S(1)} %fusion.21, f32[128]{0:T(128)S(1)} %convert_element_type.7, f32[]{:T(128)} %constant.11.clone.1), kind=kCustom, calls=%fused_computation.39 | custom fusion | bytes 2052 | tf_op jit(solution)/shard_map/scatter | solution.py:110
  5.8 0.1 reshape.37
  6.0 16.6 %shard_map.136 = f32[128,512]{1,0:T(8,128)} custom-call(f32[128,1]{1,0:T(8,128)} %broadcast_in_dim_reshape.5.factor_ref, bf16[128,128,128]{2,1,0:T(8,128)(2,1)} %bitcast.29, bf16[64,128,128]{2,1,0:T(8,128)(2,1)} %eff_ref.1, bf16[128,128,256]{2,1,0:T(8,128)(2,1)} %bitcast.25, bf16[128,128,256]{2,1,0:T(8,128)(2,1)} %bitcast.26), custom_call_target="tpu_custom_call" | custom-call | tf_op jit(solution)/shard_map/pallas_call | solution.py:67
  22.5 1.7 %scatter_custom_fusion = f32[512,512]{1,0:T(8,128)S(1)} fusion(s32[128]{0:T(128)S(1)} %fusion.21, f32[128,512]{1,0:T(8,128)} %shard_map.136, f32[]{:T(128)} %constant.13.clone.1), kind=kCustom, calls=%fused_computation.17 | custom fusion | bytes 1049088 | tf_op jit(solution)/shard_map/scatter | solution.py:109
  24.2 0.5 reshape.36
  24.7 0.1 select_maximum_fusion
  24.8 0.8 all_to_all.8
  25.6 31.6 %all_to_all.12 = f32[128,1,2176]{2,1,0:T(1,128)S(1)} all-to-all(f32[128,1,2176]{2,1,0:T(1,128)S(1)} %all_to_all.8), channel_id=1, replica_groups=mesh['bx'=4,'by'=8,'bz'=4] {'bx','by','bz'}, dimensions={0} | all-to-all | bytes 2228224 | tf_op jit(solution)/shard_map/all_to_all | solution.py:118
  57.2 0.1 copy.25
  57.2 0.1 slice.17
  57.3 0.1 eq.129
  57.5 0.3 reshape.38
  57.8 0.0 copy-start.5
  57.8 0.0 copy-start.2
  57.8 0.0 copy-start.4
  57.8 0.5 fusion.8
  58.3 0.0 copy-start.1
  58.3 1.0 %collective-permute-start = (f32[128,512]{1,0:T(8,128)S(1)}, f32[128,512]{1,0:T(8,128)S(1)}, u32[]{:S(2)}, u32[]{:S(2)}) collective-permute-start(f32[128,512]{1,0:T(8,128)S(1)} %fusion.8), channel_id=1, source_target_pairs={{0,96},{32,64},{64,32},{96,0},{1,97},{33,65},{65,33},{97,1},{2,98}... | collective-permute-start | bytes 786440 | tf_op jit(solution)/shard_map/ppermute | solution.py:25
  59.3 7.8 %collective-permute-done = f32[128,512]{1,0:T(8,128)S(1)} collective-permute-done((f32[128,512]{1,0:T(8,128)S(1)}, f32[128,512]{1,0:T(8,128)S(1)}, u32[]{:S(2)}, u32[]{:S(2)}) %collective-permute-start) | collective-permute-done | bytes 262176 | tf_op jit(solution)/shard_map/ppermute | solution.py:25
  67.1 0.0 copy-done.5
  67.1 0.3 fusion.12
  67.4 0.0 copy-done.2
  67.4 0.0 copy-start.3
  67.5 0.8 fusion.2
  68.2 0.0 copy-start
  68.3 1.2 %collective-permute-start.1 = (f32[128,512]{1,0:T(8,128)S(1)}, f32[128,512]{1,0:T(8,128)S(1)}, u32[]{:S(2)}, u32[]{:S(2)}) collective-permute-start(f32[128,512]{1,0:T(8,128)S(1)} %fusion.2), channel_id=1, source_target_pairs={{0,28},{4,24},{8,20},{12,16},{16,12},{20,8},{24,4},{28,0},{1,29},{... | collective-permute-start | bytes 786440 | tf_op jit(solution)/shard_map/ppermute | solution.py:25
  69.5 8.5 %collective-permute-done.1 = f32[128,512]{1,0:T(8,128)S(1)} collective-permute-done((f32[128,512]{1,0:T(8,128)S(1)}, f32[128,512]{1,0:T(8,128)S(1)}, u32[]{:S(2)}, u32[]{:S(2)}) %collective-permute-start.1) | collective-permute-done | bytes 262176 | tf_op jit(solution)/shard_map/ppermute | solution.py:25
  78.0 0.0 copy-done.4
  78.0 0.3 fusion.13
  78.3 0.0 copy-done.1
  78.3 0.8 fusion.1
  79.1 0.1 collective-permute-start.2
  79.2 8.1 %collective-permute-done.2 = f32[128,512]{1,0:T(8,128)S(1)} collective-permute-done((f32[128,512]{1,0:T(8,128)S(1)}, f32[128,512]{1,0:T(8,128)S(1)}, u32[]{:S(2)}, u32[]{:S(2)}) %collective-permute-start.2) | collective-permute-done | bytes 262176 | tf_op jit(solution)/shard_map/ppermute | solution.py:25
  87.3 0.0 copy-done.3
  87.3 0.3 fusion.14
  87.6 0.0 copy-done
  87.7 0.8 fusion
  88.4 0.7 fusion.9
  (1 shorter events, 0.0 us)
Async XLA Ops:
  57.8 9.4 %copy-start.5 = (s32[128]{0:T(128)S(1)}, s32[128]{0:T(128)}, u32[]{:S(2)}) copy-start(s32[128]{0:T(128)} %constant.33.clone) | copy-start | bytes 1540
  57.8 9.7 %copy-start.2 = (s32[512]{0:T(512)S(1)}, s32[512]{0:T(512)}, u32[]{:S(2)}) copy-start(s32[512]{0:T(512)} %constant.34.clone) | copy-start | bytes 6148
  57.8 20.2 %copy-start.4 = (s32[128]{0:T(128)S(1)}, s32[128]{0:T(128)}, u32[]{:S(2)}) copy-start(s32[128]{0:T(128)} %constant.35.clone) | copy-start | bytes 1540
  58.3 20.0 %copy-start.1 = (s32[512]{0:T(512)S(1)}, s32[512]{0:T(512)}, u32[]{:S(2)}) copy-start(s32[512]{0:T(512)} %constant.36.clone) | copy-start | bytes 6148
  58.3 8.8 %collective-permute-start = (f32[128,512]{1,0:T(8,128)S(1)}, f32[128,512]{1,0:T(8,128)S(1)}, u32[]{:S(2)}, u32[]{:S(2)}) collective-permute-start(f32[128,512]{1,0:T(8,128)S(1)} %fusion.8), channel_id=1, source_target_pairs={{0,96},{32,64},{64,32},{96,0},{1,97},{33,65},{65,33},{97,1},{2,98}... | collective-permute-start | bytes 786440 | tf_op jit(solution)/shard_map/ppermute | solution.py:25
  67.4 19.9 %copy-start.3 = (s32[128]{0:T(128)S(1)}, s32[128]{0:T(128)}, u32[]{:S(2)}) copy-start(s32[128]{0:T(128)} %constant.37.clone) | copy-start | bytes 1540
  68.2 19.4 %copy-start = (s32[512]{0:T(512)S(1)}, s32[512]{0:T(512)}, u32[]{:S(2)}) copy-start(s32[512]{0:T(512)} %constant.38.clone) | copy-start | bytes 6148
  68.3 9.7 %collective-permute-start.1 = (f32[128,512]{1,0:T(8,128)S(1)}, f32[128,512]{1,0:T(8,128)S(1)}, u32[]{:S(2)}, u32[]{:S(2)}) collective-permute-start(f32[128,512]{1,0:T(8,128)S(1)} %fusion.2), channel_id=1, source_target_pairs={{0,28},{4,24},{8,20},{12,16},{16,12},{20,8},{24,4},{28,0},{1,29},{... | collective-permute-start | bytes 786440 | tf_op jit(solution)/shard_map/ppermute | solution.py:25
  79.1 8.2 %collective-permute-start.2 = (f32[128,512]{1,0:T(8,128)S(1)}, f32[128,512]{1,0:T(8,128)S(1)}, u32[]{:S(2)}, u32[]{:S(2)}) collective-permute-start(f32[128,512]{1,0:T(8,128)S(1)} %fusion.1), channel_id=1, source_target_pairs={{0,3},{1,2},{2,1},{3,0},{4,7},{5,6},{6,5},{7,4},{8,11},{9,10},{10,... | collective-permute-start | bytes 786440 | tf_op jit(solution)/shard_map/ppermute | solution.py:25

commit v3 on v2

--- a/solution.py
+++ b/solution.py
@@ -1,3 +1,5 @@
+import functools
+
 import numpy as np
 import jax
 import jax.numpy as jnp
@@ -18,30 +20,97 @@
 BOX_BRICK = 64
 
 
-def mirrored(array, axis):
-    size = lax.axis_size(axis)
-    if size == 1:
-        return array
-    return lax.ppermute(array, axis, [(i, size - 1 - i) for i in range(size)])
-
-
-def flip_table(sizes, flipped):
-    index = np.arange(int(np.prod(sizes))).reshape(sizes)
-    return np.flip(index, flipped).reshape(-1).astype(np.int32)
-
-
-def permuting(table):
-    size = table.shape[0]
-    return (jnp.asarray(table)[:, None] == lax.iota(jnp.int32, size)[None, :]).astype(jnp.float32)
-
-
-def laue_step(volume, axis, row_table, lane_table):
-    partner = mirrored(volume, axis)
-    rows = permuting(row_table)
-    lanes = permuting(np.concatenate([lane_table, lane_table + lane_table.shape[0]])).T
-    moved = jnp.dot(rows, partner, precision=lax.Precision.HIGHEST, preferred_element_type=jnp.float32)
-    moved = jnp.dot(moved, lanes, precision=lax.Precision.HIGHEST, preferred_element_type=jnp.float32)
-    return 0.5 * (volume + moved)
+def digits_flipped(index, sizes, flipped):
+    result = jnp.zeros_like(index)
+    stride = 1
+    rest = index
+    for dim in reversed(range(len(sizes))):
+        digit = rest % sizes[dim]
+        rest = rest // sizes[dim]
+        if dim in flipped:
+            digit = sizes[dim] - 1 - digit
+        result = result + digit * stride
+        stride = stride * sizes[dim]
+    return result
+
+
+def flip_matrices(row_sizes, lane_sizes, stage):
+    rows = int(np.prod(row_sizes))
+    lanes = int(np.prod(lane_sizes))
+    out_row = lax.broadcasted_iota(jnp.int32, (rows, rows), 0)
+    in_row = lax.broadcasted_iota(jnp.int32, (rows, rows), 1)
+    row_flip = (in_row == digits_flipped(out_row, row_sizes, (stage, stage + 3))).astype(jnp.float32)
+    in_lane = lax.broadcasted_iota(jnp.int32, (lanes, lanes), 0)
+    out_lane = lax.broadcasted_iota(jnp.int32, (lanes, lanes), 1)
+    lane_flip = (in_lane == digits_flipped(out_lane, lane_sizes, (stage,))).astype(jnp.float32)
+    return row_flip, lane_flip
+
+
+def flipped_volume(volume, row_flip, lane_flip, voxels):
+    exact = lax.Precision.HIGHEST
+    moved = jnp.dot(row_flip, volume, precision=exact, preferred_element_type=jnp.float32)
+    value = jnp.dot(moved[:, :voxels], lane_flip, precision=exact, preferred_element_type=jnp.float32)
+    weight = jnp.dot(moved[:, voxels:], lane_flip, precision=exact, preferred_element_type=jnp.float32)
+    return value, weight
+
+
+def laue_kernel(row_sizes, lane_sizes, sums_ref, out_ref, received, held, send_sems, recv_sems):
+    voxels = int(np.prod(lane_sizes))
+    axes = ("bx", "by", "bz")
+    here = tuple(lax.axis_index(axis) for axis in axes)
+    sizes = tuple(lax.axis_size(axis) for axis in axes)
+    partners = []
+    for stage in range(3):
+        partner = list(here)
+        partner[stage] = sizes[stage] - 1 - here[stage]
+        partners.append(tuple(partner))
+    remote = [stage for stage in range(3) if sizes[stage] > 1]
+    if remote:
+        barrier = pltpu.get_barrier_semaphore()
+        for stage in remote:
+            pl.semaphore_signal(
+                barrier, 1, device_id=partners[stage], device_id_type=pl.DeviceIdType.MESH
+            )
+        pl.semaphore_wait(barrier, len(remote))
+    current = sums_ref
+    for stage in range(3):
+        source = current
+        if stage in remote:
+            copy = pltpu.make_async_remote_copy(
+                src_ref=current,
+                dst_ref=received.at[stage],
+                send_sem=send_sems.at[stage],
+                recv_sem=recv_sems.at[stage],
+                device_id=partners[stage],
+                device_id_type=pl.DeviceIdType.MESH,
+            )
+            copy.start()
+            copy.wait()
+            source = received.at[stage]
+        row_flip, lane_flip = flip_matrices(row_sizes, lane_sizes, stage)
+        value, weight = flipped_volume(source[...], row_flip, lane_flip, voxels)
+        held[stage, :, :voxels] = 0.5 * (current[:, :voxels] + value)
+        held[stage, :, voxels:] = 0.5 * (current[:, voxels:] + weight)
+        current = held.at[stage]
+    out_ref[...] = current[:, :voxels] / jnp.maximum(current[:, voxels:], 1.0)
+
+
+def laue_average(sums, row_sizes, lane_sizes):
+    rows, width = sums.shape
+    voxels = width // 2
+    return pl.pallas_call(
+        functools.partial(laue_kernel, row_sizes, lane_sizes),
+        in_specs=[pl.BlockSpec(memory_space=pltpu.VMEM)],
+        out_specs=pl.BlockSpec(memory_space=pltpu.VMEM),
+        out_shape=jax.ShapeDtypeStruct((rows, voxels), jnp.float32),
+        scratch_shapes=[
+            pltpu.VMEM((3, rows, width), jnp.float32),
+            pltpu.VMEM((3, rows, width), jnp.float32),
+            pltpu.SemaphoreType.DMA((3,)),
+            pltpu.SemaphoreType.DMA((3,)),
+        ],
+        compiler_params=pltpu.CompilerParams(collective_id=0, has_side_effects=True),
+    )(sums)
 
 
 def tile_kernel(factor_ref, counts_ref, eff_ref, rows_ref, cols_ref, out_ref):
@@ -128,10 +197,7 @@
     )
     row_sizes = (local_x, local_y, local_z, BOXX, BOXY, BOXZ)
     lane_sizes = (VX, VY, VZ)
-    volume = laue_step(sums, "bx", flip_table(row_sizes, (0, 3)), flip_table(lane_sizes, (0,)))
-    volume = laue_step(volume, "by", flip_table(row_sizes, (1, 4)), flip_table(lane_sizes, (1,)))
-    volume = laue_step(volume, "bz", flip_table(row_sizes, (2, 5)), flip_table(lane_sizes, (2,)))
-    result = volume[:, :voxels] / jnp.maximum(volume[:, voxels:], 1.0)
+    result = laue_average(sums, row_sizes, lane_sizes)
     return result.reshape(local_x, local_y, local_z, BOX_BRICK, voxels)
 
 

time: 90.1 us -> 89.7 us (level)
  Pallas kernels: 16.6 us -> 45.1 us
  waiting for transfers between devices: 24.4 us -> 0 us
  matrix products: 3.8 us -> 1.22 us
  starting transfers between devices: 2.27 us -> 0 us
  local copies, waits for them, and re-layouts: 5.46 us -> 6.98 us
    pallas_call x0 -> x1, Pallas kernels: none -> 28.5 us  [laue_average(): pl.pallas_call(functools.partial(laue_kernel, row_sizes, lane_sizes), in_...]
    ppermute x3 -> x0, waiting for transfers between devices: 24.4 us -> none  [mirrored(): return lax.ppermute(array, axis, [(i, size - 1 - i) for i in range(size)])]
    dot_general x6 -> x0, matrix products: 3.28 us -> none  [the longest x3 2.35 us: laue_step(): jnp.dot(moved, lanes, precision=lax.Precision.HIGHEST, preferred_element_...]
    ppermute x3 -> x0, starting transfers between devices: 2.27 us -> none  [mirrored(): return lax.ppermute(array, axis, [(i, size - 1 - i) for i in range(size)])]
    unnamed x13 -> x2, local copies, waits for them, and re-layouts: 0.11 us -> 1.64 us
  transfers between devices with their start and end apart: 3 -> 0, of which waited for: 3 -> 0; matrix products, arithmetic and copies ran while one was open for 0% -> 0% of each run, Pallas kernels for 0% -> 0%
where the time goes in v3:
time: 89.7 us; the launch traced here: 89.1 us
  Pallas kernels  45.1 us (50%)
  blocking collectives  31.6 us (35%)
  local copies, waits for them, and re-layouts  6.98 us (8%)
  other arithmetic  4.08 us (5%)
  matrix products  1.22 us (1%)
    all_to_all x1, blocking collectives, shards(): lax.all_to_all(packed, ('bx', 'by', 'bz'), split_axis=0, concat_axis=0, t...  31.6 us
    pallas_call x1, Pallas kernels, laue_average(): pl.pallas_call(functools.partial(laue_kernel, row_sizes, lane_sizes), in_...  28.5 us
    pallas_call x1, Pallas kernels, tile_payload(): pl.pallas_call(tile_kernel, grid=(tiles_here // block,), in_specs=[pl.Blo...  16.6 us

profile of v3, /device:TPU:1, one launch (start us, length us, event | category | flops | bytes accessed | tf_op | source)
XLA Modules:
  0.0 89.1 jit_solution(12252904295869996956)
XLA Ops:
  0.0 0.7 convert_element_type.10
  0.7 0.9 %fusion.5 = f32[2]{0:T(128)S(1)} fusion(s32[2]{0:T(128)} %param.13, f32[3600]{0:T(1024)} %param.12), kind=kLoop, calls=%fused_computation.14 | loop fusion | flops 21598 | bytes 14416 | tf_op jit(solution)/shard_map/reduce_sum | solution.py:171
  1.6 0.1 broadcast_in_dim.31
  1.7 0.8 broadcast_in_dim_reshape.5.factor_ref
  2.4 0.7 fusion.4
  3.2 0.2 reduce_window_sum.11
  3.4 0.8 select_reduce_fusion
  4.2 0.7 fusion.8
  4.9 1.0 %scatter_custom_fusion.1 = f32[512]{0:T(512)S(1)} fusion(s32[128]{0:T(128)S(1)} %fusion.8, f32[128]{0:T(128)S(1)} %convert_element_type.10, f32[]{:T(128)} %constant.16.clone.1), kind=kCustom, calls=%fused_computation.16 | custom fusion | bytes 2052 | tf_op jit(solution)/shard_map/scatter | solution.py:179
  5.8 0.1 reshape.31
  6.0 16.6 %shard_map.82 = f32[128,512]{1,0:T(8,128)} custom-call(f32[128,1]{1,0:T(8,128)} %broadcast_in_dim_reshape.5.factor_ref, bf16[128,128,128]{2,1,0:T(8,128)(2,1)} %bitcast.23, bf16[64,128,128]{2,1,0:T(8,128)(2,1)} %eff_ref.1, bf16[128,128,256]{2,1,0:T(8,128)(2,1)} %bitcast.19, bf16[128,128,256]{2,1,0:T(8,128)(2,1)} %bitcast.20), custom_call_target="tpu_custom_call" | custom-call | tf_op jit(solution)/shard_map/pallas_call | solution.py:136
  22.5 1.7 %scatter_custom_fusion = f32[512,512]{1,0:T(8,128)S(1)} fusion(s32[128]{0:T(128)S(1)} %fusion.8, f32[128,512]{1,0:T(8,128)} %shard_map.82, f32[]{:T(128)} %constant.5.clone.1), kind=kCustom, calls=%fused_computation.5 | custom fusion | bytes 1049088 | tf_op jit(solution)/shard_map/scatter | solution.py:178
  24.2 0.5 reshape.30
  24.7 0.1 select_maximum_fusion
  24.8 0.8 all_to_all.8
  25.6 31.6 %all_to_all.12 = f32[128,1,2176]{2,1,0:T(1,128)S(1)} all-to-all(f32[128,1,2176]{2,1,0:T(1,128)S(1)} %all_to_all.8), channel_id=1, replica_groups=mesh['bx'=4,'by'=8,'bz'=4] {'bx','by','bz'}, dimensions={0} | all-to-all | bytes 2228224 | tf_op jit(solution)/shard_map/all_to_all | solution.py:187
  57.2 0.1 copy.19
  57.2 0.1 slice.9
  57.3 0.1 eq.51
  57.5 0.3 reshape.32
  57.8 1.2 %fusion.2.sums_ref = f32[128,512]{1,0:T(8,128)} fusion(f32[512,512]{1,0:T(8,128)S(1)} %reshape.32, f32[512]{0:T(512)S(1)} %eq.51), kind=kOutput, calls=%fused_computation.8 | convolution fusion | flops 402718720 | bytes 1312768 | tf_op jit(solution)/shard_map/dot_general | solution.py:195
  59.0 28.5 %shard_map.83 = f32[128,256]{1,0:T(8,128)} custom-call(f32[128,512]{1,0:T(8,128)} %fusion.2.sums_ref), custom_call_target="tpu_custom_call" | custom-call | tf_op jit(solution)/shard_map/pallas_call | solution.py:101
  87.5 1.6 %copy.21 = f32[2,1,1,64,256]{4,3,2,1,0:T(8,128)} copy(f32[2,1,1,64,256]{4,3,2,1,0:T(8,128)} %bitcast.24) | data formatting | bytes 262144
  (1 shorter events, 0.0 us)

commit v4 on v3

--- a/solution.py
+++ b/solution.py
@@ -154,6 +154,67 @@
     )
 
 
+def flat_device(flat, sizes):
+    return (flat // (sizes[1] * sizes[2]), (flat // sizes[2]) % sizes[1], flat % sizes[2])
+
+
+def exchange_kernel(packed_ref, arrived_ref, inbox, send_sem, recv_sem):
+    axes = ("bx", "by", "bz")
+    sizes = tuple(lax.axis_size(axis) for axis in axes)
+    count = sizes[0] * sizes[1] * sizes[2]
+    me = (lax.axis_index("bx") * sizes[1] + lax.axis_index("by")) * sizes[2] + lax.axis_index("bz")
+    barrier = pltpu.get_barrier_semaphore()
+
+    def greet(step, carry):
+        target = flat_device((me + step) % count, sizes)
+        pl.semaphore_signal(barrier, 1, device_id=target, device_id_type=pl.DeviceIdType.MESH)
+        return carry
+
+    lax.fori_loop(1, count, greet, 0)
+    pl.semaphore_wait(barrier, count - 1)
+
+    def send(step, carry):
+        target = (me + step) % count
+        pltpu.make_async_remote_copy(
+            src_ref=packed_ref.at[target],
+            dst_ref=inbox.at[me],
+            send_sem=send_sem,
+            recv_sem=recv_sem,
+            device_id=flat_device(target, sizes),
+            device_id_type=pl.DeviceIdType.MESH,
+        ).start()
+        return carry
+
+    lax.fori_loop(1, count, send, 0)
+    every = pltpu.make_async_remote_copy(
+        src_ref=packed_ref.at[pl.ds(0, count - 1)],
+        dst_ref=inbox.at[pl.ds(0, count - 1)],
+        send_sem=send_sem,
+        recv_sem=recv_sem,
+        device_id=flat_device((me + 1) % count, sizes),
+        device_id_type=pl.DeviceIdType.MESH,
+    )
+    every.wait_send()
+    every.wait_recv()
+    arrived_ref[...] = inbox[...]
+    arrived_ref[me] = packed_ref[me]
+
+
+def exchange(packed):
+    return pl.pallas_call(
+        exchange_kernel,
+        in_specs=[pl.BlockSpec(memory_space=pltpu.VMEM)],
+        out_specs=pl.BlockSpec(memory_space=pltpu.VMEM),
+        out_shape=jax.ShapeDtypeStruct(packed.shape, packed.dtype),
+        scratch_shapes=[
+            pltpu.VMEM(packed.shape, packed.dtype),
+            pltpu.SemaphoreType.DMA(()),
+            pltpu.SemaphoreType.DMA(()),
+        ],
+        compiler_params=pltpu.CompilerParams(collective_id=1, has_side_effects=True),
+    )(packed)
+
+
 def shards(counts, row_split, col_split, efficiency, lorentz, angles, tile_owner, tile_box):
     frames_here, tiles_frame, pixels, unused_width = counts.shape
     voxels = row_split.shape[-1]
@@ -176,21 +237,21 @@
     rank = jnp.sum(before * marks, axis=1)
     slot = owner * capacity + rank
     outgoing = jnp.zeros((devices_all * capacity, 2 * voxels), jnp.float32).at[slot].set(payload)
-    labels = jnp.full((devices_all * capacity,), -1.0, jnp.float32).at[slot].set(
-        tile_box.astype(jnp.float32)
-    )
-    label_width = 128
-    labels = jnp.pad(labels.reshape(devices_all, capacity), ((0, 0), (0, label_width - capacity)))
-    packed = jnp.concatenate(
-        [outgoing.reshape(devices_all, capacity * 2 * voxels), labels], axis=1
-    )
-    arrived = lax.all_to_all(packed, ("bx", "by", "bz"), split_axis=0, concat_axis=0, tiled=True)
-    arrived_payload = arrived[:, : capacity * 2 * voxels].reshape(devices_all * capacity, 2 * voxels)
-    arrived_ids = arrived[:, capacity * 2 * voxels : capacity * 2 * voxels + capacity].reshape(
-        devices_all * capacity
-    )
+    arrived = exchange(outgoing.reshape(devices_all, capacity * 2, voxels))
+    arrived_payload = arrived.reshape(devices_all * capacity, 2 * voxels)
+    ids = jnp.concatenate([owner, tile_box])
+    everyone = lax.all_gather(ids, ("bx", "by", "bz"), tiled=True).reshape(devices_all, 2, tiles_here)
+    me = (lax.axis_index("bx") * size_y + lax.axis_index("by")) * size_z + lax.axis_index("bz")
+    mine = everyone[:, 0, :] == me
+    order = jnp.cumsum(mine.astype(jnp.int32), axis=1) - 1
+    labels = []
+    for k in range(capacity):
+        hit = mine & (order == k)
+        found = jnp.sum(jnp.where(hit, everyone[:, 1, :], 0), axis=1)
+        labels.append(jnp.where(jnp.any(hit, axis=1), found, -1))
+    arrived_ids = jnp.stack(labels, axis=1).reshape(devices_all * capacity)
     wanted = (
-        jnp.arange(boxes_here, dtype=jnp.float32)[:, None] == arrived_ids[None, :]
+        jnp.arange(boxes_here, dtype=jnp.int32)[:, None] == arrived_ids[None, :]
     ).astype(jnp.float32)
     sums = jnp.dot(
         wanted, arrived_payload, precision=lax.Precision.HIGHEST, preferred_element_type=jnp.float32

time: 89.7 us -> 141 us (1.57)
  Pallas kernels: 45.1 us -> 74.9 us
  blocking collectives: 31.6 us -> 53 us
    all_gather x0 -> x1, blocking collectives: none -> 53 us  [shards(): lax.all_gather(ids, ('bx', 'by', 'bz'), tiled=True)]
    all_to_all x1 -> x0, blocking collectives: 31.6 us -> none  [shards(): lax.all_to_all(packed, ('bx', 'by', 'bz'), split_axis=0, concat_axis=0, t...]
    pallas_call x0 -> x1, Pallas kernels: none -> 29.1 us  [exchange(): pl.pallas_call(exchange_kernel, in_specs=[pl.BlockSpec(memory_space=pltpu...]
    reshape x3 -> x2, local copies, waits for them, and re-layouts: 0.87 us -> 2.69 us  [the longest x1 1.54 us: shards(): arrived_payload = arrived.reshape(devices_all * capacity, 2 * voxels)]
where the time goes in v4:
time: 141 us; the launch traced here: 140 us
  Pallas kernels  74.9 us (53%)
  blocking collectives  53 us (38%)
  local copies, waits for them, and re-layouts  7.29 us (5%)
  other arithmetic  3.52 us (2%)
    all_gather x1, blocking collectives, shards(): lax.all_gather(ids, ('bx', 'by', 'bz'), tiled=True)  53 us
    pallas_call x1, Pallas kernels, laue_average(): pl.pallas_call(functools.partial(laue_kernel, row_sizes, lane_sizes), in_...  29.3 us
    pallas_call x1, Pallas kernels, exchange(): pl.pallas_call(exchange_kernel, in_specs=[pl.BlockSpec(memory_space=pltpu...  29.1 us
    pallas_call x1, Pallas kernels, tile_payload(): pl.pallas_call(tile_kernel, grid=(tiles_here // block,), in_specs=[pl.Blo...  16.6 us

profile of v4, /device:TPU:1, one launch (start us, length us, event | category | flops | bytes accessed | tf_op | source)
XLA Modules:
  0.0 140.0 jit_solution(7507712103651633428)
XLA Ops:
  0.0 0.7 fusion.4
  0.7 0.1 copy.27
  0.8 0.2 reduce_window_sum.23
  0.9 0.1 copy.28
  1.0 0.7 select_reduce_fusion
  1.7 0.7 fusion.7
  2.4 0.9 fusion.6
  3.3 0.1 broadcast_in_dim.40
  3.4 0.8 broadcast_in_dim_reshape.5.factor_ref
  4.2 0.0 copy-start
  4.2 0.0 copy-start.1
  4.2 16.6 %shard_map.82 = f32[128,512]{1,0:T(8,128)} custom-call(f32[128,1]{1,0:T(8,128)} %broadcast_in_dim_reshape.5.factor_ref, bf16[128,128,128]{2,1,0:T(8,128)(2,1)} %bitcast.39, bf16[64,128,128]{2,1,0:T(8,128)(2,1)} %eff_ref.1, bf16[128,128,256]{2,1,0:T(8,128)(2,1)} %bitcast.37, bf16[128,128,256]{2,1,0:T(8,128)(2,1)} %bitcast.38), custom_call_target="tpu_custom_call" | custom-call | tf_op jit(solution)/shard_map/pallas_call | solution.py:136
  20.8 1.7 %scatter_custom_fusion = f32[512,512]{1,0:T(8,128)S(1)} fusion(s32[128]{0:T(128)S(1)} %fusion.7, f32[128,512]{1,0:T(8,128)} %shard_map.82, f32[]{:T(128)} %constant.43.clone.1), kind=kCustom, calls=%fused_computation.1 | custom fusion | bytes 1049088 | tf_op jit(solution)/shard_map/scatter | solution.py:239
  22.4 1.1 reshape.83.packed_ref
  23.6 29.1 %shard_map.83 = f32[128,8,256]{2,1,0:T(8,128)} custom-call(f32[128,8,256]{2,1,0:T(8,128)} %reshape.83.packed_ref), custom_call_target="tpu_custom_call" | custom-call | tf_op jit(solution)/shard_map/pallas_call | solution.py:204
  52.7 1.5 %reshape.84 = f32[512,512]{1,0:T(8,128)S(1)} reshape(f32[128,8,256]{2,1,0:T(8,128)} %shard_map.83) | data formatting | bytes 2097152 | tf_op jit(solution)/shard_map/reshape | solution.py:241
  54.2 0.0 copy-done
  54.2 0.0 copy-done.1
  54.3 53.0 %all-gather = s32[128,1,256]{2,1,0:T(1,128)S(1)} all-gather(s32[1,1,256]{2,1,0:T(1,128)S(1)} %bitcast.46), channel_id=1, replica_groups=mesh['bx'=4,'by'=8,'bz'=4] {'bx','by','bz'}, dimensions={0}, use_global_device_ids=true | all-gather | bytes 132096 | tf_op jit(solution)/shard_map/all_gather | solution.py:243
  107.2 0.1 copy.25
  107.4 0.2 reduce_window_sum.22
  107.5 0.1 fusion.10
  107.6 0.1 select_reduce_fusion.4
  107.7 0.1 copy.26
  107.9 0.1 eq.82
  108.0 1.2 fusion.2.sums_ref
  109.2 29.3 %shard_map.84 = f32[128,256]{1,0:T(8,128)} custom-call(f32[128,512]{1,0:T(8,128)} %fusion.2.sums_ref), custom_call_target="tpu_custom_call" | custom-call | tf_op jit(solution)/shard_map/pallas_call | solution.py:101
  138.5 1.6 %copy.32 = f32[2,1,1,64,256]{4,3,2,1,0:T(8,128)} copy(f32[2,1,1,64,256]{4,3,2,1,0:T(8,128)} %bitcast.40) | data formatting | bytes 262144
  (6 shorter events, 0.1 us)
Async XLA Ops:
  4.2 50.1 %copy-start = (s32[128,1]{0,1:T(1,128)S(1)}, s32[128,1]{0,1:T(1,128)}, u32[]{:S(2)}) copy-start(s32[128,1]{0,1:T(1,128)} %param.14) | copy-start | bytes 1540
  4.2 50.1 %copy-start.1 = (s32[128]{0:T(128)S(1)}, s32[128]{0:T(128)}, u32[]{:S(2)}) copy-start(s32[128]{0:T(128)} %param.15) | copy-start | bytes 1540

commit v5 on v3

--- a/solution.py
+++ b/solution.py
@@ -46,12 +46,18 @@
     return row_flip, lane_flip
 
 
-def flipped_volume(volume, row_flip, lane_flip, voxels):
+def flipped(pair, row_sizes, lane_sizes, stage):
     exact = lax.Precision.HIGHEST
-    moved = jnp.dot(row_flip, volume, precision=exact, preferred_element_type=jnp.float32)
-    value = jnp.dot(moved[:, :voxels], lane_flip, precision=exact, preferred_element_type=jnp.float32)
-    weight = jnp.dot(moved[:, voxels:], lane_flip, precision=exact, preferred_element_type=jnp.float32)
-    return value, weight
+    row_flip, lane_flip = flip_matrices(row_sizes, lane_sizes, stage)
+    result = []
+    for half in pair:
+        moved = jnp.dot(row_flip, half, precision=exact, preferred_element_type=jnp.float32)
+        result.append(jnp.dot(moved, lane_flip, precision=exact, preferred_element_type=jnp.float32))
+    return result
+
+
+def averaged(pair, other):
+    return [0.5 * (mine + moved) for mine, moved in zip(pair, other)]
 
 
 def laue_kernel(row_sizes, lane_sizes, sums_ref, out_ref, received, held, send_sems, recv_sems):
@@ -59,40 +65,47 @@
     axes = ("bx", "by", "bz")
     here = tuple(lax.axis_index(axis) for axis in axes)
     sizes = tuple(lax.axis_size(axis) for axis in axes)
-    partners = []
-    for stage in range(3):
-        partner = list(here)
-        partner[stage] = sizes[stage] - 1 - here[stage]
-        partners.append(tuple(partner))
-    remote = [stage for stage in range(3) if sizes[stage] > 1]
-    if remote:
-        barrier = pltpu.get_barrier_semaphore()
-        for stage in remote:
-            pl.semaphore_signal(
-                barrier, 1, device_id=partners[stage], device_id_type=pl.DeviceIdType.MESH
-            )
-        pl.semaphore_wait(barrier, len(remote))
-    current = sums_ref
-    for stage in range(3):
-        source = current
-        if stage in remote:
-            copy = pltpu.make_async_remote_copy(
-                src_ref=current,
-                dst_ref=received.at[stage],
-                send_sem=send_sems.at[stage],
-                recv_sem=recv_sems.at[stage],
-                device_id=partners[stage],
-                device_id_type=pl.DeviceIdType.MESH,
-            )
-            copy.start()
-            copy.wait()
-            source = received.at[stage]
-        row_flip, lane_flip = flip_matrices(row_sizes, lane_sizes, stage)
-        value, weight = flipped_volume(source[...], row_flip, lane_flip, voxels)
-        held[stage, :, :voxels] = 0.5 * (current[:, :voxels] + value)
-        held[stage, :, voxels:] = 0.5 * (current[:, voxels:] + weight)
-        current = held.at[stage]
-    out_ref[...] = current[:, :voxels] / jnp.maximum(current[:, voxels:], 1.0)
+
+    def mirror(flags):
+        return tuple(sizes[a] - 1 - here[a] if flags[a] else here[a] for a in range(3))
+
+    first = (mirror((1, 0, 0)), mirror((0, 1, 0)), mirror((1, 1, 0)))
+    last = mirror((0, 0, 1))
+    barrier = pltpu.get_barrier_semaphore()
+    for target in first + (last,):
+        pl.semaphore_signal(barrier, 1, device_id=target, device_id_type=pl.DeviceIdType.MESH)
+    pl.semaphore_wait(barrier, 4)
+
+    def send(source, slot, target):
+        copy = pltpu.make_async_remote_copy(
+            src_ref=source,
+            dst_ref=received.at[slot],
+            send_sem=send_sems.at[slot],
+            recv_sem=recv_sems.at[slot],
+            device_id=target,
+            device_id_type=pl.DeviceIdType.MESH,
+        )
+        copy.start()
+        return copy
+
+    copies = [send(sums_ref, slot, target) for slot, target in enumerate(first)]
+    for copy in copies:
+        copy.wait()
+
+    def halves(ref):
+        return [ref[:, :voxels], ref[:, voxels:]]
+
+    stage_x = averaged(halves(sums_ref), flipped(halves(received.at[0]), row_sizes, lane_sizes, 0))
+    stage_x_there = averaged(
+        halves(received.at[1]), flipped(halves(received.at[2]), row_sizes, lane_sizes, 0)
+    )
+    stage_y = averaged(stage_x, flipped(stage_x_there, row_sizes, lane_sizes, 1))
+    held[:, :voxels] = stage_y[0]
+    held[:, voxels:] = stage_y[1]
+    copy = send(held, 3, last)
+    copy.wait()
+    stage_z = averaged(halves(held), flipped(halves(received.at[3]), row_sizes, lane_sizes, 2))
+    out_ref[...] = stage_z[0] / jnp.maximum(stage_z[1], 1.0)
 
 
 def laue_average(sums, row_sizes, lane_sizes):
@@ -104,49 +117,55 @@
         out_specs=pl.BlockSpec(memory_space=pltpu.VMEM),
         out_shape=jax.ShapeDtypeStruct((rows, voxels), jnp.float32),
         scratch_shapes=[
-            pltpu.VMEM((3, rows, width), jnp.float32),
-            pltpu.VMEM((3, rows, width), jnp.float32),
-            pltpu.SemaphoreType.DMA((3,)),
-            pltpu.SemaphoreType.DMA((3,)),
+            pltpu.VMEM((4, rows, width), jnp.float32),
+            pltpu.VMEM((rows, width), jnp.float32),
+            pltpu.SemaphoreType.DMA((4,)),
+            pltpu.SemaphoreType.DMA((4,)),
         ],
         compiler_params=pltpu.CompilerParams(collective_id=0, has_side_effects=True),
     )(sums)
 
 
-def tile_kernel(factor_ref, counts_ref, eff_ref, rows_ref, cols_ref, out_ref):
+def tile_kernel(tiles_frame, factor_ref, counts_ref, eff_ref, rows_ref, cols_ref, out_ref):
     block, unused_pixels, voxels = rows_ref.shape
-    for t in range(block):
+    factor = factor_ref[(pl.program_id(0) * block) // tiles_frame]
+
+    def one_tile(t, carry):
         cols = cols_ref[t]
         rows = rows_ref[t].astype(jnp.float32)
         counted = jnp.dot(counts_ref[t], cols, preferred_element_type=jnp.float32)
         seen = jnp.dot(eff_ref[t], cols, preferred_element_type=jnp.float32)
         value = jnp.sum(rows * counted, axis=0, keepdims=True)
         weight = jnp.sum(rows * seen, axis=0, keepdims=True)
-        out_ref[t : t + 1, :voxels] = value * factor_ref[t : t + 1, :]
-        out_ref[t : t + 1, voxels:] = weight
+        out_ref[pl.ds(t, 1), :voxels] = value * factor
+        out_ref[pl.ds(t, 1), voxels:] = weight
+        return carry
+
+    lax.fori_loop(0, block, one_tile, 0, unroll=2)
 
 
 def tile_payload(counts, row_split, col_split, efficiency, factor):
     frames_here, tiles_frame, pixels, columns = counts.shape
     voxels = row_split.shape[-1]
     tiles_here = frames_here * tiles_frame
-    block = 8
+    block = 32
     per_frame = tiles_frame // block
-    tile_factor = jnp.repeat(factor, tiles_frame)[:, None]
     return pl.pallas_call(
-        tile_kernel,
-        grid=(tiles_here // block,),
-        in_specs=[
-            pl.BlockSpec((block, 1), lambda i: (i, 0)),
-            pl.BlockSpec((block, pixels, columns), lambda i: (i, 0, 0)),
-            pl.BlockSpec((block, pixels, columns), lambda i: (i % per_frame, 0, 0)),
-            pl.BlockSpec((block, pixels, voxels), lambda i: (i, 0, 0)),
-            pl.BlockSpec((block, pixels, voxels), lambda i: (i, 0, 0)),
-        ],
-        out_specs=pl.BlockSpec((block, 2 * voxels), lambda i: (i, 0)),
+        functools.partial(tile_kernel, tiles_frame),
+        grid_spec=pltpu.PrefetchScalarGridSpec(
+            num_scalar_prefetch=1,
+            grid=(tiles_here // block,),
+            in_specs=[
+                pl.BlockSpec((block, pixels, columns), lambda i, f: (i, 0, 0)),
+                pl.BlockSpec((block, pixels, columns), lambda i, f: (i % per_frame, 0, 0)),
+                pl.BlockSpec((block, pixels, voxels), lambda i, f: (i, 0, 0)),
+                pl.BlockSpec((block, pixels, voxels), lambda i, f: (i, 0, 0)),
+            ],
+            out_specs=pl.BlockSpec((block, 2 * voxels), lambda i, f: (i, 0)),
+        ),
         out_shape=jax.ShapeDtypeStruct((tiles_here, 2 * voxels), jnp.float32),
     )(
-        tile_factor,
+        factor,
         counts.reshape(tiles_here, pixels, columns),
         efficiency,
         row_split.reshape(tiles_here, pixels, voxels),

time: 89.7 us -> 91.6 us (1.021)
  Pallas kernels: 45.1 us -> 47.7 us
    pallas_call x1, Pallas kernels: 16.6 us -> 18.9 us  [tile_payload(): pl.pallas_call(functools.partial(tile_kernel, tiles_frame), grid_spec=plt...]
where the time goes in v5:
time: 91.6 us; the launch traced here: 91.3 us
  Pallas kernels  47.7 us (52%)
  blocking collectives  31.6 us (34%)
  local copies, waits for them, and re-layouts  6.14 us (7%)
  other arithmetic  4.59 us (5%)
  matrix products  1.22 us (1%)
    all_to_all x1, blocking collectives, shards(): lax.all_to_all(packed, ('bx', 'by', 'bz'), split_axis=0, concat_axis=0, t...  31.6 us
    pallas_call x1, Pallas kernels, laue_average(): pl.pallas_call(functools.partial(laue_kernel, row_sizes, lane_sizes), in_...  28.8 us
    pallas_call x1, Pallas kernels, tile_payload(): pl.pallas_call(functools.partial(tile_kernel, tiles_frame), grid_spec=plt...  18.9 us

profile of v5, /device:TPU:1, one launch (start us, length us, event | category | flops | bytes accessed | tf_op | source)
XLA Modules:
  0.0 91.3 jit_solution(16986905725132505837)
XLA Ops:
  0.0 0.7 convert_element_type.10
  0.7 0.7 fusion.4
  1.4 0.2 reduce_window_sum.11
  1.6 0.8 select_reduce_fusion
  2.4 0.7 fusion.8
  3.1 1.0 %scatter_custom_fusion.1 = f32[512]{0:T(512)S(1)} fusion(s32[128]{0:T(128)S(1)} %fusion.8, f32[128]{0:T(128)S(1)} %convert_element_type.10, f32[]{:T(128)} %constant.16.clone.1), kind=kCustom, calls=%fused_computation.16 | custom fusion | bytes 2052 | tf_op jit(solution)/shard_map/scatter | solution.py:198
  4.1 0.1 reshape.31
  4.2 1.5 %fusion.5.factor_ref = f32[2]{0:T(128)} fusion(s32[2]{0:T(128)} %param.13, f32[3600]{0:T(1024)} %param.12), kind=kLoop, calls=%fused_computation.14 | loop fusion | flops 21598 | bytes 14416 | tf_op jit(solution)/shard_map/reduce_sum | solution.py:190
  5.6 18.9 %shard_map.82 = f32[128,512]{1,0:T(8,128)} custom-call(f32[2]{0:T(128)} %fusion.5.factor_ref, bf16[128,128,128]{2,1,0:T(8,128)(2,1)} %bitcast.23, bf16[64,128,128]{2,1,0:T(8,128)(2,1)} %eff_ref.1, bf16[128,128,256]{2,1,0:T(8,128)(2,1)} %bitcast.19, bf16[128,128,256]{2,1,0:T(8,128)(2,1)} %bitcast.20), custom_call_target="tpu_custom_call" | custom-call | tf_op jit(solution)/shard_map/pallas_call | solution.py:153
  24.5 1.7 %scatter_custom_fusion = f32[512,512]{1,0:T(8,128)S(1)} fusion(s32[128]{0:T(128)S(1)} %fusion.8, f32[128,512]{1,0:T(8,128)} %shard_map.82, f32[]{:T(128)} %constant.5.clone.1), kind=kCustom, calls=%fused_computation.5 | custom fusion | bytes 1049088 | tf_op jit(solution)/shard_map/scatter | solution.py:197
  26.2 0.5 reshape.30
  26.7 0.1 select_maximum_fusion
  26.7 0.8 all_to_all.8
  27.5 31.6 %all_to_all.12 = f32[128,1,2176]{2,1,0:T(1,128)S(1)} all-to-all(f32[128,1,2176]{2,1,0:T(1,128)S(1)} %all_to_all.8), channel_id=1, replica_groups=mesh['bx'=4,'by'=8,'bz'=4] {'bx','by','bz'}, dimensions={0} | all-to-all | bytes 2228224 | tf_op jit(solution)/shard_map/all_to_all | solution.py:206
  59.1 0.1 copy.15
  59.2 0.1 slice.9
  59.3 0.1 eq.51
  59.4 0.3 reshape.32
  59.7 1.2 %fusion.2.sums_ref = f32[128,512]{1,0:T(8,128)} fusion(f32[512,512]{1,0:T(8,128)S(1)} %reshape.32, f32[512]{0:T(512)S(1)} %eq.51), kind=kOutput, calls=%fused_computation.8 | convolution fusion | flops 402718720 | bytes 1312768 | tf_op jit(solution)/shard_map/dot_general | solution.py:214
  60.9 28.8 %shard_map.83 = f32[128,256]{1,0:T(8,128)} custom-call(f32[128,512]{1,0:T(8,128)} %fusion.2.sums_ref), custom_call_target="tpu_custom_call" | custom-call | tf_op jit(solution)/shard_map/pallas_call | solution.py:114
  89.8 1.6 %copy.17 = f32[2,1,1,64,256]{4,3,2,1,0:T(8,128)} copy(f32[2,1,1,64,256]{4,3,2,1,0:T(8,128)} %bitcast.24) | data formatting | bytes 262144
  (1 shorter events, 0.0 us)

commit v6 on v5

--- a/solution.py
+++ b/solution.py
@@ -20,18 +20,14 @@
 BOX_BRICK = 64
 
 
-def digits_flipped(index, sizes, flipped):
-    result = jnp.zeros_like(index)
-    stride = 1
-    rest = index
+def flip_mask(sizes, flipped):
+    mask, stride = 0, 1
     for dim in reversed(range(len(sizes))):
-        digit = rest % sizes[dim]
-        rest = rest // sizes[dim]
+        assert sizes[dim] & (sizes[dim] - 1) == 0
         if dim in flipped:
-            digit = sizes[dim] - 1 - digit
-        result = result + digit * stride
-        stride = stride * sizes[dim]
-    return result
+            mask |= (sizes[dim] - 1) * stride
+        stride *= sizes[dim]
+    return mask
 
 
 def flip_matrices(row_sizes, lane_sizes, stage):
@@ -39,10 +35,10 @@
     lanes = int(np.prod(lane_sizes))
     out_row = lax.broadcasted_iota(jnp.int32, (rows, rows), 0)
     in_row = lax.broadcasted_iota(jnp.int32, (rows, rows), 1)
-    row_flip = (in_row == digits_flipped(out_row, row_sizes, (stage, stage + 3))).astype(jnp.float32)
+    row_flip = (in_row == (out_row ^ flip_mask(row_sizes, (stage, stage + 3)))).astype(jnp.float32)
     in_lane = lax.broadcasted_iota(jnp.int32, (lanes, lanes), 0)
     out_lane = lax.broadcasted_iota(jnp.int32, (lanes, lanes), 1)
-    lane_flip = (in_lane == digits_flipped(out_lane, lane_sizes, (stage,))).astype(jnp.float32)
+    lane_flip = (in_lane == (out_lane ^ flip_mask(lane_sizes, (stage,)))).astype(jnp.float32)
     return row_flip, lane_flip
 
 
@@ -126,46 +122,40 @@
     )(sums)
 
 
-def tile_kernel(tiles_frame, factor_ref, counts_ref, eff_ref, rows_ref, cols_ref, out_ref):
+def tile_kernel(factor_ref, counts_ref, eff_ref, rows_ref, cols_ref, out_ref):
     block, unused_pixels, voxels = rows_ref.shape
-    factor = factor_ref[(pl.program_id(0) * block) // tiles_frame]
-
-    def one_tile(t, carry):
+    for t in range(block):
         cols = cols_ref[t]
         rows = rows_ref[t].astype(jnp.float32)
         counted = jnp.dot(counts_ref[t], cols, preferred_element_type=jnp.float32)
         seen = jnp.dot(eff_ref[t], cols, preferred_element_type=jnp.float32)
         value = jnp.sum(rows * counted, axis=0, keepdims=True)
         weight = jnp.sum(rows * seen, axis=0, keepdims=True)
-        out_ref[pl.ds(t, 1), :voxels] = value * factor
-        out_ref[pl.ds(t, 1), voxels:] = weight
-        return carry
-
-    lax.fori_loop(0, block, one_tile, 0, unroll=2)
+        out_ref[t : t + 1, :voxels] = value * factor_ref[t : t + 1, :]
+        out_ref[t : t + 1, voxels:] = weight
 
 
 def tile_payload(counts, row_split, col_split, efficiency, factor):
     frames_here, tiles_frame, pixels, columns = counts.shape
     voxels = row_split.shape[-1]
     tiles_here = frames_here * tiles_frame
-    block = 32
+    block = 8
     per_frame = tiles_frame // block
+    tile_factor = jnp.repeat(factor, tiles_frame)[:, None]
     return pl.pallas_call(
-        functools.partial(tile_kernel, tiles_frame),
-        grid_spec=pltpu.PrefetchScalarGridSpec(
-            num_scalar_prefetch=1,
-            grid=(tiles_here // block,),
-            in_specs=[
-                pl.BlockSpec((block, pixels, columns), lambda i, f: (i, 0, 0)),
-                pl.BlockSpec((block, pixels, columns), lambda i, f: (i % per_frame, 0, 0)),
-                pl.BlockSpec((block, pixels, voxels), lambda i, f: (i, 0, 0)),
-                pl.BlockSpec((block, pixels, voxels), lambda i, f: (i, 0, 0)),
-            ],
-            out_specs=pl.BlockSpec((block, 2 * voxels), lambda i, f: (i, 0)),
-        ),
+        tile_kernel,
+        grid=(tiles_here // block,),
+        in_specs=[
+            pl.BlockSpec((block, 1), lambda i: (i, 0)),
+            pl.BlockSpec((block, pixels, columns), lambda i: (i, 0, 0)),
+            pl.BlockSpec((block, pixels, columns), lambda i: (i % per_frame, 0, 0)),
+            pl.BlockSpec((block, pixels, voxels), lambda i: (i, 0, 0)),
+            pl.BlockSpec((block, pixels, voxels), lambda i: (i, 0, 0)),
+        ],
+        out_specs=pl.BlockSpec((block, 2 * voxels), lambda i: (i, 0)),
         out_shape=jax.ShapeDtypeStruct((tiles_here, 2 * voxels), jnp.float32),
     )(
-        factor,
+        tile_factor,
         counts.reshape(tiles_here, pixels, columns),
         efficiency,
         row_split.reshape(tiles_here, pixels, voxels),

time: 91.6 us -> 89.9 us (0.981)
  Pallas kernels: 47.7 us -> 45.3 us
    pallas_call x1, Pallas kernels: 18.9 us -> 16.6 us  [tile_payload(): pl.pallas_call(tile_kernel, grid=(tiles_here // block,), in_specs=[pl.Blo...]
where the time goes in v6:
time: 89.9 us; the launch traced here: 89.2 us
  Pallas kernels  45.3 us (50%)
  blocking collectives  31.6 us (35%)
  local copies, waits for them, and re-layouts  6.98 us (8%)
  other arithmetic  4.08 us (5%)
  matrix products  1.22 us (1%)
    all_to_all x1, blocking collectives, shards(): lax.all_to_all(packed, ('bx', 'by', 'bz'), split_axis=0, concat_axis=0, t...  31.6 us
    pallas_call x1, Pallas kernels, laue_average(): pl.pallas_call(functools.partial(laue_kernel, row_sizes, lane_sizes), in_...  28.7 us
    pallas_call x1, Pallas kernels, tile_payload(): pl.pallas_call(tile_kernel, grid=(tiles_here // block,), in_specs=[pl.Blo...  16.6 us

profile of v6, /device:TPU:1, one launch (start us, length us, event | category | flops | bytes accessed | tf_op | source)
XLA Modules:
  0.0 89.2 jit_solution(17025794202256072165)
XLA Ops:
  0.0 0.7 convert_element_type.10
  0.7 0.9 %fusion.5 = f32[2]{0:T(128)S(1)} fusion(s32[2]{0:T(128)} %param.13, f32[3600]{0:T(1024)} %param.12), kind=kLoop, calls=%fused_computation.14 | loop fusion | flops 21598 | bytes 14416 | tf_op jit(solution)/shard_map/reduce_sum | solution.py:180
  1.6 0.1 broadcast_in_dim.31
  1.7 0.8 broadcast_in_dim_reshape.5.factor_ref
  2.4 0.7 fusion.4
  3.2 0.2 reduce_window_sum.11
  3.4 0.8 select_reduce_fusion
  4.2 0.7 fusion.8
  4.9 1.0 %scatter_custom_fusion.1 = f32[512]{0:T(512)S(1)} fusion(s32[128]{0:T(128)S(1)} %fusion.8, f32[128]{0:T(128)S(1)} %convert_element_type.10, f32[]{:T(128)} %constant.16.clone.1), kind=kCustom, calls=%fused_computation.16 | custom fusion | bytes 2052 | tf_op jit(solution)/shard_map/scatter | solution.py:188
  5.8 0.1 reshape.31
  6.0 16.6 %shard_map.82 = f32[128,512]{1,0:T(8,128)} custom-call(f32[128,1]{1,0:T(8,128)} %broadcast_in_dim_reshape.5.factor_ref, bf16[128,128,128]{2,1,0:T(8,128)(2,1)} %bitcast.23, bf16[64,128,128]{2,1,0:T(8,128)(2,1)} %eff_ref.1, bf16[128,128,256]{2,1,0:T(8,128)(2,1)} %bitcast.19, bf16[128,128,256]{2,1,0:T(8,128)(2,1)} %bitcast.20), custom_call_target="tpu_custom_call" | custom-call | tf_op jit(solution)/shard_map/pallas_call | solution.py:145
  22.5 1.7 %scatter_custom_fusion = f32[512,512]{1,0:T(8,128)S(1)} fusion(s32[128]{0:T(128)S(1)} %fusion.8, f32[128,512]{1,0:T(8,128)} %shard_map.82, f32[]{:T(128)} %constant.5.clone.1), kind=kCustom, calls=%fused_computation.5 | custom fusion | bytes 1049088 | tf_op jit(solution)/shard_map/scatter | solution.py:187
  24.2 0.5 reshape.30
  24.7 0.1 select_maximum_fusion
  24.8 0.8 all_to_all.8
  25.6 31.6 %all_to_all.12 = f32[128,1,2176]{2,1,0:T(1,128)S(1)} all-to-all(f32[128,1,2176]{2,1,0:T(1,128)S(1)} %all_to_all.8), channel_id=1, replica_groups=mesh['bx'=4,'by'=8,'bz'=4] {'bx','by','bz'}, dimensions={0} | all-to-all | bytes 2228224 | tf_op jit(solution)/shard_map/all_to_all | solution.py:196
  57.2 0.1 copy.19
  57.2 0.1 slice.9
  57.3 0.1 eq.51
  57.5 0.3 reshape.32
  57.8 1.2 %fusion.2.sums_ref = f32[128,512]{1,0:T(8,128)} fusion(f32[512,512]{1,0:T(8,128)S(1)} %reshape.32, f32[512]{0:T(512)S(1)} %eq.51), kind=kOutput, calls=%fused_computation.8 | convolution fusion | flops 402718720 | bytes 1312768 | tf_op jit(solution)/shard_map/dot_general | solution.py:204
  59.0 28.7 %shard_map.83 = f32[128,256]{1,0:T(8,128)} custom-call(f32[128,512]{1,0:T(8,128)} %fusion.2.sums_ref), custom_call_target="tpu_custom_call" | custom-call | tf_op jit(solution)/shard_map/pallas_call | solution.py:110
  87.7 1.6 %copy.21 = f32[2,1,1,64,256]{4,3,2,1,0:T(8,128)} copy(f32[2,1,1,64,256]{4,3,2,1,0:T(8,128)} %bitcast.24) | data formatting | bytes 262144
  (1 shorter events, 0.0 us)

commit v7 on v6

--- a/solution.py
+++ b/solution.py
@@ -42,13 +42,25 @@
     return row_flip, lane_flip
 
 
+def split_three(x):
+    hi = x.astype(jnp.bfloat16)
+    rest = x - hi.astype(jnp.float32)
+    mid = rest.astype(jnp.bfloat16)
+    lo = (rest - mid.astype(jnp.float32)).astype(jnp.bfloat16)
+    return hi, mid, lo
+
+
 def flipped(pair, row_sizes, lane_sizes, stage):
-    exact = lax.Precision.HIGHEST
     row_flip, lane_flip = flip_matrices(row_sizes, lane_sizes, stage)
+    row_flip = row_flip.astype(jnp.bfloat16)
+    lane_flip = lane_flip.astype(jnp.bfloat16)
     result = []
     for half in pair:
-        moved = jnp.dot(row_flip, half, precision=exact, preferred_element_type=jnp.float32)
-        result.append(jnp.dot(moved, lane_flip, precision=exact, preferred_element_type=jnp.float32))
+        parts = []
+        for piece in split_three(half):
+            moved = jnp.dot(row_flip, piece, preferred_element_type=jnp.float32).astype(jnp.bfloat16)
+            parts.append(jnp.dot(moved, lane_flip, preferred_element_type=jnp.float32))
+        result.append((parts[0] + parts[1]) + parts[2])
     return result
 
 

time: 89.9 us -> 88.8 us (0.988)
  Pallas kernels: 45.3 us -> 44.2 us
    pallas_call x1, Pallas kernels: 28.7 us -> 27.6 us  [laue_average(): pl.pallas_call(functools.partial(laue_kernel, row_sizes, lane_sizes), in_...]
where the time goes in v7:
time: 88.8 us; the launch traced here: 88.2 us
  Pallas kernels  44.2 us (50%)
  blocking collectives  31.6 us (36%)
  local copies, waits for them, and re-layouts  6.98 us (8%)
  other arithmetic  4.08 us (5%)
  matrix products  1.22 us (1%)
    all_to_all x1, blocking collectives, shards(): lax.all_to_all(packed, ('bx', 'by', 'bz'), split_axis=0, concat_axis=0, t...  31.6 us
    pallas_call x1, Pallas kernels, laue_average(): pl.pallas_call(functools.partial(laue_kernel, row_sizes, lane_sizes), in_...  27.6 us
    pallas_call x1, Pallas kernels, tile_payload(): pl.pallas_call(tile_kernel, grid=(tiles_here // block,), in_specs=[pl.Blo...  16.6 us

profile of v7, /device:TPU:1, one launch (start us, length us, event | category | flops | bytes accessed | tf_op | source)
XLA Modules:
  0.0 88.2 jit_solution(2058458729237622495)
XLA Ops:
  0.0 0.7 convert_element_type.10
  0.7 0.9 %fusion.5 = f32[2]{0:T(128)S(1)} fusion(s32[2]{0:T(128)} %param.13, f32[3600]{0:T(1024)} %param.12), kind=kLoop, calls=%fused_computation.14 | loop fusion | flops 21598 | bytes 14416 | tf_op jit(solution)/shard_map/reduce_sum | solution.py:192
  1.6 0.1 broadcast_in_dim.31
  1.7 0.8 broadcast_in_dim_reshape.5.factor_ref
  2.4 0.7 fusion.4
  3.2 0.2 reduce_window_sum.11
  3.4 0.8 select_reduce_fusion
  4.2 0.7 fusion.8
  4.9 1.0 %scatter_custom_fusion.1 = f32[512]{0:T(512)S(1)} fusion(s32[128]{0:T(128)S(1)} %fusion.8, f32[128]{0:T(128)S(1)} %convert_element_type.10, f32[]{:T(128)} %constant.16.clone.1), kind=kCustom, calls=%fused_computation.16 | custom fusion | bytes 2052 | tf_op jit(solution)/shard_map/scatter | solution.py:200
  5.8 0.1 reshape.31
  6.0 16.6 %shard_map.82 = f32[128,512]{1,0:T(8,128)} custom-call(f32[128,1]{1,0:T(8,128)} %broadcast_in_dim_reshape.5.factor_ref, bf16[128,128,128]{2,1,0:T(8,128)(2,1)} %bitcast.23, bf16[64,128,128]{2,1,0:T(8,128)(2,1)} %eff_ref.1, bf16[128,128,256]{2,1,0:T(8,128)(2,1)} %bitcast.19, bf16[128,128,256]{2,1,0:T(8,128)(2,1)} %bitcast.20), custom_call_target="tpu_custom_call" | custom-call | tf_op jit(solution)/shard_map/pallas_call | solution.py:157
  22.5 1.7 %scatter_custom_fusion = f32[512,512]{1,0:T(8,128)S(1)} fusion(s32[128]{0:T(128)S(1)} %fusion.8, f32[128,512]{1,0:T(8,128)} %shard_map.82, f32[]{:T(128)} %constant.5.clone.1), kind=kCustom, calls=%fused_computation.5 | custom fusion | bytes 1049088 | tf_op jit(solution)/shard_map/scatter | solution.py:199
  24.2 0.5 reshape.30
  24.7 0.1 select_maximum_fusion
  24.8 0.8 all_to_all.8
  25.6 31.6 %all_to_all.12 = f32[128,1,2176]{2,1,0:T(1,128)S(1)} all-to-all(f32[128,1,2176]{2,1,0:T(1,128)S(1)} %all_to_all.8), channel_id=1, replica_groups=mesh['bx'=4,'by'=8,'bz'=4] {'bx','by','bz'}, dimensions={0} | all-to-all | bytes 2228224 | tf_op jit(solution)/shard_map/all_to_all | solution.py:208
  57.2 0.1 copy.19
  57.2 0.1 slice.9
  57.3 0.1 eq.51
  57.5 0.3 reshape.32
  57.8 1.2 %fusion.2.sums_ref = f32[128,512]{1,0:T(8,128)} fusion(f32[512,512]{1,0:T(8,128)S(1)} %reshape.32, f32[512]{0:T(512)S(1)} %eq.51), kind=kOutput, calls=%fused_computation.8 | convolution fusion | flops 402718720 | bytes 1312768 | tf_op jit(solution)/shard_map/dot_general | solution.py:216
  59.0 27.6 %shard_map.83 = f32[128,256]{1,0:T(8,128)} custom-call(f32[128,512]{1,0:T(8,128)} %fusion.2.sums_ref), custom_call_target="tpu_custom_call" | custom-call | tf_op jit(solution)/shard_map/pallas_call | solution.py:122
  86.6 1.6 %copy.21 = f32[2,1,1,64,256]{4,3,2,1,0:T(8,128)} copy(f32[2,1,1,64,256]{4,3,2,1,0:T(8,128)} %bitcast.24) | data formatting | bytes 262144
  (1 shorter events, 0.0 us)

commit v8 on v7

--- a/solution.py
+++ b/solution.py
@@ -134,8 +134,16 @@
     )(sums)
 
 
-def tile_kernel(factor_ref, counts_ref, eff_ref, rows_ref, cols_ref, out_ref):
+def tile_kernel(capacity, slot_ref, factor_ref, counts_ref, eff_ref, rows_ref, cols_ref, labels_ref, out_ref):
     block, unused_pixels, voxels = rows_ref.shape
+    width = 2 * voxels
+    step = pl.program_id(0)
+
+    @pl.when(step == 0)
+    def _():
+        out_ref[:, : capacity * width] = jnp.zeros((out_ref.shape[0], capacity * width), jnp.float32)
+        out_ref[:, capacity * width :] = labels_ref[...]
+
     for t in range(block):
         cols = cols_ref[t]
         rows = rows_ref[t].astype(jnp.float32)
@@ -143,35 +151,46 @@
         seen = jnp.dot(eff_ref[t], cols, preferred_element_type=jnp.float32)
         value = jnp.sum(rows * counted, axis=0, keepdims=True)
         weight = jnp.sum(rows * seen, axis=0, keepdims=True)
-        out_ref[t : t + 1, :voxels] = value * factor_ref[t : t + 1, :]
-        out_ref[t : t + 1, voxels:] = weight
-
-
-def tile_payload(counts, row_split, col_split, efficiency, factor):
+        slot = slot_ref[step * block + t]
+        target = slot // capacity
+        start = pl.multiple_of((slot % capacity) * width, width)
+        out_ref[pl.ds(target, 1), pl.ds(start, voxels)] = value * factor_ref[t : t + 1, :]
+        out_ref[pl.ds(target, 1), pl.ds(start + voxels, voxels)] = weight
+
+
+def tile_payload(counts, row_split, col_split, efficiency, factor, slot, labels, capacity):
     frames_here, tiles_frame, pixels, columns = counts.shape
     voxels = row_split.shape[-1]
     tiles_here = frames_here * tiles_frame
+    devices_all, label_width = labels.shape
     block = 8
     per_frame = tiles_frame // block
     tile_factor = jnp.repeat(factor, tiles_frame)[:, None]
+    width = capacity * 2 * voxels + label_width
     return pl.pallas_call(
-        tile_kernel,
-        grid=(tiles_here // block,),
-        in_specs=[
-            pl.BlockSpec((block, 1), lambda i: (i, 0)),
-            pl.BlockSpec((block, pixels, columns), lambda i: (i, 0, 0)),
-            pl.BlockSpec((block, pixels, columns), lambda i: (i % per_frame, 0, 0)),
-            pl.BlockSpec((block, pixels, voxels), lambda i: (i, 0, 0)),
-            pl.BlockSpec((block, pixels, voxels), lambda i: (i, 0, 0)),
-        ],
-        out_specs=pl.BlockSpec((block, 2 * voxels), lambda i: (i, 0)),
-        out_shape=jax.ShapeDtypeStruct((tiles_here, 2 * voxels), jnp.float32),
+        functools.partial(tile_kernel, capacity),
+        grid_spec=pltpu.PrefetchScalarGridSpec(
+            num_scalar_prefetch=1,
+            grid=(tiles_here // block,),
+            in_specs=[
+                pl.BlockSpec((block, 1), lambda i, s: (i, 0)),
+                pl.BlockSpec((block, pixels, columns), lambda i, s: (i, 0, 0)),
+                pl.BlockSpec((block, pixels, columns), lambda i, s: (i % per_frame, 0, 0)),
+                pl.BlockSpec((block, pixels, voxels), lambda i, s: (i, 0, 0)),
+                pl.BlockSpec((block, pixels, voxels), lambda i, s: (i, 0, 0)),
+                pl.BlockSpec((devices_all, label_width), lambda i, s: (0, 0)),
+            ],
+            out_specs=pl.BlockSpec((devices_all, width), lambda i, s: (0, 0)),
+        ),
+        out_shape=jax.ShapeDtypeStruct((devices_all, width), jnp.float32),
     )(
+        slot,
         tile_factor,
         counts.reshape(tiles_here, pixels, columns),
         efficiency,
         row_split.reshape(tiles_here, pixels, voxels),
         col_split.reshape(tiles_here, pixels, voxels),
+        labels,
     )
 
 
@@ -190,21 +209,18 @@
     boxes_here = local_x * local_y * local_z * BOX_BRICK
     picks = angles[:, None] == jnp.arange(lorentz.shape[0], dtype=jnp.int32)[None, :]
     factor = jnp.sum(jnp.where(picks, lorentz[None, :], 0.0), axis=1)
-    payload = tile_payload(counts, row_split, col_split, efficiency, factor)
     owner = tile_owner[:, 0]
-    marks = (owner[:, None] == jnp.arange(devices_all, dtype=jnp.int32)[None, :]).astype(jnp.int32)
-    before = jnp.cumsum(marks, axis=0) - marks
-    rank = jnp.sum(before * marks, axis=1)
+    same = owner[:, None] == owner[None, :]
+    earlier = lax.broadcasted_iota(jnp.int32, same.shape, 1) < lax.broadcasted_iota(jnp.int32, same.shape, 0)
+    rank = jnp.sum((same & earlier).astype(jnp.int32), axis=1)
     slot = owner * capacity + rank
-    outgoing = jnp.zeros((devices_all * capacity, 2 * voxels), jnp.float32).at[slot].set(payload)
-    labels = jnp.full((devices_all * capacity,), -1.0, jnp.float32).at[slot].set(
-        tile_box.astype(jnp.float32)
-    )
     label_width = 128
-    labels = jnp.pad(labels.reshape(devices_all, capacity), ((0, 0), (0, label_width - capacity)))
-    packed = jnp.concatenate(
-        [outgoing.reshape(devices_all, capacity * 2 * voxels), labels], axis=1
-    )
+    to_device = (owner[None, :] == jnp.arange(devices_all, dtype=jnp.int32)[:, None]).astype(jnp.bfloat16)
+    at_rank = jnp.where(
+        rank[:, None] == jnp.arange(label_width, dtype=jnp.int32)[None, :], tile_box[:, None] + 1, 0
+    ).astype(jnp.bfloat16)
+    labels = jnp.dot(to_device, at_rank, preferred_element_type=jnp.float32) - 1.0
+    packed = tile_payload(counts, row_split, col_split, efficiency, factor, slot, labels, capacity)
     arrived = lax.all_to_all(packed, ("bx", "by", "bz"), split_axis=0, concat_axis=0, tiled=True)
     arrived_payload = arrived[:, : capacity * 2 * voxels].reshape(devices_all * capacity, 2 * voxels)
     arrived_ids = arrived[:, capacity * 2 * voxels : capacity * 2 * voxels + capacity].reshape(

time: 88.8 us -> 89.3 us (level)
  local copies, waits for them, and re-layouts: 6.98 us -> 5.38 us
  matrix products: 1.22 us -> 2.71 us
  Pallas kernels: 44.2 us -> 45.3 us
    scatter x2 -> x0, local copies, waits for them, and re-layouts: 2.65 us -> none  [the longest x1 1.68 us: shards(): jnp.zeros((devices_all * capacity, 2 * voxels), jnp.float32).at[slot]]
    add x0 -> x2, other arithmetic: none -> 1.89 us  [the longest x1 1.24 us: shards(): slot = owner * capacity + rank]
    all_to_all x1, local copies, waits for them, and re-layouts: 0.77 us -> 2.39 us  [shards(): lax.all_to_all(packed, ('bx', 'by', 'bz'), split_axis=0, concat_axis=0, t...]
    dot_general x0 -> x1, matrix products: none -> 1.49 us  [shards(): jnp.dot(to_device, at_rank, preferred_element_type=jnp.float32) - 1.0]
    convert_element_type x2 -> x0, other arithmetic: 1.39 us -> none  [the longest x1 0.73 us: shards(): (owner[:, None] == jnp.arange(devices_all, dtype=jnp.int32)[None, :]).ast...]
    pallas_call x1, Pallas kernels: 16.6 us -> 17.7 us  [tile_payload(): pl.pallas_call(functools.partial(tile_kernel, capacity), grid_spec=pltpu....]
where the time goes in v8:
time: 89.3 us; the launch traced here: 88.8 us
  Pallas kernels  45.3 us (51%)
  blocking collectives  31.6 us (35%)
  local copies, waits for them, and re-layouts  5.38 us (6%)
  other arithmetic  3.73 us (4%)
  matrix products  2.71 us (3%)
    all_to_all x1, blocking collectives, shards(): lax.all_to_all(packed, ('bx', 'by', 'bz'), split_axis=0, concat_axis=0, t...  31.6 us
    pallas_call x1, Pallas kernels, laue_average(): pl.pallas_call(functools.partial(laue_kernel, row_sizes, lane_sizes), in_...  27.6 us
    pallas_call x1, Pallas kernels, tile_payload(): pl.pallas_call(functools.partial(tile_kernel, capacity), grid_spec=pltpu....  17.7 us
    all_to_all x1, local copies, waits for them, and re-layouts, shards(): lax.all_to_all(packed, ('bx', 'by', 'bz'), split_axis=0, concat_axis=0, t...  2.39 us

profile of v8, /device:TPU:1, one launch (start us, length us, event | category | flops | bytes accessed | tf_op | source)
XLA Modules:
  0.0 88.8 jit_solution(968367734280034221)
XLA Ops:
  0.0 0.9 %convert_reduce_fusion = s32[128]{0:T(128)S(1)} fusion(s32[128]{0:T(128)} %bitcast.20), kind=kLoop, calls=%fused_computation.8 | loop fusion | flops 81792 | bytes 1024 | tf_op jit(solution)/shard_map/reduce_sum | solution.py:215
  0.9 1.2 %multiply_add_fusion.slot_ref = s32[128]{0:T(128)} fusion(s32[128]{0:T(128)S(1)} %convert_reduce_fusion, s32[128,1]{0,1:T(1,128)} %param.14), kind=kLoop, calls=%fused_computation.17 | loop fusion | flops 256 | bytes 1536 | tf_op jit(solution)/shard_map/add | solution.py:216
  2.1 0.7 broadcast_add_fusion
  2.8 1.5 %convolution_add_fusion.labels_ref = f32[128,128]{1,0:T(8,128)} fusion(s32[128]{0:T(128)S(1)} %broadcast_add_fusion, s32[128]{0:T(128)S(1)} %convert_reduce_fusion, s32[128]{0:T(128)} %bitcast.21), kind=kOutput, calls=%fused_computation | convolution fusion | flops 4276224 | bytes 67072 | tf_op jit(solution)/shard_map/dot_general | solution.py:222
  4.3 0.9 %fusion.7 = f32[2]{0:T(128)S(1)} fusion(s32[2]{0:T(128)} %param.13, f32[3600]{0:T(1024)} %param.12), kind=kLoop, calls=%fused_computation.16 | loop fusion | flops 21598 | bytes 14416 | tf_op jit(solution)/shard_map/reduce_sum | solution.py:211
  5.2 0.1 broadcast_in_dim.37
  5.3 0.8 broadcast_in_dim_reshape.5.factor_ref
  6.1 17.7 %shard_map.82 = f32[128,2176]{1,0:T(8,128)} custom-call(s32[128]{0:T(128)} %multiply_add_fusion.slot_ref, f32[128,1]{1,0:T(8,128)} %broadcast_in_dim_reshape.5.factor_ref, bf16[128,128,128]{2,1,0:T(8,128)(2,1)} %bitcast.18, bf16[64,128,128]{2,1,0:T(8,128)(2,1)} %eff_ref.1, bf16[128,128,256]{2,1,0:T(8,128)(2,1)} %bitcast.13, bf16[128,128,256]{2,1,0:T(8,128)(2,1)} %bitcast.14, ...), custom_call_target="tpu_custom_call" | custom-call | tf_op jit(solution)/shard_map/pallas_call | solution.py:170
  23.7 2.4 %copy.17 = f32[128,1,2176]{2,1,0:T(1,128)S(1)} copy(f32[128,1,2176]{2,0,1:T(8,128)} %bitcast.17) | data formatting | bytes 2228224 | tf_op jit(solution)/shard_map/all_to_all | solution.py:224
  26.1 31.6 %all_to_all.12 = f32[128,1,2176]{2,1,0:T(1,128)S(1)} all-to-all(f32[128,1,2176]{2,1,0:T(1,128)S(1)} %copy.17), channel_id=1, replica_groups=mesh['bx'=4,'by'=8,'bz'=4] {'bx','by','bz'}, dimensions={0} | all-to-all | bytes 2228224 | tf_op jit(solution)/shard_map/all_to_all | solution.py:224
  57.7 0.1 copy.21
  57.8 0.1 slice.9
  57.9 0.1 eq.77
  58.0 0.3 reshape.27
  58.3 1.2 %fusion.sums_ref = f32[128,512]{1,0:T(8,128)} fusion(f32[512,512]{1,0:T(8,128)S(1)} %reshape.27, f32[512]{0:T(512)S(1)} %eq.77), kind=kOutput, calls=%fused_computation.3 | convolution fusion | flops 402718720 | bytes 1312768 | tf_op jit(solution)/shard_map/dot_general | solution.py:232
  59.6 27.6 %shard_map.83 = f32[128,256]{1,0:T(8,128)} custom-call(f32[128,512]{1,0:T(8,128)} %fusion.sums_ref), custom_call_target="tpu_custom_call" | custom-call | tf_op jit(solution)/shard_map/pallas_call | solution.py:122
  87.2 1.6 %copy.23 = f32[2,1,1,64,256]{4,3,2,1,0:T(8,128)} copy(f32[2,1,1,64,256]{4,3,2,1,0:T(8,128)} %bitcast.19) | data formatting | bytes 262144
  (1 shorter events, 0.0 us)

commit v9 on v8

--- a/solution.py
+++ b/solution.py
@@ -134,63 +134,81 @@
     )(sums)
 
 
-def tile_kernel(capacity, slot_ref, factor_ref, counts_ref, eff_ref, rows_ref, cols_ref, labels_ref, out_ref):
+def tile_kernel(
+    capacity, tiles_frame, owner_ref, box_ref, angle_ref, lorentz_ref,
+    counts_ref, eff_ref, rows_ref, cols_ref, out_ref, taken,
+):
     block, unused_pixels, voxels = rows_ref.shape
+    devices_all, unused_one, total = out_ref.shape
     width = 2 * voxels
     step = pl.program_id(0)
 
     @pl.when(step == 0)
     def _():
-        out_ref[:, : capacity * width] = jnp.zeros((out_ref.shape[0], capacity * width), jnp.float32)
-        out_ref[:, capacity * width :] = labels_ref[...]
-
+        out_ref[:, :, : capacity * width] = jnp.zeros((devices_all, 1, capacity * width), jnp.float32)
+        out_ref[:, :, capacity * width :] = jnp.full((devices_all, 1, total - capacity * width), -1.0, jnp.float32)
+
+        def clear(d, carry):
+            taken[d] = 0
+            return carry
+
+        lax.fori_loop(0, devices_all, clear, 0)
+
+    lanes = lax.broadcasted_iota(jnp.int32, (1, total - capacity * width), 1)
     for t in range(block):
+        tile = step * block + t
+        target = owner_ref[tile]
+        rank = taken[target]
+        taken[target] = rank + 1
+        factor = lorentz_ref[angle_ref[tile // tiles_frame]]
         cols = cols_ref[t]
         rows = rows_ref[t].astype(jnp.float32)
         counted = jnp.dot(counts_ref[t], cols, preferred_element_type=jnp.float32)
         seen = jnp.dot(eff_ref[t], cols, preferred_element_type=jnp.float32)
         value = jnp.sum(rows * counted, axis=0, keepdims=True)
         weight = jnp.sum(rows * seen, axis=0, keepdims=True)
-        slot = slot_ref[step * block + t]
-        target = slot // capacity
-        start = pl.multiple_of((slot % capacity) * width, width)
-        out_ref[pl.ds(target, 1), pl.ds(start, voxels)] = value * factor_ref[t : t + 1, :]
-        out_ref[pl.ds(target, 1), pl.ds(start + voxels, voxels)] = weight
-
-
-def tile_payload(counts, row_split, col_split, efficiency, factor, slot, labels, capacity):
+        start = pl.multiple_of(rank * width, width)
+        out_ref[target, :, pl.ds(start, voxels)] = value * factor
+        out_ref[target, :, pl.ds(start + voxels, voxels)] = weight
+        label = jnp.full(lanes.shape, box_ref[tile], jnp.int32).astype(jnp.float32)
+        out_ref[target, :, capacity * width :] = jnp.where(
+            lanes == rank, label, out_ref[target, :, capacity * width :]
+        )
+
+
+def tile_payload(counts, row_split, col_split, efficiency, lorentz, angles, owner, box, devices_all, capacity):
     frames_here, tiles_frame, pixels, columns = counts.shape
     voxels = row_split.shape[-1]
     tiles_here = frames_here * tiles_frame
-    devices_all, label_width = labels.shape
+    label_width = 128
     block = 8
     per_frame = tiles_frame // block
-    tile_factor = jnp.repeat(factor, tiles_frame)[:, None]
-    width = capacity * 2 * voxels + label_width
+    total = capacity * 2 * voxels + label_width
     return pl.pallas_call(
-        functools.partial(tile_kernel, capacity),
+        functools.partial(tile_kernel, capacity, tiles_frame),
         grid_spec=pltpu.PrefetchScalarGridSpec(
-            num_scalar_prefetch=1,
+            num_scalar_prefetch=3,
             grid=(tiles_here // block,),
             in_specs=[
-                pl.BlockSpec((block, 1), lambda i, s: (i, 0)),
-                pl.BlockSpec((block, pixels, columns), lambda i, s: (i, 0, 0)),
-                pl.BlockSpec((block, pixels, columns), lambda i, s: (i % per_frame, 0, 0)),
-                pl.BlockSpec((block, pixels, voxels), lambda i, s: (i, 0, 0)),
-                pl.BlockSpec((block, pixels, voxels), lambda i, s: (i, 0, 0)),
-                pl.BlockSpec((devices_all, label_width), lambda i, s: (0, 0)),
+                pl.BlockSpec(memory_space=pltpu.SMEM),
+                pl.BlockSpec((block, pixels, columns), lambda i, *s: (i, 0, 0)),
+                pl.BlockSpec((block, pixels, columns), lambda i, *s: (i % per_frame, 0, 0)),
+                pl.BlockSpec((block, pixels, voxels), lambda i, *s: (i, 0, 0)),
+                pl.BlockSpec((block, pixels, voxels), lambda i, *s: (i, 0, 0)),
             ],
-            out_specs=pl.BlockSpec((devices_all, width), lambda i, s: (0, 0)),
+            out_specs=pl.BlockSpec((devices_all, 1, total), lambda i, *s: (0, 0, 0)),
+            scratch_shapes=[pltpu.SMEM((devices_all,), jnp.int32)],
         ),
-        out_shape=jax.ShapeDtypeStruct((devices_all, width), jnp.float32),
+        out_shape=jax.ShapeDtypeStruct((devices_all, 1, total), jnp.float32),
     )(
-        slot,
-        tile_factor,
+        owner,
+        box,
+        angles,
+        lorentz,
         counts.reshape(tiles_here, pixels, columns),
         efficiency,
         row_split.reshape(tiles_here, pixels, voxels),
         col_split.reshape(tiles_here, pixels, voxels),
-        labels,
     )
 
 
@@ -207,21 +225,12 @@
     local_y = GY // size_y
     local_z = GZ // size_z
     boxes_here = local_x * local_y * local_z * BOX_BRICK
-    picks = angles[:, None] == jnp.arange(lorentz.shape[0], dtype=jnp.int32)[None, :]
-    factor = jnp.sum(jnp.where(picks, lorentz[None, :], 0.0), axis=1)
-    owner = tile_owner[:, 0]
-    same = owner[:, None] == owner[None, :]
-    earlier = lax.broadcasted_iota(jnp.int32, same.shape, 1) < lax.broadcasted_iota(jnp.int32, same.shape, 0)
-    rank = jnp.sum((same & earlier).astype(jnp.int32), axis=1)
-    slot = owner * capacity + rank
-    label_width = 128
-    to_device = (owner[None, :] == jnp.arange(devices_all, dtype=jnp.int32)[:, None]).astype(jnp.bfloat16)
-    at_rank = jnp.where(
-        rank[:, None] == jnp.arange(label_width, dtype=jnp.int32)[None, :], tile_box[:, None] + 1, 0
-    ).astype(jnp.bfloat16)
-    labels = jnp.dot(to_device, at_rank, preferred_element_type=jnp.float32) - 1.0
-    packed = tile_payload(counts, row_split, col_split, efficiency, factor, slot, labels, capacity)
+    packed = tile_payload(
+        counts, row_split, col_split, efficiency, lorentz, angles,
+        tile_owner[:, 0], tile_box, devices_all, capacity,
+    )
     arrived = lax.all_to_all(packed, ("bx", "by", "bz"), split_axis=0, concat_axis=0, tiled=True)
+    arrived = arrived.reshape(devices_all, -1)
     arrived_payload = arrived[:, : capacity * 2 * voxels].reshape(devices_all * capacity, 2 * voxels)
     arrived_ids = arrived[:, capacity * 2 * voxels : capacity * 2 * voxels + capacity].reshape(
         devices_all * capacity

time: 89.3 us -> 81.7 us (0.915)
  other arithmetic: 3.73 us -> 0 us
  local copies, waits for them, and re-layouts: 5.38 us -> 2.14 us
  matrix products: 2.71 us -> 1.22 us
    all_to_all x1 -> x0, local copies, waits for them, and re-layouts: 2.39 us -> none  [shards(): lax.all_to_all(packed, ('bx', 'by', 'bz'), split_axis=0, concat_axis=0, t...]
    add x2 -> x0, other arithmetic: 1.89 us -> none  [the longest x1 1.24 us: shards(): slot = owner * capacity + rank]
    reduce_sum x2 -> x0, other arithmetic: 1.84 us -> none  [the longest x1 0.94 us: shards(): factor = jnp.sum(jnp.where(picks, lorentz[None, :], 0.0), axis=1)]
    dot_general x1 -> x0, matrix products: 1.49 us -> none  [shards(): jnp.dot(to_device, at_rank, preferred_element_type=jnp.float32) - 1.0]
where the time goes in v9:
time: 81.7 us; the launch traced here: 81.2 us
  Pallas kernels  46 us (56%)
  blocking collectives  31.8 us (39%)
  local copies, waits for them, and re-layouts  2.14 us (3%)
  matrix products  1.22 us (1%)
    all_to_all x1, blocking collectives, shards(): lax.all_to_all(packed, ('bx', 'by', 'bz'), split_axis=0, concat_axis=0, t...  31.8 us
    pallas_call x1, Pallas kernels, laue_average(): pl.pallas_call(functools.partial(laue_kernel, row_sizes, lane_sizes), in_...  27.6 us
    pallas_call x1, Pallas kernels, tile_payload(): pl.pallas_call(functools.partial(tile_kernel, capacity, tiles_frame), gri...  18.4 us
    unnamed x2, local copies, waits for them, and re-layouts  1.64 us

profile of v9, /device:TPU:1, one launch (start us, length us, event | category | flops | bytes accessed | tf_op | source)
XLA Modules:
  0.0 81.2 jit_solution(6817346969399099671)
XLA Ops:
  0.0 18.4 %shard_map.82 = f32[128,1,2176]{2,1,0:T(1,128)} custom-call(s32[128]{0:T(128)} %bitcast.17, s32[128]{0:T(128)} %box_ref.1, s32[2]{0:T(128)} %angle_ref.1, f32[3600]{0:T(1024)} %lorentz_ref.1, bf16[128,128,128]{2,1,0:T(8,128)(2,1)} %bitcast.15, bf16[64,128,128]{2,1,0:T(8,128)(2,1)} %eff_ref.1, bf16[128,128,256]{2,1,0:T(8,128)(2,1)} %bitcast.11, ...), custom_call_target="tpu_custom_call" | custom-call | tf_op jit(solution)/shard_map/pallas_call | solution.py:187
  18.4 31.8 %all_to_all.5 = f32[128,1,2176]{2,1,0:T(1,128)S(1)} all-to-all(f32[128,1,2176]{2,1,0:T(1,128)} %shard_map.82), channel_id=1, replica_groups=mesh['bx'=4,'by'=8,'bz'=4] {'bx','by','bz'}, dimensions={0} | all-to-all | bytes 2228224 | tf_op jit(solution)/shard_map/all_to_all | solution.py:232
  50.2 0.1 copy.13
  50.3 0.1 slice.9
  50.4 0.1 eq.16
  50.5 0.3 reshape.23
  50.8 1.2 %fusion.sums_ref = f32[128,512]{1,0:T(8,128)} fusion(f32[512,512]{1,0:T(8,128)S(1)} %reshape.23, f32[512]{0:T(512)S(1)} %eq.16), kind=kOutput, calls=%fused_computation.2 | convolution fusion | flops 402718720 | bytes 1312768 | tf_op jit(solution)/shard_map/dot_general | solution.py:241
  52.0 27.6 %shard_map.83 = f32[128,256]{1,0:T(8,128)} custom-call(f32[128,512]{1,0:T(8,128)} %fusion.sums_ref), custom_call_target="tpu_custom_call" | custom-call | tf_op jit(solution)/shard_map/pallas_call | solution.py:122
  79.6 1.6 %copy.15 = f32[2,1,1,64,256]{4,3,2,1,0:T(8,128)} copy(f32[2,1,1,64,256]{4,3,2,1,0:T(8,128)} %bitcast.16) | data formatting | bytes 262144
  (1 shorter events, 0.0 us)

commit v10 on v9

v10 whole, which is shorter than its diff:
```python
import functools

import numpy as np
import jax
import jax.numpy as jnp
from jax import lax
from jax.sharding import PartitionSpec as P
from jax.experimental import pallas as pl
from jax.experimental.pallas import tpu as pltpu

VX = 8
VY = 8
VZ = 4
GX = 8
GY = 8
GZ = 4
BOXX = 4
BOXY = 4
BOXZ = 4
BOX_BRICK = 64


def flip_mask(sizes, flipped):
    mask, stride = 0, 1
    for dim in reversed(range(len(sizes))):
        assert sizes[dim] & (sizes[dim] - 1) == 0
        if dim in flipped:
            mask |= (sizes[dim] - 1) * stride
        stride *= sizes[dim]
    return mask


def flip_matrices(row_sizes, lane_sizes, stage):
    rows = int(np.prod(row_sizes))
    lanes = int(np.prod(lane_sizes))
    out_row = lax.broadcasted_iota(jnp.int32, (rows, rows), 0)
    in_row = lax.broadcasted_iota(jnp.int32, (rows, rows), 1)
    row_flip = (in_row == (out_row ^ flip_mask(row_sizes, (stage, stage + 3)))).astype(jnp.float32)
    in_lane = lax.broadcasted_iota(jnp.int32, (lanes, lanes), 0)
    out_lane = lax.broadcasted_iota(jnp.int32, (lanes, lanes), 1)
    lane_flip = (in_lane == (out_lane ^ flip_mask(lane_sizes, (stage,)))).astype(jnp.float32)
    return row_flip, lane_flip


def split_three(x):
    hi = x.astype(jnp.bfloat16)
    rest = x - hi.astype(jnp.float32)
    mid = rest.astype(jnp.bfloat16)
    lo = (rest - mid.astype(jnp.float32)).astype(jnp.bfloat16)
    return hi, mid, lo


def flipped(pair, row_sizes, lane_sizes, stage):
    row_flip, lane_flip = flip_matrices(row_sizes, lane_sizes, stage)
    row_flip = row_flip.astype(jnp.bfloat16)
    lane_flip = lane_flip.astype(jnp.bfloat16)
    result = []
    for half in pair:
        parts = []
        for piece in split_three(half):
            moved = jnp.dot(row_flip, piece, preferred_element_type=jnp.float32).astype(jnp.bfloat16)
            parts.append(jnp.dot(moved, lane_flip, preferred_element_type=jnp.float32))
        result.append((parts[0] + parts[1]) + parts[2])
    return result


def averaged(pair, other):
    return [0.5 * (mine + moved) for mine, moved in zip(pair, other)]


def flat_device(flat, sizes):
    return (flat // (sizes[1] * sizes[2]), (flat // sizes[2]) % sizes[1], flat % sizes[2])


def exact_dot(one_hot, values):
    parts = [
        jnp.dot(one_hot, piece, preferred_element_type=jnp.float32) for piece in split_three(values)
    ]
    return (parts[0] + parts[1]) + parts[2]


def exchange_kernel(
    row_sizes, lane_sizes, capacity, payload_ref, labels_ref, out_ref,
    inbox, label_inbox, received, held, bulk_sems, stage_sems,
):
    voxels = int(np.prod(lane_sizes))
    boxes = int(np.prod(row_sizes))
    axes = ("bx", "by", "bz")
    here = tuple(lax.axis_index(axis) for axis in axes)
    sizes = tuple(lax.axis_size(axis) for axis in axes)
    count = sizes[0] * sizes[1] * sizes[2]
    me = (here[0] * sizes[1] + here[1]) * sizes[2] + here[2]
    mesh_id = pl.DeviceIdType.MESH
    barrier = pltpu.get_barrier_semaphore()

    def greet(step, carry):
        pl.semaphore_signal(barrier, 1, device_id=flat_device((me + step) % count, sizes), device_id_type=mesh_id)
        return carry

    lax.fori_loop(1, count, greet, 0)
    pl.semaphore_wait(barrier, count - 1)

    def payload_copy(target, source_row, target_row):
        return pltpu.make_async_remote_copy(
            src_ref=payload_ref.at[source_row], dst_ref=inbox.at[target_row],
            send_sem=bulk_sems.at[0], recv_sem=bulk_sems.at[1],
            device_id=target, device_id_type=mesh_id,
        )

    def label_copy(target, source_rows, target_rows):
        return pltpu.make_async_remote_copy(
            src_ref=labels_ref.at[source_rows], dst_ref=label_inbox.at[target_rows],
            send_sem=bulk_sems.at[2], recv_sem=bulk_sems.at[3],
            device_id=target, device_id_type=mesh_id,
        )

    def send(step, carry):
        flat = (me + step) % count
        target = flat_device(flat, sizes)
        payload_copy(target, flat, me).start()
        label_copy(target, pl.ds(flat, 1), pl.ds(me, 1)).start()
        return carry

    lax.fori_loop(1, count, send, 0)
    neighbour = flat_device((me + 1) % count, sizes)
    every = payload_copy(neighbour, pl.ds(0, count - 1), pl.ds(0, count - 1))
    every.wait_send()
    every.wait_recv()
    every = label_copy(neighbour, pl.ds(0, count - 1), pl.ds(0, count - 1))
    every.wait_send()
    every.wait_recv()
    inbox[me] = payload_ref[me]
    label_inbox[pl.ds(me, 1), :] = labels_ref[pl.ds(me, 1), :]

    names = jnp.transpose(label_inbox[...])
    box_ids = lax.broadcasted_iota(jnp.int32, (boxes, count), 0).astype(jnp.float32)
    value = jnp.zeros((boxes, voxels), jnp.float32)
    weight = jnp.zeros((boxes, voxels), jnp.float32)
    for k in range(capacity):
        one_hot = (box_ids == names[k : k + 1, :]).astype(jnp.bfloat16)
        value = value + exact_dot(one_hot, inbox[:, 2 * k, :])
        weight = weight + exact_dot(one_hot, inbox[:, 2 * k + 1, :])
    held[0, :, :voxels] = value
    held[0, :, voxels:] = weight

    def halves(ref):
        return [ref[:, :voxels], ref[:, voxels:]]

    current = held.at[0]
    for stage in range(3):
        partner = list(here)
        partner[stage] = sizes[stage] - 1 - here[stage]
        copy = pltpu.make_async_remote_copy(
            src_ref=current, dst_ref=received.at[stage],
            send_sem=stage_sems.at[0, stage], recv_sem=stage_sems.at[1, stage],
            device_id=tuple(partner), device_id_type=mesh_id,
        )
        copy.start()
        copy.wait()
        result = averaged(halves(current), flipped(halves(received.at[stage]), row_sizes, lane_sizes, stage))
        if stage < 2:
            held[stage + 1, :, :voxels] = result[0]
            held[stage + 1, :, voxels:] = result[1]
            current = held.at[stage + 1]
    out_ref[...] = result[0] / jnp.maximum(result[1], 1.0)


def exchange_and_average(payload, labels, row_sizes, lane_sizes, capacity):
    devices_all, slots, voxels = payload.shape
    boxes = int(np.prod(row_sizes))
    return pl.pallas_call(
        functools.partial(exchange_kernel, row_sizes, lane_sizes, capacity),
        in_specs=[pl.BlockSpec(memory_space=pltpu.VMEM)] * 2,
        out_specs=pl.BlockSpec(memory_space=pltpu.VMEM),
        out_shape=jax.ShapeDtypeStruct((boxes, voxels), jnp.float32),
        scratch_shapes=[
            pltpu.VMEM(payload.shape, jnp.float32),
            pltpu.VMEM(labels.shape, jnp.float32),
            pltpu.VMEM((3, boxes, 2 * voxels), jnp.float32),
            pltpu.VMEM((3, boxes, 2 * voxels), jnp.float32),
            pltpu.SemaphoreType.DMA((4,)),
            pltpu.SemaphoreType.DMA((2, 3)),
        ],
        compiler_params=pltpu.CompilerParams(collective_id=0, has_side_effects=True),
    )(payload, labels)


def tile_kernel(
    capacity, tiles_frame, owner_ref, box_ref, angle_ref, lorentz_ref,
    counts_ref, eff_ref, rows_ref, cols_ref, out_ref, labels_ref, taken,
):
    block, unused_pixels, voxels = rows_ref.shape
    devices_all, label_width = labels_ref.shape
    step = pl.program_id(0)

    @pl.when(step == 0)
    def _():
        out_ref[...] = jnp.zeros(out_ref.shape, jnp.float32)
        labels_ref[...] = jnp.full(labels_ref.shape, -1.0, jnp.float32)

        def clear(d, carry):
            taken[d] = 0
            return carry

        lax.fori_loop(0, devices_all, clear, 0)

    lanes = lax.broadcasted_iota(jnp.int32, (1, label_width), 1)
    for t in range(block):
        tile = step * block + t
        target = owner_ref[tile]
        rank = taken[target]
        taken[target] = rank + 1
        factor = lorentz_ref[angle_ref[tile // tiles_frame]]
        cols = cols_ref[t]
        rows = rows_ref[t].astype(jnp.float32)
        counted = jnp.dot(counts_ref[t], cols, preferred_element_type=jnp.float32)
        seen = jnp.dot(eff_ref[t], cols, preferred_element_type=jnp.float32)
        value = jnp.sum(rows * counted, axis=0, keepdims=True)
        weight = jnp.sum(rows * seen, axis=0, keepdims=True)
        out_ref[target, pl.ds(2 * rank, 1), :] = value * factor
        out_ref[target, pl.ds(2 * rank + 1, 1), :] = weight
        label = jnp.full(lanes.shape, box_ref[tile], jnp.int32).astype(jnp.float32)
        labels_ref[pl.ds(target, 1), :] = jnp.where(lanes == rank, label, labels_ref[pl.ds(target, 1), :])


def tile_payload(counts, row_split, col_split, efficiency, lorentz, angles, owner, box, devices_all, capacity):
    frames_here, tiles_frame, pixels, columns = counts.shape
    voxels = row_split.shape[-1]
    tiles_here = frames_here * tiles_frame
    label_width = 128
    block = 8
    per_frame = tiles_frame // block
    return pl.pallas_call(
        functools.partial(tile_kernel, capacity, tiles_frame),
        grid_spec=pltpu.PrefetchScalarGridSpec(
            num_scalar_prefetch=3,
            grid=(tiles_here // block,),
            in_specs=[
                pl.BlockSpec(memory_space=pltpu.SMEM),
                pl.BlockSpec((block, pixels, columns), lambda i, *s: (i, 0, 0)),
                pl.BlockSpec((block, pixels, columns), lambda i, *s: (i % per_frame, 0, 0)),
                pl.BlockSpec((block, pixels, voxels), lambda i, *s: (i, 0, 0)),
                pl.BlockSpec((block, pixels, voxels), lambda i, *s: (i, 0, 0)),
            ],
            out_specs=[
                pl.BlockSpec((devices_all, 2 * capacity, voxels), lambda i, *s: (0, 0, 0)),
                pl.BlockSpec((devices_all, label_width), lambda i, *s: (0, 0)),
            ],
            scratch_shapes=[pltpu.SMEM((devices_all,), jnp.int32)],
        ),
        out_shape=[
            jax.ShapeDtypeStruct((devices_all, 2 * capacity, voxels), jnp.float32),
            jax.ShapeDtypeStruct((devices_all, label_width), jnp.float32),
        ],
    )(
        owner,
        box,
        angles,
        lorentz,
        counts.reshape(tiles_here, pixels, columns),
        efficiency,
        row_split.reshape(tiles_here, pixels, voxels),
        col_split.reshape(tiles_here, pixels, voxels),
    )


def shards(counts, row_split, col_split, efficiency, lorentz, angles, tile_owner, tile_box):
    frames_here, tiles_frame, pixels, unused_width = counts.shape
    voxels = row_split.shape[-1]
    size_x = lax.axis_size("bx")
    size_y = lax.axis_size("by")
    size_z = lax.axis_size("bz")
    devices_all = size_x * size_y * size_z
    tiles_here = frames_here * tiles_frame
    capacity = max(4, 4 * tiles_here // devices_all)
    local_x = GX // size_x
    local_y = GY // size_y
    local_z = GZ // size_z
    boxes_here = local_x * local_y * local_z * BOX_BRICK
    payload, labels = tile_payload(
        counts, row_split, col_split, efficiency, lorentz, angles,
        tile_owner[:, 0], tile_box, devices_all, capacity,
    )
    row_sizes = (local_x, local_y, local_z, BOXX, BOXY, BOXZ)
    lane_sizes = (VX, VY, VZ)
    result = exchange_and_average(payload, labels, row_sizes, lane_sizes, capacity)
    return result.reshape(local_x, local_y, local_z, BOX_BRICK, voxels)


def solution(mesh):
    return jax.shard_map(
        shards,
        mesh=mesh,
        in_specs=(
            P(("bx", "by", "bz"), None, None, None),
            P(("bx", "by", "bz"), None, None, None),
            P(("bx", "by", "bz"), None, None, None),
            P(),
            P(),
            P(("bx", "by", "bz")),
            P(("bx", "by", "bz"), None),
            P(("bx", "by", "bz")),
        ),
        out_specs=P("bx", "by", "bz", None, None),
        check_vma=False,
    )
```

time: 81.7 us -> 84.6 us (1.035)
  Pallas kernels: 46 us -> 82.6 us
  blocking collectives: 31.8 us -> 0 us
  matrix products: 1.22 us -> 0 us
    pallas_call x1, Pallas kernels: 27.6 us -> 64.3 us  [exchange_and_average(): pl.pallas_call(functools.partial(exchange_kernel, row_sizes, lane_sizes,...]
    all_to_all x1 -> x0, blocking collectives: 31.8 us -> none  [shards(): lax.all_to_all(packed, ('bx', 'by', 'bz'), split_axis=0, concat_axis=0, t...]
    dot_general x1 -> x0, matrix products: 1.22 us -> none  [shards(): jnp.dot(wanted, arrived_payload, precision=lax.Precision.HIGHEST, preferr...]
where the time goes in v10:
time: 84.6 us; the launch traced here: 84.2 us
  Pallas kernels  82.6 us (98%)
  local copies, waits for them, and re-layouts  1.57 us (2%)
    pallas_call x1, Pallas kernels, exchange_and_average(): pl.pallas_call(functools.partial(exchange_kernel, row_sizes, lane_sizes,...  64.3 us
    pallas_call x1, Pallas kernels, tile_payload(): pl.pallas_call(functools.partial(tile_kernel, capacity, tiles_frame), gri...  18.3 us

profile of v10, /device:TPU:1, one launch (start us, length us, event | category | flops | bytes accessed | tf_op | source)
XLA Modules:
  0.0 84.2 jit_solution(5311560595742188205)
XLA Ops:
  0.0 18.3 %shard_map.82 = (f32[128,8,256]{2,1,0:T(8,128)}, f32[128,128]{1,0:T(8,128)}) custom-call(s32[128]{0:T(128)} %bitcast.11, s32[128]{0:T(128)} %box_ref.1, s32[2]{0:T(128)} %angle_ref.1, f32[3600]{0:T(1024)} %lorentz_ref.1, bf16[128,128,128]{2,1,0:T(8,128)(2,1)} %bitcast.9, bf16[64,128,128]{2,1,0:T(8,128)(2,1)} %eff_ref.1, bf16[128,128,256]{2,1,0:T(8,128)(2,1)} %bitcast.7, ...), custom_call_target="tpu_custom_call" | custom-call | tf_op jit(solution)/shard_map/pallas_call | solution.py:233
  18.3 64.3 %shard_map.83 = f32[128,256]{1,0:T(8,128)} custom-call(f32[128,8,256]{2,1,0:T(8,128)} %get-tuple-element.7.payload_ref, f32[128,128]{1,0:T(8,128)} %get-tuple-element.8.labels_ref), custom_call_target="tpu_custom_call" | custom-call | tf_op jit(solution)/shard_map/pallas_call | solution.py:171
  82.6 1.6 %copy.11 = f32[2,1,1,64,256]{4,3,2,1,0:T(8,128)} copy(f32[2,1,1,64,256]{4,3,2,1,0:T(8,128)} %bitcast.10) | data formatting | bytes 262144

commit v11 on v9

--- a/solution.py
+++ b/solution.py
@@ -163,8 +163,11 @@
         factor = lorentz_ref[angle_ref[tile // tiles_frame]]
         cols = cols_ref[t]
         rows = rows_ref[t].astype(jnp.float32)
-        counted = jnp.dot(counts_ref[t], cols, preferred_element_type=jnp.float32)
-        seen = jnp.dot(eff_ref[t], cols, preferred_element_type=jnp.float32)
+        both = jnp.dot(
+            jnp.concatenate([counts_ref[t], eff_ref[t]], axis=0), cols, preferred_element_type=jnp.float32
+        )
+        counted = both[: counts_ref.shape[1]]
+        seen = both[counts_ref.shape[1] :]
         value = jnp.sum(rows * counted, axis=0, keepdims=True)
         weight = jnp.sum(rows * seen, axis=0, keepdims=True)
         start = pl.multiple_of(rank * width, width)

time: 81.7 us -> 81.7 us (level)
  no operation moved by 1% of the time
where the time goes in v11:
time: 81.7 us; the launch traced here: 81.2 us
  Pallas kernels  46 us (56%)
  blocking collectives  31.8 us (39%)
  local copies, waits for them, and re-layouts  2.14 us (3%)
  matrix products  1.22 us (1%)
    all_to_all x1, blocking collectives, shards(): lax.all_to_all(packed, ('bx', 'by', 'bz'), split_axis=0, concat_axis=0, t...  31.8 us
    pallas_call x1, Pallas kernels, laue_average(): pl.pallas_call(functools.partial(laue_kernel, row_sizes, lane_sizes), in_...  27.6 us
    pallas_call x1, Pallas kernels, tile_payload(): pl.pallas_call(functools.partial(tile_kernel, capacity, tiles_frame), gri...  18.4 us
    unnamed x2, local copies, waits for them, and re-layouts  1.64 us

profile of v11, /device:TPU:1, one launch (start us, length us, event | category | flops | bytes accessed | tf_op | source)
XLA Modules:
  0.0 81.2 jit_solution(5335308849614116940)
XLA Ops:
  0.0 18.4 %shard_map.82 = f32[128,1,2176]{2,1,0:T(1,128)} custom-call(s32[128]{0:T(128)} %bitcast.17, s32[128]{0:T(128)} %box_ref.1, s32[2]{0:T(128)} %angle_ref.1, f32[3600]{0:T(1024)} %lorentz_ref.1, bf16[128,128,128]{2,1,0:T(8,128)(2,1)} %bitcast.15, bf16[64,128,128]{2,1,0:T(8,128)(2,1)} %eff_ref.1, bf16[128,128,256]{2,1,0:T(8,128)(2,1)} %bitcast.11, ...), custom_call_target="tpu_custom_call" | custom-call | tf_op jit(solution)/shard_map/pallas_call | solution.py:190
  18.4 31.8 %all_to_all.5 = f32[128,1,2176]{2,1,0:T(1,128)S(1)} all-to-all(f32[128,1,2176]{2,1,0:T(1,128)} %shard_map.82), channel_id=1, replica_groups=mesh['bx'=4,'by'=8,'bz'=4] {'bx','by','bz'}, dimensions={0} | all-to-all | bytes 2228224 | tf_op jit(solution)/shard_map/all_to_all | solution.py:235
  50.2 0.1 copy.13
  50.3 0.1 slice.9
  50.4 0.1 eq.16
  50.5 0.3 reshape.23
  50.8 1.2 %fusion.sums_ref = f32[128,512]{1,0:T(8,128)} fusion(f32[512,512]{1,0:T(8,128)S(1)} %reshape.23, f32[512]{0:T(512)S(1)} %eq.16), kind=kOutput, calls=%fused_computation.2 | convolution fusion | flops 402718720 | bytes 1312768 | tf_op jit(solution)/shard_map/dot_general | solution.py:244
  52.0 27.6 %shard_map.83 = f32[128,256]{1,0:T(8,128)} custom-call(f32[128,512]{1,0:T(8,128)} %fusion.sums_ref), custom_call_target="tpu_custom_call" | custom-call | tf_op jit(solution)/shard_map/pallas_call | solution.py:122
  79.6 1.6 %copy.15 = f32[2,1,1,64,256]{4,3,2,1,0:T(8,128)} copy(f32[2,1,1,64,256]{4,3,2,1,0:T(8,128)} %bitcast.16) | data formatting | bytes 262144
  (1 shorter events, 0.0 us)

commit v12 on v11

--- a/solution.py
+++ b/solution.py
@@ -64,12 +64,34 @@
     return result
 
 
+def exact_dot(one_hot, values):
+    parts = [
+        jnp.dot(one_hot, piece, preferred_element_type=jnp.float32) for piece in split_three(values)
+    ]
+    return (parts[0] + parts[1]) + parts[2]
+
+
 def averaged(pair, other):
     return [0.5 * (mine + moved) for mine, moved in zip(pair, other)]
 
 
-def laue_kernel(row_sizes, lane_sizes, sums_ref, out_ref, received, held, send_sems, recv_sems):
+def laue_kernel(
+    row_sizes, lane_sizes, capacity, arrived_ref, out_ref, sums_ref, received, held, send_sems, recv_sems
+):
     voxels = int(np.prod(lane_sizes))
+    boxes = int(np.prod(row_sizes))
+    sources = arrived_ref.shape[0]
+    width = 2 * voxels
+    names = jnp.transpose(arrived_ref[:, capacity * width : capacity * width + 128])
+    box_ids = lax.broadcasted_iota(jnp.int32, (boxes, sources), 0).astype(jnp.float32)
+    value = jnp.zeros((boxes, voxels), jnp.float32)
+    weight = jnp.zeros((boxes, voxels), jnp.float32)
+    for k in range(capacity):
+        one_hot = (box_ids == names[k : k + 1, :]).astype(jnp.bfloat16)
+        value = value + exact_dot(one_hot, arrived_ref[:, k * width : k * width + voxels])
+        weight = weight + exact_dot(one_hot, arrived_ref[:, k * width + voxels : (k + 1) * width])
+    sums_ref[:, :voxels] = value
+    sums_ref[:, voxels:] = weight
     axes = ("bx", "by", "bz")
     here = tuple(lax.axis_index(axis) for axis in axes)
     sizes = tuple(lax.axis_size(axis) for axis in axes)
@@ -113,25 +135,27 @@
     copy = send(held, 3, last)
     copy.wait()
     stage_z = averaged(halves(held), flipped(halves(received.at[3]), row_sizes, lane_sizes, 2))
-    out_ref[...] = stage_z[0] / jnp.maximum(stage_z[1], 1.0)
-
-
-def laue_average(sums, row_sizes, lane_sizes):
-    rows, width = sums.shape
-    voxels = width // 2
+    out_ref[:, :voxels] = stage_z[0]
+    out_ref[:, voxels:] = stage_z[1]
+
+
+def laue_average(arrived, row_sizes, lane_sizes, capacity):
+    rows = int(np.prod(row_sizes))
+    width = 2 * int(np.prod(lane_sizes))
     return pl.pallas_call(
-        functools.partial(laue_kernel, row_sizes, lane_sizes),
+        functools.partial(laue_kernel, row_sizes, lane_sizes, capacity),
         in_specs=[pl.BlockSpec(memory_space=pltpu.VMEM)],
         out_specs=pl.BlockSpec(memory_space=pltpu.VMEM),
-        out_shape=jax.ShapeDtypeStruct((rows, voxels), jnp.float32),
+        out_shape=jax.ShapeDtypeStruct((rows, width), jnp.float32),
         scratch_shapes=[
+            pltpu.VMEM((rows, width), jnp.float32),
             pltpu.VMEM((4, rows, width), jnp.float32),
             pltpu.VMEM((rows, width), jnp.float32),
             pltpu.SemaphoreType.DMA((4,)),
             pltpu.SemaphoreType.DMA((4,)),
         ],
         compiler_params=pltpu.CompilerParams(collective_id=0, has_side_effects=True),
-    )(sums)
+    )(arrived)
 
 
 def tile_kernel(
@@ -234,19 +258,10 @@
     )
     arrived = lax.all_to_all(packed, ("bx", "by", "bz"), split_axis=0, concat_axis=0, tiled=True)
     arrived = arrived.reshape(devices_all, -1)
-    arrived_payload = arrived[:, : capacity * 2 * voxels].reshape(devices_all * capacity, 2 * voxels)
-    arrived_ids = arrived[:, capacity * 2 * voxels : capacity * 2 * voxels + capacity].reshape(
-        devices_all * capacity
-    )
-    wanted = (
-        jnp.arange(boxes_here, dtype=jnp.float32)[:, None] == arrived_ids[None, :]
-    ).astype(jnp.float32)
-    sums = jnp.dot(
-        wanted, arrived_payload, precision=lax.Precision.HIGHEST, preferred_element_type=jnp.float32
-    )
     row_sizes = (local_x, local_y, local_z, BOXX, BOXY, BOXZ)
     lane_sizes = (VX, VY, VZ)
-    result = laue_average(sums, row_sizes, lane_sizes)
+    volume = laue_average(arrived, row_sizes, lane_sizes, capacity)
+    result = volume[:, :voxels] / jnp.maximum(volume[:, voxels:], 1.0)
     return result.reshape(local_x, local_y, local_z, BOX_BRICK, voxels)
 
 

time: 81.7 us -> 81.9 us (level)
  other arithmetic: 0 us -> 1.65 us
  matrix products: 1.22 us -> 0 us
  local copies, waits for them, and re-layouts: 2.14 us -> 1.06 us
  Pallas kernels: 46 us -> 46.9 us
    div x0 -> x1, other arithmetic: none -> 1.65 us  [shards(): result = volume[:, :voxels] / jnp.maximum(volume[:, voxels:], 1.0)]
    dot_general x1 -> x0, matrix products: 1.22 us -> none  [shards(): jnp.dot(wanted, arrived_payload, precision=lax.Precision.HIGHEST, preferr...]
    pallas_call x1, Pallas kernels: 27.6 us -> 28.5 us  [laue_average(): pl.pallas_call(functools.partial(laue_kernel, row_sizes, lane_sizes, capa...]
    unnamed x2 -> x1, local copies, waits for them, and re-layouts: 1.64 us -> 1.06 us
where the time goes in v12:
time: 81.9 us; the launch traced here: 81.4 us
  Pallas kernels  46.9 us (57%)
  blocking collectives  31.8 us (39%)
  other arithmetic  1.65 us (2%)
  local copies, waits for them, and re-layouts  1.06 us (1%)
    all_to_all x1, blocking collectives, shards(): lax.all_to_all(packed, ('bx', 'by', 'bz'), split_axis=0, concat_axis=0, t...  31.8 us
    pallas_call x1, Pallas kernels, laue_average(): pl.pallas_call(functools.partial(laue_kernel, row_sizes, lane_sizes, capa...  28.5 us
    pallas_call x1, Pallas kernels, tile_payload(): pl.pallas_call(functools.partial(tile_kernel, capacity, tiles_frame), gri...  18.4 us
    div x1, other arithmetic, shards(): result = volume[:, :voxels] / jnp.maximum(volume[:, voxels:], 1.0)  1.65 us

profile of v12, /device:TPU:1, one launch (start us, length us, event | category | flops | bytes accessed | tf_op | source)
XLA Modules:
  0.0 81.4 jit_solution(2211562068802566874)
XLA Ops:
  0.0 18.4 %shard_map.82 = f32[128,1,2176]{2,1,0:T(1,128)} custom-call(s32[128]{0:T(128)} %bitcast.14, s32[128]{0:T(128)} %box_ref.1, s32[2]{0:T(128)} %angle_ref.1, f32[3600]{0:T(1024)} %lorentz_ref.1, bf16[128,128,128]{2,1,0:T(8,128)(2,1)} %bitcast.13, bf16[64,128,128]{2,1,0:T(8,128)(2,1)} %eff_ref.1, bf16[128,128,256]{2,1,0:T(8,128)(2,1)} %bitcast.10, ...), custom_call_target="tpu_custom_call" | custom-call | tf_op jit(solution)/shard_map/pallas_call | solution.py:214
  18.4 31.8 %all_to_all.5 = f32[128,1,2176]{2,1,0:T(1,128)S(1)} all-to-all(f32[128,1,2176]{2,1,0:T(1,128)} %shard_map.82), channel_id=1, replica_groups=mesh['bx'=4,'by'=8,'bz'=4] {'bx','by','bz'}, dimensions={0} | all-to-all | bytes 2228224 | tf_op jit(solution)/shard_map/all_to_all | solution.py:259
  50.2 1.1 %copy.14 = f32[128,1,2176]{2,0,1:T(8,128)} copy(f32[128,1,2176]{2,1,0:T(1,128)S(1)} %all_to_all.5) | data formatting | bytes 2228224
  51.2 28.5 %shard_map.83 = f32[128,512]{1,0:T(8,128)} custom-call(f32[128,2176]{1,0:T(8,128)} %bitcast.12), custom_call_target="tpu_custom_call" | custom-call | tf_op jit(solution)/shard_map/pallas_call | solution.py:145
  79.8 1.6 %maximum_divide_fusion = f32[128,256]{1,0:T(8,128)} fusion(f32[128,512]{1,0:T(8,128)} %shard_map.83), kind=kLoop, calls=%fused_computation.1 | loop fusion | flops 65536 | bytes 393216 | tf_op jit(solution)/shard_map/div | solution.py:264

commit v13 on v11

--- a/solution.py
+++ b/solution.py
@@ -184,7 +184,7 @@
     voxels = row_split.shape[-1]
     tiles_here = frames_here * tiles_frame
     label_width = 128
-    block = 8
+    block = 16
     per_frame = tiles_frame // block
     total = capacity * 2 * voxels + label_width
     return pl.pallas_call(

time: 81.7 us -> 77.5 us (0.949)
  Pallas kernels: 46 us -> 42 us
    pallas_call x1, Pallas kernels: 18.4 us -> 14.4 us  [tile_payload(): pl.pallas_call(functools.partial(tile_kernel, capacity, tiles_frame), gri...]
where the time goes in v13:
time: 77.5 us; the launch traced here: 77.2 us
  Pallas kernels  42 us (54%)
  blocking collectives  31.8 us (41%)
  local copies, waits for them, and re-layouts  2.14 us (3%)
  matrix products  1.22 us (2%)
    all_to_all x1, blocking collectives, shards(): lax.all_to_all(packed, ('bx', 'by', 'bz'), split_axis=0, concat_axis=0, t...  31.8 us
    pallas_call x1, Pallas kernels, laue_average(): pl.pallas_call(functools.partial(laue_kernel, row_sizes, lane_sizes), in_...  27.6 us
    pallas_call x1, Pallas kernels, tile_payload(): pl.pallas_call(functools.partial(tile_kernel, capacity, tiles_frame), gri...  14.4 us
    unnamed x2, local copies, waits for them, and re-layouts  1.64 us

profile of v13, /device:TPU:1, one launch (start us, length us, event | category | flops | bytes accessed | tf_op | source)
XLA Modules:
  0.0 77.2 jit_solution(7199291596236597442)
XLA Ops:
  0.0 14.4 %shard_map.82 = f32[128,1,2176]{2,1,0:T(1,128)} custom-call(s32[128]{0:T(128)} %bitcast.17, s32[128]{0:T(128)} %box_ref.1, s32[2]{0:T(128)} %angle_ref.1, f32[3600]{0:T(1024)} %lorentz_ref.1, bf16[128,128,128]{2,1,0:T(8,128)(2,1)} %bitcast.15, bf16[64,128,128]{2,1,0:T(8,128)(2,1)} %eff_ref.1, bf16[128,128,256]{2,1,0:T(8,128)(2,1)} %bitcast.11, ...), custom_call_target="tpu_custom_call" | custom-call | tf_op jit(solution)/shard_map/pallas_call | solution.py:190
  14.4 31.8 %all_to_all.5 = f32[128,1,2176]{2,1,0:T(1,128)S(1)} all-to-all(f32[128,1,2176]{2,1,0:T(1,128)} %shard_map.82), channel_id=1, replica_groups=mesh['bx'=4,'by'=8,'bz'=4] {'bx','by','bz'}, dimensions={0} | all-to-all | bytes 2228224 | tf_op jit(solution)/shard_map/all_to_all | solution.py:235
  46.2 0.1 copy.13
  46.3 0.1 slice.9
  46.4 0.1 eq.16
  46.5 0.3 reshape.23
  46.8 1.2 %fusion.sums_ref = f32[128,512]{1,0:T(8,128)} fusion(f32[512,512]{1,0:T(8,128)S(1)} %reshape.23, f32[512]{0:T(512)S(1)} %eq.16), kind=kOutput, calls=%fused_computation.2 | convolution fusion | flops 402718720 | bytes 1312768 | tf_op jit(solution)/shard_map/dot_general | solution.py:244
  48.0 27.6 %shard_map.83 = f32[128,256]{1,0:T(8,128)} custom-call(f32[128,512]{1,0:T(8,128)} %fusion.sums_ref), custom_call_target="tpu_custom_call" | custom-call | tf_op jit(solution)/shard_map/pallas_call | solution.py:122
  75.6 1.6 %copy.15 = f32[2,1,1,64,256]{4,3,2,1,0:T(8,128)} copy(f32[2,1,1,64,256]{4,3,2,1,0:T(8,128)} %bitcast.16) | data formatting | bytes 262144
  (1 shorter events, 0.0 us)

commit v14 on v13

--- a/solution.py
+++ b/solution.py
@@ -184,7 +184,7 @@
     voxels = row_split.shape[-1]
     tiles_here = frames_here * tiles_frame
     label_width = 128
-    block = 16
+    block = 32
     per_frame = tiles_frame // block
     total = capacity * 2 * voxels + label_width
     return pl.pallas_call(

time: 77.5 us -> 75.9 us (0.979)
  Pallas kernels: 42 us -> 40.5 us
    pallas_call x1, Pallas kernels: 14.4 us -> 12.8 us  [tile_payload(): pl.pallas_call(functools.partial(tile_kernel, capacity, tiles_frame), gri...]
where the time goes in v14:
time: 75.9 us; the launch traced here: 75.7 us
  Pallas kernels  40.5 us (53%)
  blocking collectives  31.8 us (42%)
  local copies, waits for them, and re-layouts  2.14 us (3%)
  matrix products  1.22 us (2%)
    all_to_all x1, blocking collectives, shards(): lax.all_to_all(packed, ('bx', 'by', 'bz'), split_axis=0, concat_axis=0, t...  31.8 us
    pallas_call x1, Pallas kernels, laue_average(): pl.pallas_call(functools.partial(laue_kernel, row_sizes, lane_sizes), in_...  27.6 us
    pallas_call x1, Pallas kernels, tile_payload(): pl.pallas_call(functools.partial(tile_kernel, capacity, tiles_frame), gri...  12.8 us
    unnamed x2, local copies, waits for them, and re-layouts  1.64 us

profile of v14, /device:TPU:1, one launch (start us, length us, event | category | flops | bytes accessed | tf_op | source)
XLA Modules:
  0.0 75.7 jit_solution(4377960758541649241)
XLA Ops:
  0.0 12.8 %shard_map.82 = f32[128,1,2176]{2,1,0:T(1,128)} custom-call(s32[128]{0:T(128)} %bitcast.17, s32[128]{0:T(128)} %box_ref.1, s32[2]{0:T(128)} %angle_ref.1, f32[3600]{0:T(1024)} %lorentz_ref.1, bf16[128,128,128]{2,1,0:T(8,128)(2,1)} %bitcast.15, bf16[64,128,128]{2,1,0:T(8,128)(2,1)} %eff_ref.1, bf16[128,128,256]{2,1,0:T(8,128)(2,1)} %bitcast.11, ...), custom_call_target="tpu_custom_call" | custom-call | tf_op jit(solution)/shard_map/pallas_call | solution.py:190
  12.8 31.8 %all_to_all.5 = f32[128,1,2176]{2,1,0:T(1,128)S(1)} all-to-all(f32[128,1,2176]{2,1,0:T(1,128)} %shard_map.82), channel_id=1, replica_groups=mesh['bx'=4,'by'=8,'bz'=4] {'bx','by','bz'}, dimensions={0} | all-to-all | bytes 2228224 | tf_op jit(solution)/shard_map/all_to_all | solution.py:235
  44.6 0.1 copy.13
  44.7 0.1 slice.9
  44.8 0.1 eq.16
  44.9 0.3 reshape.23
  45.2 1.2 %fusion.sums_ref = f32[128,512]{1,0:T(8,128)} fusion(f32[512,512]{1,0:T(8,128)S(1)} %reshape.23, f32[512]{0:T(512)S(1)} %eq.16), kind=kOutput, calls=%fused_computation.2 | convolution fusion | flops 402718720 | bytes 1312768 | tf_op jit(solution)/shard_map/dot_general | solution.py:244
  46.4 27.6 %shard_map.83 = f32[128,256]{1,0:T(8,128)} custom-call(f32[128,512]{1,0:T(8,128)} %fusion.sums_ref), custom_call_target="tpu_custom_call" | custom-call | tf_op jit(solution)/shard_map/pallas_call | solution.py:122
  74.1 1.6 %copy.15 = f32[2,1,1,64,256]{4,3,2,1,0:T(8,128)} copy(f32[2,1,1,64,256]{4,3,2,1,0:T(8,128)} %bitcast.16) | data formatting | bytes 262144
  (1 shorter events, 0.0 us)

commit v15 on v14

--- a/solution.py
+++ b/solution.py
@@ -184,7 +184,7 @@
     voxels = row_split.shape[-1]
     tiles_here = frames_here * tiles_frame
     label_width = 128
-    block = 32
+    block = 64
     per_frame = tiles_frame // block
     total = capacity * 2 * voxels + label_width
     return pl.pallas_call(

time: 75.9 us -> 76.2 us (level)
  no operation moved by 1% of the time
where the time goes in v15:
time: 76.2 us; the launch traced here: 76 us
  Pallas kernels  40.8 us (54%)
  blocking collectives  31.8 us (42%)
  local copies, waits for them, and re-layouts  2.14 us (3%)
  matrix products  1.22 us (2%)
    all_to_all x1, blocking collectives, shards(): lax.all_to_all(packed, ('bx', 'by', 'bz'), split_axis=0, concat_axis=0, t...  31.8 us
    pallas_call x1, Pallas kernels, laue_average(): pl.pallas_call(functools.partial(laue_kernel, row_sizes, lane_sizes), in_...  27.6 us
    pallas_call x1, Pallas kernels, tile_payload(): pl.pallas_call(functools.partial(tile_kernel, capacity, tiles_frame), gri...  13.1 us
    unnamed x2, local copies, waits for them, and re-layouts  1.64 us

profile of v15, /device:TPU:1, one launch (start us, length us, event | category | flops | bytes accessed | tf_op | source)
XLA Modules:
  0.0 76.0 jit_solution(13306595133392431055)
XLA Ops:
  0.0 13.1 %shard_map.82 = f32[128,1,2176]{2,1,0:T(1,128)} custom-call(s32[128]{0:T(128)} %bitcast.17, s32[128]{0:T(128)} %box_ref.1, s32[2]{0:T(128)} %angle_ref.1, f32[3600]{0:T(1024)} %lorentz_ref.1, bf16[128,128,128]{2,1,0:T(8,128)(2,1)} %bitcast.15, bf16[64,128,128]{2,1,0:T(8,128)(2,1)} %eff_ref.1, bf16[128,128,256]{2,1,0:T(8,128)(2,1)} %bitcast.11, ...), custom_call_target="tpu_custom_call" | custom-call | tf_op jit(solution)/shard_map/pallas_call | solution.py:190
  13.1 31.8 %all_to_all.5 = f32[128,1,2176]{2,1,0:T(1,128)S(1)} all-to-all(f32[128,1,2176]{2,1,0:T(1,128)} %shard_map.82), channel_id=1, replica_groups=mesh['bx'=4,'by'=8,'bz'=4] {'bx','by','bz'}, dimensions={0} | all-to-all | bytes 2228224 | tf_op jit(solution)/shard_map/all_to_all | solution.py:235
  44.9 0.1 copy.13
  45.0 0.1 slice.9
  45.1 0.1 eq.16
  45.2 0.3 reshape.23
  45.5 1.2 %fusion.sums_ref = f32[128,512]{1,0:T(8,128)} fusion(f32[512,512]{1,0:T(8,128)S(1)} %reshape.23, f32[512]{0:T(512)S(1)} %eq.16), kind=kOutput, calls=%fused_computation.2 | convolution fusion | flops 402718720 | bytes 1312768 | tf_op jit(solution)/shard_map/dot_general | solution.py:244
  46.8 27.6 %shard_map.83 = f32[128,256]{1,0:T(8,128)} custom-call(f32[128,512]{1,0:T(8,128)} %fusion.sums_ref), custom_call_target="tpu_custom_call" | custom-call | tf_op jit(solution)/shard_map/pallas_call | solution.py:122
  74.4 1.6 %copy.15 = f32[2,1,1,64,256]{4,3,2,1,0:T(8,128)} copy(f32[2,1,1,64,256]{4,3,2,1,0:T(8,128)} %bitcast.16) | data formatting | bytes 262144
  (1 shorter events, 0.0 us)

commit v16 on v14

--- a/solution.py
+++ b/solution.py
@@ -163,8 +163,9 @@
         factor = lorentz_ref[angle_ref[tile // tiles_frame]]
         cols = cols_ref[t]
         rows = rows_ref[t].astype(jnp.float32)
+        position = (step * block + t) % tiles_frame
         both = jnp.dot(
-            jnp.concatenate([counts_ref[t], eff_ref[t]], axis=0), cols, preferred_element_type=jnp.float32
+            jnp.concatenate([counts_ref[t], eff_ref[position]], axis=0), cols, preferred_element_type=jnp.float32
         )
         counted = both[: counts_ref.shape[1]]
         seen = both[counts_ref.shape[1] :]
@@ -185,7 +186,6 @@
     tiles_here = frames_here * tiles_frame
     label_width = 128
     block = 32
-    per_frame = tiles_frame // block
     total = capacity * 2 * voxels + label_width
     return pl.pallas_call(
         functools.partial(tile_kernel, capacity, tiles_frame),
@@ -195,7 +195,7 @@
             in_specs=[
                 pl.BlockSpec(memory_space=pltpu.SMEM),
                 pl.BlockSpec((block, pixels, columns), lambda i, *s: (i, 0, 0)),
-                pl.BlockSpec((block, pixels, columns), lambda i, *s: (i % per_frame, 0, 0)),
+                pl.BlockSpec((tiles_frame, pixels, columns), lambda i, *s: (0, 0, 0)),
                 pl.BlockSpec((block, pixels, voxels), lambda i, *s: (i, 0, 0)),
                 pl.BlockSpec((block, pixels, voxels), lambda i, *s: (i, 0, 0)),
             ],

time: 75.9 us -> 76.7 us (1.011)
  Pallas kernels: 40.5 us -> 41.3 us
    pallas_call x1, Pallas kernels: 12.8 us -> 13.7 us  [tile_payload(): pl.pallas_call(functools.partial(tile_kernel, capacity, tiles_frame), gri...]
where the time goes in v16:
time: 76.7 us; the launch traced here: 76.5 us
  Pallas kernels  41.3 us (54%)
  blocking collectives  31.8 us (41%)
  local copies, waits for them, and re-layouts  2.14 us (3%)
  matrix products  1.22 us (2%)
    all_to_all x1, blocking collectives, shards(): lax.all_to_all(packed, ('bx', 'by', 'bz'), split_axis=0, concat_axis=0, t...  31.8 us
    pallas_call x1, Pallas kernels, laue_average(): pl.pallas_call(functools.partial(laue_kernel, row_sizes, lane_sizes), in_...  27.6 us
    pallas_call x1, Pallas kernels, tile_payload(): pl.pallas_call(functools.partial(tile_kernel, capacity, tiles_frame), gri...  13.7 us
    unnamed x2, local copies, waits for them, and re-layouts  1.64 us

profile of v16, /device:TPU:1, one launch (start us, length us, event | category | flops | bytes accessed | tf_op | source)
XLA Modules:
  0.0 76.5 jit_solution(5706985098544502769)
XLA Ops:
  0.0 13.7 %shard_map.82 = f32[128,1,2176]{2,1,0:T(1,128)} custom-call(s32[128]{0:T(128)} %bitcast.17, s32[128]{0:T(128)} %box_ref.1, s32[2]{0:T(128)} %angle_ref.1, f32[3600]{0:T(1024)} %lorentz_ref.1, bf16[128,128,128]{2,1,0:T(8,128)(2,1)} %bitcast.15, bf16[64,128,128]{2,1,0:T(8,128)(2,1)} %eff_ref.1, bf16[128,128,256]{2,1,0:T(8,128)(2,1)} %bitcast.11, ...), custom_call_target="tpu_custom_call" | custom-call | tf_op jit(solution)/shard_map/pallas_call | solution.py:190
  13.7 31.8 %all_to_all.5 = f32[128,1,2176]{2,1,0:T(1,128)S(1)} all-to-all(f32[128,1,2176]{2,1,0:T(1,128)} %shard_map.82), channel_id=1, replica_groups=mesh['bx'=4,'by'=8,'bz'=4] {'bx','by','bz'}, dimensions={0} | all-to-all | bytes 2228224 | tf_op jit(solution)/shard_map/all_to_all | solution.py:235
  45.5 0.1 copy.13
  45.6 0.1 slice.9
  45.7 0.1 eq.16
  45.8 0.3 reshape.23
  46.1 1.2 %fusion.sums_ref = f32[128,512]{1,0:T(8,128)} fusion(f32[512,512]{1,0:T(8,128)S(1)} %reshape.23, f32[512]{0:T(512)S(1)} %eq.16), kind=kOutput, calls=%fused_computation.2 | convolution fusion | flops 402718720 | bytes 1312768 | tf_op jit(solution)/shard_map/dot_general | solution.py:244
  47.3 27.6 %shard_map.83 = f32[128,256]{1,0:T(8,128)} custom-call(f32[128,512]{1,0:T(8,128)} %fusion.sums_ref), custom_call_target="tpu_custom_call" | custom-call | tf_op jit(solution)/shard_map/pallas_call | solution.py:122
  74.9 1.6 %copy.15 = f32[2,1,1,64,256]{4,3,2,1,0:T(8,128)} copy(f32[2,1,1,64,256]{4,3,2,1,0:T(8,128)} %bitcast.16) | data formatting | bytes 262144
  (1 shorter events, 0.0 us)

commit v17 on v14

--- a/solution.py
+++ b/solution.py
@@ -232,7 +232,9 @@
         counts, row_split, col_split, efficiency, lorentz, angles,
         tile_owner[:, 0], tile_box, devices_all, capacity,
     )
-    arrived = lax.all_to_all(packed, ("bx", "by", "bz"), split_axis=0, concat_axis=0, tiled=True)
+    packed = packed.reshape(size_x * size_y, size_z, 1, -1)
+    packed = lax.all_to_all(packed, "bz", split_axis=1, concat_axis=1, tiled=True)
+    arrived = lax.all_to_all(packed, ("bx", "by"), split_axis=0, concat_axis=0, tiled=True)
     arrived = arrived.reshape(devices_all, -1)
     arrived_payload = arrived[:, : capacity * 2 * voxels].reshape(devices_all * capacity, 2 * voxels)
     arrived_ids = arrived[:, capacity * 2 * voxels : capacity * 2 * voxels + capacity].reshape(

time: 75.9 us -> 96.9 us (1.28)
  blocking collectives: 31.8 us -> 47.7 us
  other arithmetic: 0 us -> 3.09 us
  local copies, waits for them, and re-layouts: 2.14 us -> 3.94 us
    all_to_all x1 -> x2, blocking collectives: 31.8 us -> 47.7 us  [the longest x1 27.5 us: shards(): lax.all_to_all(packed, ('bx', 'by'), split_axis=0, concat_axis=0, tiled=T...]
    all_to_all x0 -> x1, other arithmetic: none -> 3.09 us  [shards(): lax.all_to_all(packed, ('bx', 'by'), split_axis=0, concat_axis=0, tiled=T...]
    reshape x0 -> x2, local copies, waits for them, and re-layouts: none -> 1.76 us  [the longest x1 1.37 us: shards(): packed = packed.reshape(size_x * size_y, size_z, 1, -1)]
where the time goes in v17:
time: 96.9 us; the launch traced here: 96.7 us
  blocking collectives  47.7 us (49%)
  Pallas kernels  40.6 us (42%)
  local copies, waits for them, and re-layouts  3.94 us (4%)
  other arithmetic  3.09 us (3%)
  matrix products  1.22 us (1%)
    pallas_call x1, Pallas kernels, laue_average(): pl.pallas_call(functools.partial(laue_kernel, row_sizes, lane_sizes), in_...  27.8 us
    all_to_all x1, blocking collectives, shards(): lax.all_to_all(packed, ('bx', 'by'), split_axis=0, concat_axis=0, tiled=T...  27.5 us
    all_to_all x1, blocking collectives, shards(): lax.all_to_all(packed, 'bz', split_axis=1, concat_axis=1, tiled=True)  20.3 us
    pallas_call x1, Pallas kernels, tile_payload(): pl.pallas_call(functools.partial(tile_kernel, capacity, tiles_frame), gri...  12.8 us
    all_to_all x1, other arithmetic, shards(): lax.all_to_all(packed, ('bx', 'by'), split_axis=0, concat_axis=0, tiled=T...  3.09 us

profile of v17, /device:TPU:1, one launch (start us, length us, event | category | flops | bytes accessed | tf_op | source)
XLA Modules:
  0.0 96.7 jit_solution(15979844299837988290)
XLA Ops:
  0.0 12.8 %shard_map.82 = f32[128,1,2176]{2,1,0:T(1,128)} custom-call(s32[128]{0:T(128)} %bitcast.14, s32[128]{0:T(128)} %box_ref.1, s32[2]{0:T(128)} %angle_ref.1, f32[3600]{0:T(1024)} %lorentz_ref.1, bf16[128,128,128]{2,1,0:T(8,128)(2,1)} %bitcast.12, bf16[64,128,128]{2,1,0:T(8,128)(2,1)} %eff_ref.1, bf16[128,128,256]{2,1,0:T(8,128)(2,1)} %bitcast.9, ...), custom_call_target="tpu_custom_call" | custom-call | tf_op jit(solution)/shard_map/pallas_call | solution.py:190
  12.8 1.4 %copy.16 = f32[32,4,1,2176]{3,2,0,1:T(1,128)S(1)} copy(f32[32,4,1,2176]{3,2,1,0:T(1,128)} %bitcast.11) | data formatting | bytes 2228224 | tf_op jit(solution)/shard_map/reshape | solution.py:235
  14.2 20.3 %all_to_all.10 = f32[32,4,1,2176]{3,2,0,1:T(1,128)S(1)} all-to-all(f32[32,4,1,2176]{3,2,0,1:T(1,128)S(1)} %copy.16), channel_id=1, replica_groups=mesh['bx'=4,'by'=8,'bz'=4] {'bz'}, dimensions={1} | all-to-all | bytes 2228224 | tf_op jit(solution)/shard_map/all_to_all | solution.py:236
  34.5 0.1 copy.17
  34.6 27.5 %all_to_all.11 = f32[32,4,1,2176]{3,2,1,0:T(1,128)S(1)} all-to-all(f32[32,4,1,2176]{3,2,1,0:T(1,128)S(1)} %copy.17), channel_id=1, replica_groups=mesh['bx'=4,'by'=8,'bz'=4] {'bx','by'}, dimensions={0} | all-to-all | bytes 2228224 | tf_op jit(solution)/shard_map/all_to_all | solution.py:237
  62.0 3.1 %reduce = f32[32,4,2176]{2,1,0:T(4,128)S(1)} reduce(f32[32,4,1,2176]{3,2,1,0:T(1,128)S(1)} %all_to_all.11, f32[]{:T(128)} %constant.4), dimensions={2}, to_apply=%all_to_all.7.reduce_sub_computation | reduce | bytes 2228228 | tf_op jit(solution)/shard_map/all_to_all | solution.py:237
  65.1 0.4 reshape.26
  65.5 0.1 slice.9
  65.6 0.1 eq.16
  65.7 0.3 reshape.27
  66.0 1.2 %fusion.sums_ref = f32[128,512]{1,0:T(8,128)} fusion(f32[512,512]{1,0:T(8,128)S(1)} %reshape.27, f32[512]{0:T(512)S(1)} %eq.16), kind=kOutput, calls=%fused_computation.1 | convolution fusion | flops 402718720 | bytes 1312768 | tf_op jit(solution)/shard_map/dot_general | solution.py:246
  67.3 27.8 %shard_map.83 = f32[128,256]{1,0:T(8,128)} custom-call(f32[128,512]{1,0:T(8,128)} %fusion.sums_ref), custom_call_target="tpu_custom_call" | custom-call | tf_op jit(solution)/shard_map/pallas_call | solution.py:122
  95.1 1.6 %copy.21 = f32[2,1,1,64,256]{4,3,2,1,0:T(8,128)} copy(f32[2,1,1,64,256]{4,3,2,1,0:T(8,128)} %bitcast.13) | data formatting | bytes 262144
  (1 shorter events, 0.0 us)

commit v18 on v14

--- a/solution.py
+++ b/solution.py
@@ -135,7 +135,7 @@
 
 
 def tile_kernel(
-    capacity, tiles_frame, owner_ref, box_ref, angle_ref, lorentz_ref,
+    capacity, tiles_frame, frames, owner_ref, box_ref, angle_ref, lorentz_ref,
     counts_ref, eff_ref, rows_ref, cols_ref, out_ref, taken,
 ):
     block, unused_pixels, voxels = rows_ref.shape
@@ -156,7 +156,7 @@
 
     lanes = lax.broadcasted_iota(jnp.int32, (1, total - capacity * width), 1)
     for t in range(block):
-        tile = step * block + t
+        tile = ((step % frames) * (tiles_frame // block) + step // frames) * block + t
         target = owner_ref[tile]
         rank = taken[target]
         taken[target] = rank + 1
@@ -186,18 +186,22 @@
     label_width = 128
     block = 32
     per_frame = tiles_frame // block
+
+    def order(i):
+        return (i % frames_here) * per_frame + i // frames_here
+
     total = capacity * 2 * voxels + label_width
     return pl.pallas_call(
-        functools.partial(tile_kernel, capacity, tiles_frame),
+        functools.partial(tile_kernel, capacity, tiles_frame, frames_here),
         grid_spec=pltpu.PrefetchScalarGridSpec(
             num_scalar_prefetch=3,
             grid=(tiles_here // block,),
             in_specs=[
                 pl.BlockSpec(memory_space=pltpu.SMEM),
-                pl.BlockSpec((block, pixels, columns), lambda i, *s: (i, 0, 0)),
-                pl.BlockSpec((block, pixels, columns), lambda i, *s: (i % per_frame, 0, 0)),
-                pl.BlockSpec((block, pixels, voxels), lambda i, *s: (i, 0, 0)),
-                pl.BlockSpec((block, pixels, voxels), lambda i, *s: (i, 0, 0)),
+                pl.BlockSpec((block, pixels, columns), lambda i, *s: (order(i), 0, 0)),
+                pl.BlockSpec((block, pixels, columns), lambda i, *s: (i // frames_here, 0, 0)),
+                pl.BlockSpec((block, pixels, voxels), lambda i, *s: (order(i), 0, 0)),
+                pl.BlockSpec((block, pixels, voxels), lambda i, *s: (order(i), 0, 0)),
             ],
             out_specs=pl.BlockSpec((devices_all, 1, total), lambda i, *s: (0, 0, 0)),
             scratch_shapes=[pltpu.SMEM((devices_all,), jnp.int32)],

time: 75.9 us -> 75.6 us (level)
  no operation moved by 1% of the time
where the time goes in v18:
time: 75.6 us; the launch traced here: 75.4 us
  Pallas kernels  40.2 us (53%)
  blocking collectives  31.8 us (42%)
  local copies, waits for them, and re-layouts  2.14 us (3%)
  matrix products  1.22 us (2%)
    all_to_all x1, blocking collectives, shards(): lax.all_to_all(packed, ('bx', 'by', 'bz'), split_axis=0, concat_axis=0, t...  31.8 us
    pallas_call x1, Pallas kernels, laue_average(): pl.pallas_call(functools.partial(laue_kernel, row_sizes, lane_sizes), in_...  27.7 us
    pallas_call x1, Pallas kernels, tile_payload(): pl.pallas_call(functools.partial(tile_kernel, capacity, tiles_frame, fram...  12.5 us
    unnamed x2, local copies, waits for them, and re-layouts  1.64 us

profile of v18, /device:TPU:1, one launch (start us, length us, event | category | flops | bytes accessed | tf_op | source)
XLA Modules:
  0.0 75.4 jit_solution(17725770765236547828)
XLA Ops:
  0.0 12.5 %shard_map.82 = f32[128,1,2176]{2,1,0:T(1,128)} custom-call(s32[128]{0:T(128)} %bitcast.17, s32[128]{0:T(128)} %box_ref.1, s32[2]{0:T(128)} %angle_ref.1, f32[3600]{0:T(1024)} %lorentz_ref.1, bf16[128,128,128]{2,1,0:T(8,128)(2,1)} %bitcast.15, bf16[64,128,128]{2,1,0:T(8,128)(2,1)} %eff_ref.1, bf16[128,128,256]{2,1,0:T(8,128)(2,1)} %bitcast.11, ...), custom_call_target="tpu_custom_call" | custom-call | tf_op jit(solution)/shard_map/pallas_call | solution.py:194
  12.5 31.8 %all_to_all.5 = f32[128,1,2176]{2,1,0:T(1,128)S(1)} all-to-all(f32[128,1,2176]{2,1,0:T(1,128)} %shard_map.82), channel_id=1, replica_groups=mesh['bx'=4,'by'=8,'bz'=4] {'bx','by','bz'}, dimensions={0} | all-to-all | bytes 2228224 | tf_op jit(solution)/shard_map/all_to_all | solution.py:239
  44.3 0.1 copy.13
  44.4 0.1 slice.9
  44.5 0.1 eq.16
  44.6 0.3 reshape.23
  44.9 1.2 %fusion.sums_ref = f32[128,512]{1,0:T(8,128)} fusion(f32[512,512]{1,0:T(8,128)S(1)} %reshape.23, f32[512]{0:T(512)S(1)} %eq.16), kind=kOutput, calls=%fused_computation.2 | convolution fusion | flops 402718720 | bytes 1312768 | tf_op jit(solution)/shard_map/dot_general | solution.py:248
  46.1 27.7 %shard_map.83 = f32[128,256]{1,0:T(8,128)} custom-call(f32[128,512]{1,0:T(8,128)} %fusion.sums_ref), custom_call_target="tpu_custom_call" | custom-call | tf_op jit(solution)/shard_map/pallas_call | solution.py:122
  73.8 1.6 %copy.15 = f32[2,1,1,64,256]{4,3,2,1,0:T(8,128)} copy(f32[2,1,1,64,256]{4,3,2,1,0:T(8,128)} %bitcast.16) | data formatting | bytes 262144
  (1 shorter events, 0.0 us)

commit v19 on v18

--- a/solution.py
+++ b/solution.py
@@ -97,13 +97,14 @@
         return copy
 
     copies = [send(sums_ref, slot, target) for slot, target in enumerate(first)]
-    for copy in copies:
-        copy.wait()
 
     def halves(ref):
         return [ref[:, :voxels], ref[:, voxels:]]
 
+    copies[0].wait()
     stage_x = averaged(halves(sums_ref), flipped(halves(received.at[0]), row_sizes, lane_sizes, 0))
+    copies[1].wait()
+    copies[2].wait()
     stage_x_there = averaged(
         halves(received.at[1]), flipped(halves(received.at[2]), row_sizes, lane_sizes, 0)
     )

time: 75.6 us -> 75.3 us (level)
  no operation moved by 1% of the time
where the time goes in v19:
time: 75.3 us; the launch traced here: 75.1 us
  Pallas kernels  39.9 us (53%)
  blocking collectives  31.8 us (42%)
  local copies, waits for them, and re-layouts  2.14 us (3%)
  matrix products  1.22 us (2%)
    all_to_all x1, blocking collectives, shards(): lax.all_to_all(packed, ('bx', 'by', 'bz'), split_axis=0, concat_axis=0, t...  31.8 us
    pallas_call x1, Pallas kernels, laue_average(): pl.pallas_call(functools.partial(laue_kernel, row_sizes, lane_sizes), in_...  27.4 us
    pallas_call x1, Pallas kernels, tile_payload(): pl.pallas_call(functools.partial(tile_kernel, capacity, tiles_frame, fram...  12.5 us
    unnamed x2, local copies, waits for them, and re-layouts  1.64 us

profile of v19, /device:TPU:1, one launch (start us, length us, event | category | flops | bytes accessed | tf_op | source)
XLA Modules:
  0.0 75.1 jit_solution(13047039592551578284)
XLA Ops:
  0.0 12.5 %shard_map.82 = f32[128,1,2176]{2,1,0:T(1,128)} custom-call(s32[128]{0:T(128)} %bitcast.17, s32[128]{0:T(128)} %box_ref.1, s32[2]{0:T(128)} %angle_ref.1, f32[3600]{0:T(1024)} %lorentz_ref.1, bf16[128,128,128]{2,1,0:T(8,128)(2,1)} %bitcast.15, bf16[64,128,128]{2,1,0:T(8,128)(2,1)} %eff_ref.1, bf16[128,128,256]{2,1,0:T(8,128)(2,1)} %bitcast.11, ...), custom_call_target="tpu_custom_call" | custom-call | tf_op jit(solution)/shard_map/pallas_call | solution.py:195
  12.5 31.8 %all_to_all.5 = f32[128,1,2176]{2,1,0:T(1,128)S(1)} all-to-all(f32[128,1,2176]{2,1,0:T(1,128)} %shard_map.82), channel_id=1, replica_groups=mesh['bx'=4,'by'=8,'bz'=4] {'bx','by','bz'}, dimensions={0} | all-to-all | bytes 2228224 | tf_op jit(solution)/shard_map/all_to_all | solution.py:240
  44.3 0.1 copy.13
  44.4 0.1 slice.9
  44.5 0.1 eq.16
  44.6 0.3 reshape.23
  44.9 1.2 %fusion.sums_ref = f32[128,512]{1,0:T(8,128)} fusion(f32[512,512]{1,0:T(8,128)S(1)} %reshape.23, f32[512]{0:T(512)S(1)} %eq.16), kind=kOutput, calls=%fused_computation.2 | convolution fusion | flops 402718720 | bytes 1312768 | tf_op jit(solution)/shard_map/dot_general | solution.py:249
  46.1 27.4 %shard_map.83 = f32[128,256]{1,0:T(8,128)} custom-call(f32[128,512]{1,0:T(8,128)} %fusion.sums_ref), custom_call_target="tpu_custom_call" | custom-call | tf_op jit(solution)/shard_map/pallas_call | solution.py:123
  73.5 1.6 %copy.15 = f32[2,1,1,64,256]{4,3,2,1,0:T(8,128)} copy(f32[2,1,1,64,256]{4,3,2,1,0:T(8,128)} %bitcast.16) | data formatting | bytes 262144
  (1 shorter events, 0.0 us)

commit v20 on v19

--- a/solution.py
+++ b/solution.py
@@ -50,10 +50,8 @@
     return hi, mid, lo
 
 
-def flipped(pair, row_sizes, lane_sizes, stage):
-    row_flip, lane_flip = flip_matrices(row_sizes, lane_sizes, stage)
-    row_flip = row_flip.astype(jnp.bfloat16)
-    lane_flip = lane_flip.astype(jnp.bfloat16)
+def flipped(pair, matrices):
+    row_flip, lane_flip = matrices
     result = []
     for half in pair:
         parts = []
@@ -82,6 +80,10 @@
     barrier = pltpu.get_barrier_semaphore()
     for target in first + (last,):
         pl.semaphore_signal(barrier, 1, device_id=target, device_id_type=pl.DeviceIdType.MESH)
+    flips = [
+        tuple(m.astype(jnp.bfloat16) for m in flip_matrices(row_sizes, lane_sizes, stage))
+        for stage in range(3)
+    ]
     pl.semaphore_wait(barrier, 4)
 
     def send(source, slot, target):
@@ -102,18 +104,18 @@
         return [ref[:, :voxels], ref[:, voxels:]]
 
     copies[0].wait()
-    stage_x = averaged(halves(sums_ref), flipped(halves(received.at[0]), row_sizes, lane_sizes, 0))
+    stage_x = averaged(halves(sums_ref), flipped(halves(received.at[0]), flips[0]))
     copies[1].wait()
     copies[2].wait()
     stage_x_there = averaged(
-        halves(received.at[1]), flipped(halves(received.at[2]), row_sizes, lane_sizes, 0)
-    )
-    stage_y = averaged(stage_x, flipped(stage_x_there, row_sizes, lane_sizes, 1))
+        halves(received.at[1]), flipped(halves(received.at[2]), flips[0])
+    )
+    stage_y = averaged(stage_x, flipped(stage_x_there, flips[1]))
     held[:, :voxels] = stage_y[0]
     held[:, voxels:] = stage_y[1]
     copy = send(held, 3, last)
     copy.wait()
-    stage_z = averaged(halves(held), flipped(halves(received.at[3]), row_sizes, lane_sizes, 2))
+    stage_z = averaged(halves(held), flipped(halves(received.at[3]), flips[2]))
     out_ref[...] = stage_z[0] / jnp.maximum(stage_z[1], 1.0)
 
 

time: 75.3 us -> 75.3 us (level)
  no operation moved by 1% of the time
where the time goes in v20:
time: 75.3 us; the launch traced here: 75.1 us
  Pallas kernels  39.9 us (53%)
  blocking collectives  31.8 us (42%)
  local copies, waits for them, and re-layouts  2.14 us (3%)
  matrix products  1.22 us (2%)
    all_to_all x1, blocking collectives, shards(): lax.all_to_all(packed, ('bx', 'by', 'bz'), split_axis=0, concat_axis=0, t...  31.8 us
    pallas_call x1, Pallas kernels, laue_average(): pl.pallas_call(functools.partial(laue_kernel, row_sizes, lane_sizes), in_...  27.4 us
    pallas_call x1, Pallas kernels, tile_payload(): pl.pallas_call(functools.partial(tile_kernel, capacity, tiles_frame, fram...  12.5 us
    unnamed x2, local copies, waits for them, and re-layouts  1.64 us

profile of v20, /device:TPU:1, one launch (start us, length us, event | category | flops | bytes accessed | tf_op | source)
XLA Modules:
  0.0 75.1 jit_solution(5016345087753523068)
XLA Ops:
  0.0 12.5 %shard_map.82 = f32[128,1,2176]{2,1,0:T(1,128)} custom-call(s32[128]{0:T(128)} %bitcast.17, s32[128]{0:T(128)} %box_ref.1, s32[2]{0:T(128)} %angle_ref.1, f32[3600]{0:T(1024)} %lorentz_ref.1, bf16[128,128,128]{2,1,0:T(8,128)(2,1)} %bitcast.15, bf16[64,128,128]{2,1,0:T(8,128)(2,1)} %eff_ref.1, bf16[128,128,256]{2,1,0:T(8,128)(2,1)} %bitcast.11, ...), custom_call_target="tpu_custom_call" | custom-call | tf_op jit(solution)/shard_map/pallas_call | solution.py:197
  12.5 31.8 %all_to_all.5 = f32[128,1,2176]{2,1,0:T(1,128)S(1)} all-to-all(f32[128,1,2176]{2,1,0:T(1,128)} %shard_map.82), channel_id=1, replica_groups=mesh['bx'=4,'by'=8,'bz'=4] {'bx','by','bz'}, dimensions={0} | all-to-all | bytes 2228224 | tf_op jit(solution)/shard_map/all_to_all | solution.py:242
  44.3 0.1 copy.13
  44.4 0.1 slice.9
  44.5 0.1 eq.16
  44.6 0.3 reshape.23
  44.9 1.2 %fusion.sums_ref = f32[128,512]{1,0:T(8,128)} fusion(f32[512,512]{1,0:T(8,128)S(1)} %reshape.23, f32[512]{0:T(512)S(1)} %eq.16), kind=kOutput, calls=%fused_computation.2 | convolution fusion | flops 402718720 | bytes 1312768 | tf_op jit(solution)/shard_map/dot_general | solution.py:251
  46.1 27.4 %shard_map.83 = f32[128,256]{1,0:T(8,128)} custom-call(f32[128,512]{1,0:T(8,128)} %fusion.sums_ref), custom_call_target="tpu_custom_call" | custom-call | tf_op jit(solution)/shard_map/pallas_call | solution.py:125
  73.5 1.6 %copy.15 = f32[2,1,1,64,256]{4,3,2,1,0:T(8,128)} copy(f32[2,1,1,64,256]{4,3,2,1,0:T(8,128)} %bitcast.16) | data formatting | bytes 262144
  (1 shorter events, 0.0 us)
